TPU v7x, 256 devices: a whole 4x4x8 slice. The times are simulated.
256 devices in a mesh: row: 32 (over z, x_hi, core), col: 8 (over y, x_lo).
Axes of the slice: x: 4 (x_hi: 2, x_lo: 2; x = x_hi * 2 + x_lo), y: 4, z: 8, core: 2. Of those that a mesh axis runs over, the one named last changes fastest.
Arguments:
- object_field: float32 [2, 2, 4096, 1024], P(None, None, 'row', 'col'), may hold values from -1 to 1
- probe: float32 [4, 2, 128, 128], replicated, may hold values from -3 to 3
- kernel_phase: float32 [128, 128], replicated, may hold values from -3.140625 to 3.140625
- amplitudes: float32 [3, 32, 8, 128, 128], P(None, 'row', 'col'), may hold values from 0.05 to 1
- offsets: int32 [3, 32, 8, 2], P(None, 'row', 'col'), may hold values from 0 to 64
Outputs:
- object_out: float32 [2, 2, 4096, 1024], P(None, None, 'row', 'col')
- probe_out: float32 [4, 2, 128, 128], replicated
Inputs may be any that keep to these rules, and one draw needn't show every extreme that they name: offsets[b, r + p, c] place a window of 128 x 128 pixels inside tile (r, c) extended by 32 pixels on each side.
All inputs are finite; a program needn't handle non-finite values.
Results may differ from a plain program's by a relative error of at most 0.0003.
Values sent between devices are 32-bit elements; how exact they have to be, the bound alone decides.
No kernel may reach another device: no remote copies, remote signals or barrier semaphores. Data moves between devices by JAX's collectives and lax.ppermute only.
A program may use at most 128 MiB of HBM per device.

v0:
```python
import math

import jax
import jax.numpy as jnp
from jax import lax
from jax.sharding import PartitionSpec as P

WIN = 128
OVL = 32
SLICES = 2


OBJECT_RATE = 0.5
PROBE_RATE = 0.5
FLOOR = 0.1
HIGHEST = lax.Precision.HIGHEST


def shifted(block, axis, distance):
    devices = range(lax.axis_size(axis))
    route = [(i - distance, i) for i in devices if i - distance in devices]
    return lax.ppermute(block, axis, route)


def filled_up(lines, count):
    spare = -lines.shape[0] % count
    if not spare:
        return lines
    return jnp.concatenate([lines, jnp.zeros((spare, *lines.shape[1:]), lines.dtype)])


def sum_by_parts(x, axis):
    lines = x.reshape(-1, *x.shape[1:][-1:])
    padded = filled_up(lines, lax.axis_size(axis))
    own = lax.psum_scatter(padded, axis, scatter_dimension=0, tiled=True)
    whole = lax.all_gather(own, axis, axis=0, tiled=True)
    return whole[: len(lines)].reshape(x.shape)


def extended_2(cells, sides, width):
    for axis, dim in sides:
        count = lax.axis_size(axis)
        ends = count - 1
        head = lax.slice_in_dim(cells, 0, width, axis=dim)
        tail = lax.slice_in_dim(cells, cells.shape[dim] - width, cells.shape[dim], axis=dim)
        cells = jnp.concatenate(
            [
                lax.ppermute(tail, axis, [(i, (i + 1) % count) for i in range(ends)]),
                cells,
                lax.ppermute(head, axis, [((i + 1) % count, i) for i in range(ends)]),
            ],
            axis=dim,
        )
    return cells


def dft_tables(window):
    counter = jnp.arange(window, dtype=jnp.int32)
    product = counter[:, None] * counter[None, :] % window
    phases = product.astype(jnp.float32) * (-2.0 * math.pi / window)
    scaling = 1.0 / math.sqrt(window)
    return (jnp.cos(phases) * scaling, jnp.sin(phases) * scaling)


def left_apply(matrix, values):
    return jnp.einsum("ij,bjk->bik", matrix, values, precision=HIGHEST)


def right_apply(values, matrix):
    return jnp.einsum("bij,jk->bik", values, matrix, precision=HIGHEST)


def transform(field_pair, tables, inverse):
    cosine, sine = tables
    if inverse:
        sine = -sine
    real_part, imag_part = field_pair
    shape = real_part.shape
    window = shape[-1]
    real_part = real_part.reshape(-1, window, window)
    imag_part = imag_part.reshape(-1, window, window)
    middle_real = left_apply(cosine, real_part) - left_apply(sine, imag_part)
    middle_imag = left_apply(cosine, imag_part) + left_apply(sine, real_part)
    result_real = right_apply(middle_real, cosine) - right_apply(middle_imag, sine)
    result_imag = right_apply(middle_imag, cosine) + right_apply(middle_real, sine)
    return (result_real.reshape(shape), result_imag.reshape(shape))


def complex_product(left_pair, right_pair):
    left_real, left_imag = left_pair
    right_real, right_imag = right_pair
    return (
        left_real * right_real - left_imag * right_imag,
        left_real * right_imag + left_imag * right_real,
    )


def conj_product(left_pair, right_pair):
    left_real, left_imag = left_pair
    right_real, right_imag = right_pair
    return (
        left_real * right_real + left_imag * right_imag,
        left_real * right_imag - left_imag * right_real,
    )


def propagate(field_pair, kernel, tables, adjoint):
    spectrum = transform(field_pair, tables, False)
    phase_pair = (kernel[0], -kernel[1]) if adjoint else kernel
    return transform(complex_product(spectrum, phase_pair), tables, True)


def window_gradients(windows, probe_now, kernel, measured, tables):
    first_slice = (windows[:, 0, 0][:, None], windows[:, 0, 1][:, None])
    second_slice = (windows[:, 1, 0][:, None], windows[:, 1, 1][:, None])
    probe_wave = (probe_now[None, :, 0], probe_now[None, :, 1])
    entrance = complex_product(probe_wave, first_slice)
    spread = propagate(entrance, kernel, tables, False)
    exit_wave = complex_product(spread, second_slice)
    farfield = transform(exit_wave, tables, False)
    intensity = jnp.sum(
        farfield[0] * farfield[0] + farfield[1] * farfield[1], axis=1, keepdims=True
    )
    factor = 1.0 - measured[:, None] / jnp.sqrt(intensity + FLOOR)
    back_second = transform((farfield[0] * factor, farfield[1] * factor), tables, True)
    second_terms = conj_product(spread, back_second)
    grad_second = (jnp.sum(second_terms[0], axis=1), jnp.sum(second_terms[1], axis=1))
    back_first = propagate(conj_product(second_slice, back_second), kernel, tables, True)
    first_terms = conj_product(probe_wave, back_first)
    grad_first = (jnp.sum(first_terms[0], axis=1), jnp.sum(first_terms[1], axis=1))
    probe_terms = conj_product(first_slice, back_first)
    grad_probe = (jnp.sum(probe_terms[0], axis=0), jnp.sum(probe_terms[1], axis=0))
    object_grad = jnp.stack([jnp.stack(grad_first, axis=1), jnp.stack(grad_second, axis=1)], axis=1)
    probe_grad = jnp.stack(grad_probe, axis=1)
    return (object_grad, probe_grad)


def fold_rows(buffer):
    inner = buffer.shape[2] - 2 * OVL
    upper = buffer[:, :, :OVL]
    lower = buffer[:, :, inner + OVL :]
    from_below = shifted(upper, "row", -1)
    from_above = shifted(lower, "row", 1)
    middle = buffer[:, :, OVL : inner + OVL]
    middle = middle.at[:, :, inner - OVL :].add(from_below)
    middle = middle.at[:, :, :OVL].add(from_above)
    return middle


def fold_cols(buffer):
    inner = buffer.shape[3] - 2 * OVL
    leftmost = buffer[:, :, :, :OVL]
    rightmost = buffer[:, :, :, inner + OVL :]
    from_right = shifted(leftmost, "col", -1)
    from_left = shifted(rightmost, "col", 1)
    middle = buffer[:, :, :, OVL : inner + OVL]
    middle = middle.at[:, :, :, inner - OVL :].add(from_right)
    middle = middle.at[:, :, :, :OVL].add(from_left)
    return middle


def probe_total(local_grad):
    partial_sum = sum_by_parts(local_grad, "row")
    return sum_by_parts(partial_sum, "col")


def per_device(object_field, probe, kernel_phase, amplitudes, offsets):
    tables = dft_tables(probe.shape[-1])
    kernel = (jnp.cos(kernel_phase), jnp.sin(kernel_phase))
    devices = lax.axis_size("row") * lax.axis_size("col")
    positions = offsets.shape[1]
    batch_count = offsets.shape[0]
    probe_rate = PROBE_RATE / math.sqrt(devices * positions)
    anchor = jnp.zeros((), jnp.int32)
    window_shape = (SLICES, 2, WIN, WIN)
    current = object_field
    probe_now = probe
    pending = None
    held = None
    for batch_index in range(batch_count):
        extended = extended_2(current, (("row", 2), ("col", 3)), OVL)
        position = 0
        starts = (
            anchor,
            anchor,
            offsets[batch_index, position, 0, 0],
            offsets[batch_index, position, 0, 1],
        )
        start_list = [starts]
        window_list = [lax.dynamic_slice(extended, starts, window_shape)]
        windows = jnp.stack(window_list)
        object_grad, probe_grad = window_gradients(
            windows, probe_now, kernel, amplitudes[batch_index, :, 0], tables
        )
        accumulated = jnp.zeros_like(extended)
        position = 0
        accumulated = lax.dynamic_update_slice(
            accumulated, object_grad[position], start_list[position]
        )
        folded = fold_cols(fold_rows(accumulated))
        current = current - OBJECT_RATE * folded
        if batch_index >= batch_count - 2:
            held = probe_grad if held is None else held + probe_grad
            summed = None
        else:
            summed = probe_total(probe_grad)
        if pending is not None:
            probe_now = probe_now - probe_rate * pending
        pending = summed
    probe_now = probe_now - probe_rate * probe_total(held)
    return (current, probe_now)


def solution(mesh):
    in_specs = (
        P(None, None, "row", "col"),
        P(),
        P(),
        P(None, "row", "col", None, None),
        P(None, "row", "col", None),
    )
    out_specs = (P(None, None, "row", "col"), P())
    return jax.shard_map(
        per_device, mesh=mesh, in_specs=in_specs, out_specs=out_specs, check_vma=False
    )
```

profile of v0, /device:TPU:4, one launch (start us, length us, event | category | flops | bytes accessed | tf_op | source)
XLA Modules:
  0.0 706.0 jit_solution(17390256663919883016)
XLA Ops:
  7.2 0.9 fusion.1072
  8.1 1.9 collective-permute-start
  10.1 5.1 collective-permute-start.1
  15.2 1.1 fusion.1073
  17.3 3.1 collective-permute-start.2
  20.4 1.3 collective-permute-start.3
  27.1 11.6 %collective-permute-done.3 = f32[2,2,192,32]{3,2,1,0:T(8,128)S(1)} collective-permute-done((f32[2,2,192,32]{3,2,1,0:T(8,128)S(1)}, f32[2,2,192,32]{3,2,1,0:T(8,128)S(1)}, u32[]{:S(2)}, u32[]{:S(2)}) %collective-permute-start.3) | collective-permute-done | bytes 98336 | tf_op jit(solution)/shard_map/ppermute | solution.py:50
  39.0 1.0 copy-done
  51.3 1.1 convolution_add_fusion.32
  63.0 0.9 convolution_subtract_fusion.28
  75.3 1.1 convolution_add_fusion.24
  77.4 3.0 dynamic_update_slice.9
  80.5 2.7 collective-permute-start.4
  83.2 3.0 collective-permute-start.5
  86.2 6.2 collective-permute-done.5
  92.6 1.3 collective-permute-start.6
  94.0 4.6 collective-permute-start.7
  98.6 5.1 collective-permute-done.6
  103.7 1.2 scatter-add.44
  105.5 1.9 collective-permute-start.8
  107.4 5.1 collective-permute-start.9
  112.6 1.9 collective-permute-done.9
  114.5 0.9 fusion.1068
  115.4 4.8 collective-permute-start.10
  120.2 1.3 collective-permute-start.11
  125.3 0.9 collective-permute-done.10
  126.2 12.8 %collective-permute-done.11 = f32[2,2,192,32]{3,2,1,0:T(8,128)S(1)} collective-permute-done((f32[2,2,192,32]{3,2,1,0:T(8,128)S(1)}, f32[2,2,192,32]{3,2,1,0:T(8,128)S(1)}, u32[]{:S(2)}, u32[]{:S(2)}) %collective-permute-start.11) | collective-permute-done | bytes 98336 | tf_op jit(solution)/shard_map/ppermute | solution.py:50
  150.1 0.9 convolution_subtract_fusion.20
  162.2 1.1 convolution_subtract_fusion.16
  174.7 1.2 convolution_add_fusion.12
  176.0 1.5 add_bitcast_fusion.1
  177.6 3.2 dynamic_update_slice.10
  180.8 3.6 collective-permute-start.12
  184.5 3.0 collective-permute-start.13
  187.5 6.2 collective-permute-done.13
  194.5 1.3 collective-permute-start.14
  196.9 4.6 collective-permute-start.15
  201.5 3.5 collective-permute-done.14
  205.0 1.2 scatter-add.50
  207.6 110.5 %reduce-scatter.5.cloned.1.call-done = f32[32,128]{1,0:T(8,128)} async-done(((f32[1024,128]{1,0:T(8,128)}), f32[32,128]{1,0:T(8,128)}) %reduce-scatter.5.cloned.1.call-update) | async-done | bytes 16400 | tf_op jit(solution)/shard_map/reduce_scatter | solution.py:35
  318.1 42.3 %all_gather.12 = f32[1024,128]{1,0:T(8,128)} all-gather(f32[32,128]{1,0:T(8,128)} %reduce-scatter.5.cloned.1.call-done), channel_id=1, replica_groups=mesh['row'=32,'col'=8] {'row'}, dimensions={0}, use_global_device_ids=true | all-gather | bytes 540672 | tf_op jit(solution)/shard_map/all_gather | solution.py:36
  360.5 2.3 collective-permute-start.16
  362.8 4.8 collective-permute-start.17
  367.6 1.9 collective-permute-done.17
  369.7 3.1 collective-permute-start.18
  372.8 1.3 collective-permute-start.19
  377.6 6.3 collective-permute-done.18
  383.9 16.5 %collective-permute-done.19 = f32[2,2,192,32]{3,2,1,0:T(8,128)S(1)} collective-permute-done((f32[2,2,192,32]{3,2,1,0:T(8,128)S(1)}, f32[2,2,192,32]{3,2,1,0:T(8,128)S(1)}, u32[]{:S(2)}, u32[]{:S(2)}) %collective-permute-start.19) | collective-permute-done | bytes 98336 | tf_op jit(solution)/shard_map/ppermute | solution.py:50
  400.9 2.0 reduce-scatter.7.cloned.1.call-done
  402.8 30.1 %all_gather.13 = f32[1024,128]{1,0:T(8,128)S(1)} all-gather(f32[128,128]{1,0:T(8,128)} %reduce-scatter.7.cloned.1.call-done), channel_id=1, replica_groups=mesh['row'=32,'col'=8] {'col'}, dimensions={0}, use_global_device_ids=true | all-gather | bytes 589824 | tf_op jit(solution)/shard_map/all_gather | solution.py:36
  444.3 1.1 convolution_add_fusion.8
  456.8 0.9 convolution_subtract_fusion.4
  469.1 0.9 convolution_add_fusion
  472.1 3.2 dynamic_update_slice.11
  475.3 1.9 collective-permute-start.20
  477.3 2.4 collective-permute-start.21
  479.8 105.2 %reduce-scatter.9.cloned.1.call-done = f32[32,128]{1,0:T(8,128)} async-done(((f32[1024,128]{1,0:T(8,128)}), f32[32,128]{1,0:T(8,128)}) %reduce-scatter.9.cloned.1.call-update) | async-done | bytes 16400 | tf_op jit(solution)/shard_map/reduce_scatter | solution.py:35
  585.0 42.3 %all_gather.14 = f32[1024,128]{1,0:T(8,128)} all-gather(f32[32,128]{1,0:T(8,128)} %reduce-scatter.9.cloned.1.call-done), channel_id=1, replica_groups=mesh['row'=32,'col'=8] {'row'}, dimensions={0}, use_global_device_ids=true | all-gather | bytes 540672 | tf_op jit(solution)/shard_map/all_gather | solution.py:36
  627.5 1.3 collective-permute-start.22
  628.9 4.6 collective-permute-start.23
  633.5 5.1 collective-permute-done.22
  638.6 1.2 scatter-add.56
  641.9 26.4 %reduce-scatter.11.cloned.1.call-done = f32[128,128]{1,0:T(8,128)} async-done(((f32[1024,128]{1,0:T(8,128)}), f32[128,128]{1,0:T(8,128)}) %reduce-scatter.11.cloned.1.call-update) | async-done | bytes 65552 | tf_op jit(solution)/shard_map/reduce_scatter | solution.py:35
  668.3 30.0 %all_gather.15 = f32[1024,128]{1,0:T(8,128)S(1)} all-gather(f32[128,128]{1,0:T(8,128)} %reduce-scatter.11.cloned.1.call-done), channel_id=1, replica_groups=mesh['row'=32,'col'=8] {'col'}, dimensions={0}, use_global_device_ids=true | all-gather | bytes 589824 | tf_op jit(solution)/shard_map/all_gather | solution.py:36
  (233 shorter events, 114.3 us)
Async XLA Ops:
  7.2 9.2 %copy-start.1 = (f32[2,2,128,128]{3,2,1,0:T(8,128)S(1)}, f32[2,2,128,128]{3,2,1,0:T(8,128)}, u32[]{:S(2)}) copy-start(f32[2,2,128,128]{3,2,1,0:T(8,128)} %param.29) | copy-start | bytes 786436
  7.2 311.0 %reduce-scatter.5.cloned.1.call-start = ((), (), s32[]{:S(2)}) async-start(), calls=%async_computation.4 | async-start | bytes 540672 | tf_op jit(solution)/shard_map/reduce_scatter | solution.py:35
  8.1 8.2 %collective-permute-start = (f32[2,2,32,128]{3,2,1,0:T(8,128)S(1)}, f32[2,2,32,128]{3,2,1,0:T(8,128)S(1)}, u32[]{:S(2)}, u32[]{:S(2)}) collective-permute-start(f32[2,2,32,128]{3,2,1,0:T(8,128)S(1)} %get-tuple-element.209), channel_id=1, source_target_pairs={{0,8},{8,16},{16,24},{24,32},{32,40},{40,48},{48,56},{56,64},{64,7... | collective-permute-start | bytes 196616 | tf_op jit(solution)/shard_map/ppermute | solution.py:48
  10.1 7.0 collective-permute-start.1
  17.3 4.4 copy-start.4
  17.3 9.8 %collective-permute-start.2 = (f32[2,2,192,32]{3,2,1,0:T(8,128)S(1)}, f32[2,2,192,32]{3,2,1,0:T(8,128)S(1)}, u32[]{:S(2)}, u32[]{:S(2)}) collective-permute-start(f32[2,2,192,32]{3,2,1,0:T(8,128)S(1)} %get-tuple-element.191), channel_id=1, source_target_pairs={{0,1},{1,2},{2,3},{3,4},{4,5},{5,6},{6,7},{8,9},{9,10},{10,11},{11... | collective-permute-start | bytes 294920 | tf_op jit(solution)/shard_map/ppermute | solution.py:48
  20.4 18.2 %collective-permute-start.3 = (f32[2,2,192,32]{3,2,1,0:T(8,128)S(1)}, f32[2,2,192,32]{3,2,1,0:T(8,128)S(1)}, u32[]{:S(2)}, u32[]{:S(2)}) collective-permute-start(f32[2,2,192,32]{3,2,1,0:T(8,128)S(1)} %get-tuple-element.190), channel_id=1, source_target_pairs={{1,0},{2,1},{3,2},{4,3},{5,4},{6,5},{7,6},{9,8},{10,9},{11,10},{12... | collective-permute-start | bytes 294920 | tf_op jit(solution)/shard_map/ppermute | solution.py:50
  39.0 1.0 copy-start
  57.6 0.9 copy-start.3
  80.5 5.7 collective-permute-start.4
  83.2 9.2 %collective-permute-start.5 = (f32[2,2,32,192]{3,2,1,0:T(8,128)S(1)}, f32[2,2,32,192]{3,2,1,0:T(8,128)S(1)}, u32[]{:S(2)}, u32[]{:S(2)}) collective-permute-start(f32[2,2,32,192]{3,2,1,0:T(8,128)S(1)} %get-tuple-element.166), channel_id=1, source_target_pairs={{0,8},{8,16},{16,24},{24,32},{32,40},{40,48},{48,56},{56,64},{64,7... | collective-permute-start | bytes 294920 | tf_op jit(solution)/shard_map/ppermute | solution.py:22
  92.6 11.1 %collective-permute-start.6 = (f32[2,2,128,32]{3,2,1,0:T(8,128)S(1)}, f32[2,2,128,32]{3,2,1,0:T(8,128)S(1)}, u32[]{:S(2)}, u32[]{:S(2)}) collective-permute-start(f32[2,2,128,32]{3,2,1,0:T(8,128)S(1)} %get-tuple-element.185), channel_id=1, source_target_pairs={{1,0},{2,1},{3,2},{4,3},{5,4},{6,5},{7,6},{9,8},{10,9},{11,10},{12... | collective-permute-start | bytes 196616 | tf_op jit(solution)/shard_map/ppermute | solution.py:22
  94.0 10.9 %collective-permute-start.7 = (f32[2,2,128,32]{3,2,1,0:T(8,128)S(1)}, f32[2,2,128,32]{3,2,1,0:T(8,128)S(1)}, u32[]{:S(2)}, u32[]{:S(2)}) collective-permute-start(f32[2,2,128,32]{3,2,1,0:T(8,128)S(1)} %get-tuple-element.184), channel_id=1, source_target_pairs={{0,1},{1,2},{2,3},{3,4},{4,5},{5,6},{6,7},{8,9},{9,10},{10,11},{11... | collective-permute-start | bytes 196616 | tf_op jit(solution)/shard_map/ppermute | solution.py:22
  105.5 7.1 %collective-permute-start.8 = (f32[2,2,32,128]{3,2,1,0:T(8,128)S(1)}, f32[2,2,32,128]{3,2,1,0:T(8,128)S(1)}, u32[]{:S(2)}, u32[]{:S(2)}) collective-permute-start(f32[2,2,32,128]{3,2,1,0:T(8,128)S(1)} %get-tuple-element.202), channel_id=1, source_target_pairs={{0,8},{8,16},{16,24},{24,32},{32,40},{40,48},{48,56},{56,64},{64,7... | collective-permute-start | bytes 196616 | tf_op jit(solution)/shard_map/ppermute | solution.py:48
  107.4 7.0 collective-permute-start.9
  115.4 10.8 %collective-permute-start.10 = (f32[2,2,192,32]{3,2,1,0:T(8,128)}, f32[2,2,192,32]{3,2,1,0:T(8,128)S(1)}, u32[]{:S(2)}, u32[]{:S(2)}) collective-permute-start(f32[2,2,192,32]{3,2,1,0:T(8,128)} %get-tuple-element.189), channel_id=1, source_target_pairs={{0,1},{1,2},{2,3},{3,4},{4,5},{5,6},{6,7},{8,9},{9,10},{10,11},{11... | collective-permute-start | bytes 294920 | tf_op jit(solution)/shard_map/ppermute | solution.py:48
  120.2 18.8 %collective-permute-start.11 = (f32[2,2,192,32]{3,2,1,0:T(8,128)S(1)}, f32[2,2,192,32]{3,2,1,0:T(8,128)S(1)}, u32[]{:S(2)}, u32[]{:S(2)}) collective-permute-start(f32[2,2,192,32]{3,2,1,0:T(8,128)S(1)} %get-tuple-element.188), channel_id=1, source_target_pairs={{1,0},{2,1},{3,2},{4,3},{5,4},{6,5},{7,6},{9,8},{10,9},{11,10},{12... | collective-permute-start | bytes 294920 | tf_op jit(solution)/shard_map/ppermute | solution.py:50
  180.8 6.6 collective-permute-start.12
  184.5 9.2 %collective-permute-start.13 = (f32[2,2,32,192]{3,2,1,0:T(8,128)S(1)}, f32[2,2,32,192]{3,2,1,0:T(8,128)S(1)}, u32[]{:S(2)}, u32[]{:S(2)}) collective-permute-start(f32[2,2,32,192]{3,2,1,0:T(8,128)S(1)} %get-tuple-element.164), channel_id=1, source_target_pairs={{0,8},{8,16},{16,24},{24,32},{32,40},{40,48},{48,56},{56,64},{64,7... | collective-permute-start | bytes 294920 | tf_op jit(solution)/shard_map/ppermute | solution.py:22
  194.5 10.5 %collective-permute-start.14 = (f32[2,2,128,32]{3,2,1,0:T(8,128)S(1)}, f32[2,2,128,32]{3,2,1,0:T(8,128)S(1)}, u32[]{:S(2)}, u32[]{:S(2)}) collective-permute-start(f32[2,2,128,32]{3,2,1,0:T(8,128)S(1)} %get-tuple-element.183), channel_id=1, source_target_pairs={{1,0},{2,1},{3,2},{4,3},{5,4},{6,5},{7,6},{9,8},{10,9},{11,10},{12... | collective-permute-start | bytes 196616 | tf_op jit(solution)/shard_map/ppermute | solution.py:22
  196.7 206.1 %reduce-scatter.7.cloned.1.call-start = ((), (), s32[]{:S(2)}) async-start(), calls=%async_computation.5 | async-start | bytes 589824 | tf_op jit(solution)/shard_map/reduce_scatter | solution.py:35
  196.9 10.1 %collective-permute-start.15 = (f32[2,2,128,32]{3,2,1,0:T(8,128)}, f32[2,2,128,32]{3,2,1,0:T(8,128)S(1)}, u32[]{:S(2)}, u32[]{:S(2)}) collective-permute-start(f32[2,2,128,32]{3,2,1,0:T(8,128)} %get-tuple-element.182), channel_id=1, source_target_pairs={{0,1},{1,2},{2,3},{3,4},{4,5},{5,6},{6,7},{8,9},{9,10},{10,11},{11... | collective-permute-start | bytes 196616 | tf_op jit(solution)/shard_map/ppermute | solution.py:22
  360.4 224.6 %reduce-scatter.9.cloned.1.call-start = ((), (), s32[]{:S(2)}) async-start(), calls=%async_computation.6 | async-start | bytes 540672 | tf_op jit(solution)/shard_map/reduce_scatter | solution.py:35
  360.5 7.1 %collective-permute-start.16 = (f32[2,2,32,128]{3,2,1,0:T(8,128)S(1)}, f32[2,2,32,128]{3,2,1,0:T(8,128)S(1)}, u32[]{:S(2)}, u32[]{:S(2)}) collective-permute-start(f32[2,2,32,128]{3,2,1,0:T(8,128)S(1)} %get-tuple-element.196), channel_id=1, source_target_pairs={{0,8},{8,16},{16,24},{24,32},{32,40},{40,48},{48,56},{56,64},{64,7... | collective-permute-start | bytes 196616 | tf_op jit(solution)/shard_map/ppermute | solution.py:48
  362.8 6.7 collective-permute-start.17
  369.7 14.2 %collective-permute-start.18 = (f32[2,2,192,32]{3,2,1,0:T(8,128)S(1)}, f32[2,2,192,32]{3,2,1,0:T(8,128)S(1)}, u32[]{:S(2)}, u32[]{:S(2)}) collective-permute-start(f32[2,2,192,32]{3,2,1,0:T(8,128)S(1)} %get-tuple-element.187), channel_id=1, source_target_pairs={{0,1},{1,2},{2,3},{3,4},{4,5},{5,6},{6,7},{8,9},{9,10},{10,11},{11... | collective-permute-start | bytes 294920 | tf_op jit(solution)/shard_map/ppermute | solution.py:48
  372.8 27.6 %collective-permute-start.19 = (f32[2,2,192,32]{3,2,1,0:T(8,128)S(1)}, f32[2,2,192,32]{3,2,1,0:T(8,128)S(1)}, u32[]{:S(2)}, u32[]{:S(2)}) collective-permute-start(f32[2,2,192,32]{3,2,1,0:T(8,128)S(1)} %get-tuple-element.186), channel_id=1, source_target_pairs={{1,0},{2,1},{3,2},{4,3},{5,4},{6,5},{7,6},{9,8},{10,9},{11,10},{12... | collective-permute-start | bytes 294920 | tf_op jit(solution)/shard_map/ppermute | solution.py:50
  470.1 1.0 copy-start.2
  472.0 196.4 %reduce-scatter.11.cloned.1.call-start = ((), (), s32[]{:S(2)}) async-start(), calls=%async_computation.7 | async-start | bytes 589824 | tf_op jit(solution)/shard_map/reduce_scatter | solution.py:35
  475.3 4.4 collective-permute-start.20
  477.3 150.0 %collective-permute-start.21 = (f32[2,2,32,192]{3,2,1,0:T(8,128)S(1)}, f32[2,2,32,192]{3,2,1,0:T(8,128)S(1)}, u32[]{:S(2)}, u32[]{:S(2)}) collective-permute-start(f32[2,2,32,192]{3,2,1,0:T(8,128)S(1)} %get-tuple-element.162), channel_id=1, source_target_pairs={{0,8},{8,16},{16,24},{24,32},{32,40},{40,48},{48,56},{56,64},{64,7... | collective-permute-start | bytes 294920 | tf_op jit(solution)/shard_map/ppermute | solution.py:22
  627.5 11.1 %collective-permute-start.22 = (f32[2,2,128,32]{3,2,1,0:T(8,128)S(1)}, f32[2,2,128,32]{3,2,1,0:T(8,128)S(1)}, u32[]{:S(2)}, u32[]{:S(2)}) collective-permute-start(f32[2,2,128,32]{3,2,1,0:T(8,128)S(1)} %get-tuple-element.179), channel_id=1, source_target_pairs={{1,0},{2,1},{3,2},{4,3},{5,4},{6,5},{7,6},{9,8},{10,9},{11,10},{12... | collective-permute-start | bytes 196616 | tf_op jit(solution)/shard_map/ppermute | solution.py:22
  628.9 11.8 %collective-permute-start.23 = (f32[2,2,128,32]{3,2,1,0:T(8,128)S(1)}, f32[2,2,128,32]{3,2,1,0:T(8,128)S(1)}, u32[]{:S(2)}, u32[]{:S(2)}) collective-permute-start(f32[2,2,128,32]{3,2,1,0:T(8,128)S(1)} %get-tuple-element.178), channel_id=1, source_target_pairs={{0,1},{1,2},{2,3},{3,4},{4,5},{5,6},{6,7},{8,9},{9,10},{10,11},{11... | collective-permute-start | bytes 196616 | tf_op jit(solution)/shard_map/ppermute | solution.py:22
Sparse Core Ops, SparseCore 0:
  196.8 121.2 reduce-scatter.4
  360.6 42.2 reduce-scatter.6
  472.1 112.8 reduce-scatter.8
  627.4 40.8 reduce-scatter.10
where the time goes:
time: 716 us; the launch traced here: 706 us
  waiting for transfers between devices  325 us (45%)
  blocking collectives  145 us (20%)
  matrix products  111 us (16%)
  starting transfers between devices  70.3 us (10%)
  between operations  26.9 us (4%)
  local copies, waits for them, and re-layouts  24.3 us (3%)
    reduce_scatter x4, waiting for transfers between devices, sum_by_parts(): own = lax.psum_scatter(padded, axis, scatter_dimension=0, tiled=True)  244 us
    all_gather x4, blocking collectives, sum_by_parts(): whole = lax.all_gather(own, axis, axis=0, tiled=True)  145 us
    dot_general x72, matrix products, right_apply(): return jnp.einsum('bij,jk->bik', values, matrix, precision=HIGHEST)  55.9 us
    dot_general x72, matrix products, left_apply(): return jnp.einsum('ij,bjk->bik', matrix, values, precision=HIGHEST)  55.1 us
    ppermute x6, waiting for transfers between devices, extended_2(): lax.ppermute(head, axis, [((i + 1) % count, i) for i in range(ends)])  45.5 us
    ppermute x12, starting transfers between devices, shifted(): return lax.ppermute(block, axis, route)  34.1 us
    ppermute x12, waiting for transfers between devices, shifted(): return lax.ppermute(block, axis, route)  27.7 us
    ppermute x6, starting transfers between devices, extended_2(): lax.ppermute(head, axis, [((i + 1) % count, i) for i in range(ends)])  19 us
  transfers between devices with their start and end apart: 28, of which 20 were waited for; matrix products, arithmetic and copies ran while one was open for 2% of the time, Pallas kernels for 0%

commit v1 on v0

v1 whole, which is shorter than its diff:
```python
import math

import jax
import jax.numpy as jnp
import numpy as np
from jax import lax
from jax.experimental import pallas as pl
from jax.experimental.pallas import tpu as pltpu
from jax.sharding import Mesh, PartitionSpec as P

WIN = 128
OVL = 32
EXT = WIN + 2 * OVL
TALL = EXT + 8
MODES = 4
OBJECT_RATE = 0.5
PROBE_RATE = 0.5
FLOOR = 0.1

AXES = ("z", "xh", "core", "y", "xl")
SIZES = (8, 2, 2, 4, 2)
ROW = ("z", "xh", "core")
COL = ("y", "xl")
CHIPS = ("z", "xh", "y", "xl")
N_ROW = 32
N_COL = 8
N_CHIPS = 128

F32 = jnp.float32
BF16 = jnp.bfloat16


def dft_tables():
    counter = np.arange(WIN, dtype=np.int64)
    phase = (counter[:, None] * counter[None, :] % WIN).astype(np.float64) * (-2.0 * math.pi / WIN)
    cosine = np.cos(phase) / math.sqrt(WIN)
    sine = np.sin(phase) / math.sqrt(WIN)
    forward = np.block([[cosine, sine], [-sine, cosine]])
    out = []
    for table in (forward, forward.T):
        high = table.astype(np.float32).astype(jnp.bfloat16)
        low = (table - high.astype(np.float64)).astype(np.float32).astype(jnp.bfloat16)
        out += [high, low]
    return np.stack(out)


def lanes(shape):
    return lax.broadcasted_iota(jnp.int32, shape, len(shape) - 1)


def split(x):
    high = x.astype(BF16)
    return high, (x - high.astype(F32)).astype(BF16)


def dot(a, b):
    return lax.dot_general(a, b, (((1,), (0,)), ((), ())), preferred_element_type=F32)


def grid_of(blocks):
    return jnp.concatenate([jnp.concatenate(line, axis=1) for line in blocks], axis=0)


def blocks_of(x):
    half = WIN
    return [[x[:half, :half], x[:half, half:]], [x[half:, :half], x[half:, half:]]]


def transposed(blocks):
    return [[blocks[0][0], blocks[1][0]], [blocks[0][1], blocks[1][1]]]


def apply_right(pairs, high, low):
    out = []
    for blocks in pairs:
        xh, xl = split(grid_of(blocks))
        out.append(blocks_of(dot(xh, high) + dot(xh, low) + dot(xl, high)))
    return out


def apply_left(pairs, high, low):
    out = []
    for blocks in pairs:
        xh, xl = split(grid_of(transposed(blocks)))
        out.append(transposed(blocks_of(dot(high, xh) + dot(low, xh) + dot(high, xl))))
    return out


def product(a, b):
    return [a[0] * b[0] - a[1] * b[1], a[0] * b[1] + a[1] * b[0]]


def conj_product(a, b):
    return [a[0] * b[0] + a[1] * b[1], a[0] * b[1] - a[1] * b[0]]


def per_mode(pairs, fn):
    return [[fn(pairs[m // 2][m % 2], m) for m in (2 * k, 2 * k + 1)] for k in range(2)]


def place_window(e_ref, oy, ox, which):
    base = pl.multiple_of(oy // 8 * 8, 8)
    up = (WIN + 8 - oy % 8) % (WIN + 8)
    back = (WIN - ox) % WIN
    parts = []
    for t in range(2):
        rows = e_ref[which, pl.ds(base, WIN + 8), t * WIN : (t + 1) * WIN]
        parts.append(pltpu.roll(pltpu.roll(rows, up, 0)[:WIN], back, 1))
    first, second = parts
    return jnp.where(lanes((WIN, WIN)) < WIN - ox, first, second)


def pack_cols(tile):
    half = EXT // 2
    lane = lanes((half, WIN))
    return jnp.where(lane < 64, tile[:half], pltpu.roll(tile[half:], 64, 1))


def unpack_cols(packed):
    low = lanes(packed.shape) < 64
    return jnp.concatenate(
        [jnp.where(low, packed, 0.0), jnp.where(low, pltpu.roll(packed, 64, 1), 0.0)], axis=0
    )


def pack_rows(first, second):
    lane = lanes((32, WIN))
    rest = jnp.where(lane < 64, second[:32], pltpu.roll(second[32:], 64, 1))
    return jnp.concatenate([first, rest], axis=0)


def unpack_rows(packed):
    rest = packed[64:]
    low = lanes(rest.shape) < 64
    second = jnp.concatenate(
        [jnp.where(low, rest, 0.0), jnp.where(low, pltpu.roll(rest, 64, 1), 0.0)], axis=0
    )
    return packed[:64], second


def halo_kernel(obj, north, south, left, right):
    lane = lanes((48, WIN)) // 32
    for a in range(4):
        column = jnp.concatenate([north[a], obj[a], south[a]], axis=0)
        for ref, base in ((left, 0), (right, 32)):
            out = jnp.zeros((48, WIN), F32)
            for i in range(4):
                part = column[48 * i : 48 * i + 48]
                shift = (32 * i + base) % WIN
                part = pltpu.roll(part, shift, 1) if shift else part
                out = jnp.where(lane == i, part, out)
            ref[a] = out


def build_extended(e_ref, obj, north, south, west, east):
    lane = lanes((EXT, WIN))
    for a in range(4):
        column = jnp.concatenate([north[a], obj[a], south[a]], axis=0)
        column = pltpu.roll(column, 32, 1)
        lefts, rights = [], []
        for i in range(4):
            shift = (WIN - 32 * i) % WIN
            lefts.append(pltpu.roll(west[a], shift, 1) if shift else west[a])
            shift = (32 - 32 * i) % WIN
            rights.append(pltpu.roll(east[a], shift, 1) if shift else east[a])
        e_ref[a, :EXT, :WIN] = jnp.where(lane < 32, jnp.concatenate(lefts, axis=0), column)
        e_ref[a, :EXT, WIN:] = jnp.where(
            lane < 32, column, jnp.where(lane < 64, jnp.concatenate(rights, axis=0), 0.0)
        )


def update_extended(e_ref, info, old, grad, north, south):
    row = lax.broadcasted_iota(jnp.int32, (EXT, WIN), 0)
    lane = lanes((EXT, WIN))
    in_rows = (row >= info[2]) & (row < info[3])
    keep = (in_rows & (lane >= info[4]), in_rows & (lane + WIN < info[5]))
    gap = jnp.zeros((64, WIN), F32)
    for a in range(4):
        n_parts = unpack_rows(north[a])
        s_parts = unpack_rows(south[a])
        for t in range(2):
            cols = slice(t * WIN, (t + 1) * WIN)
            bands = jnp.concatenate([n_parts[t], gap, s_parts[t]], axis=0)
            value = old[a, :EXT, cols] - OBJECT_RATE * (grad[a, :EXT, cols] + bands)
            e_ref[a, :EXT, cols] = jnp.where(keep[t], value, 0.0)


def step_core(info, e_ref, probe, kernel, measured, tables, g_ref, left, right):
    oy, ox = info[0], info[1]
    a_high, a_low, b_high, b_low = (tables[i] for i in range(4))
    o1 = [place_window(e_ref, oy, ox, 0), place_window(e_ref, oy, ox, 1)]
    o2 = [place_window(e_ref, oy, ox, 2), place_window(e_ref, oy, ox, 3)]
    phase = [kernel[0], kernel[1]]
    x = per_mode(probe, lambda p, m: product(p, o1))
    x = apply_left(apply_right(x, a_high, a_low), b_high, b_low)
    x = per_mode(x, lambda v, m: product(phase, v))
    phi = apply_right(apply_left(x, a_high, a_low), b_high, b_low)
    x = per_mode(phi, lambda v, m: product(v, o2))
    x = apply_left(apply_right(x, a_high, a_low), b_high, b_low)
    intensity = sum(x[m // 2][m % 2][c] * x[m // 2][m % 2][c] for m in range(MODES) for c in range(2))
    factor = 1.0 - measured / jnp.sqrt(intensity + FLOOR)
    x = per_mode(x, lambda v, m: [v[0] * factor, v[1] * factor])
    chi2 = apply_right(apply_left(x, a_high, a_low), b_high, b_low)
    terms2 = [conj_product(phi[m // 2][m % 2], chi2[m // 2][m % 2]) for m in range(MODES)]
    x = per_mode(chi2, lambda v, m: conj_product(o2, v))
    x = apply_left(apply_right(x, a_high, a_low), b_high, b_low)
    x = per_mode(x, lambda v, m: conj_product(phase, v))
    chi1 = apply_right(apply_left(x, a_high, a_low), b_high, b_low)
    terms1 = [conj_product(probe[m // 2][m % 2], chi1[m // 2][m % 2]) for m in range(MODES)]
    grads = [sum(t[c] for t in terms1) for c in range(2)] + [sum(t[c] for t in terms2) for c in range(2)]
    lane = lanes((WIN, WIN))
    base = pl.multiple_of(oy // 8 * 8, 8)
    gap = jnp.zeros((8, WIN), F32)
    for a in range(4):
        g_ref[a] = jnp.zeros((TALL, 2 * WIN), F32)
        turned = pltpu.roll(grads[a], ox, 1)
        for t in range(2):
            part = jnp.where(lane >= ox if t == 0 else lane < ox, turned, 0.0)
            part = pltpu.roll(jnp.concatenate([part, gap], axis=0), oy % 8, 0)
            g_ref[a, pl.ds(base, WIN + 8), t * WIN : (t + 1) * WIN] = part
        left[a] = pack_cols(g_ref[a, :EXT, :WIN])
        right[a] = pack_cols(g_ref[a, :EXT, WIN:])
    return per_mode(chi1, lambda v, m: conj_product(o1, v))


def probe_blocks(probe_ref):
    return [[[probe_ref[2 * m], probe_ref[2 * m + 1]] for m in (2 * k, 2 * k + 1)] for k in range(2)]


def write_halves(info, grads, keep, send, add=None):
    first = info[6] == 0
    for i in range(4):
        low = grads[0][i // 2][i % 2]
        high = grads[1][i // 2][i % 2]
        kept = jnp.where(first, low, high)
        sent = jnp.where(first, high, low)
        if add is not None:
            kept = kept + add[0][i]
            sent = sent + add[1][i]
        keep[i] = kept
        send[i] = sent


def first_kernel(info, obj, north, south, west, east, probe, kernel, measured, tables,
                 e_ref, g_ref, left, right, keep, send):
    build_extended(e_ref, obj, north, south, west, east)
    grads = step_core(info, e_ref, probe_blocks(probe), kernel, measured[...], tables, g_ref, left, right)
    write_halves(info, grads, keep, send)


def second_kernel(info, old, grad, north, south, probe, kernel, measured, tables,
                  e_ref, g_ref, left, right, keep, send):
    update_extended(e_ref, info, old, grad, north, south)
    grads = step_core(info, e_ref, probe_blocks(probe), kernel, measured[...], tables, g_ref, left, right)
    write_halves(info, grads, keep, send)


def third_kernel(rate, info, old, grad, north, south, probe, mine, other, keep_add, send_add,
                 kernel, measured, tables,
                 e_ref, g_ref, left, right, keep, send, p_ref):
    update_extended(e_ref, info, old, grad, north, south)
    first = info[6] == 0
    for i in range(4):
        p_ref[i] = probe[i] - rate * jnp.where(first, mine[i], other[i])
        p_ref[4 + i] = probe[4 + i] - rate * jnp.where(first, other[i], mine[i])
    grads = step_core(info, e_ref, probe_blocks(p_ref), kernel, measured[...], tables, g_ref, left, right)
    write_halves(info, grads, keep, send, (keep_add, send_add))


def middle_kernel(g_in, west, east, g_ref, up, down):
    for a in range(4):
        g_ref[a, :EXT, :WIN] = g_in[a, :EXT, :WIN] + unpack_cols(west[a])
        g_ref[a, :EXT, WIN:] = g_in[a, :EXT, WIN:] + unpack_cols(east[a])
        up[a] = pack_rows(g_ref[a, :64, :WIN], g_ref[a, :64, WIN:])
        down[a] = pack_rows(g_ref[a, 128:EXT, :WIN], g_ref[a, 128:EXT, WIN:])


def object_kernel(old, grad, north, south, out):
    lane = lanes((WIN, WIN))
    gap = jnp.zeros((64, WIN), F32)
    for a in range(4):
        n_parts = unpack_rows(north[a])
        s_parts = unpack_rows(south[a])
        parts = []
        for t in range(2):
            cols = slice(t * WIN, (t + 1) * WIN)
            bands = jnp.concatenate([n_parts[t], gap, s_parts[t]], axis=0)
            value = old[a, :EXT, cols] - OBJECT_RATE * (grad[a, :EXT, cols] + bands)
            parts.append(pltpu.roll(value[OVL : OVL + WIN], WIN - OVL, 1))
        out[a] = jnp.where(lane < WIN - OVL, parts[0], parts[1])


def probe_kernel(rate, info, probe, mine, other, out):
    first = info[6] == 0
    for i in range(4):
        out[i] = probe[i] - rate * jnp.where(first, mine[i], other[i])
        out[4 + i] = probe[4 + i] - rate * jnp.where(first, other[i], mine[i])


SMEM = pl.BlockSpec(memory_space=pltpu.SMEM)
VMEM = pl.BlockSpec(memory_space=pltpu.VMEM)


def call(kernel, outs, *args, scalars=0, name=None):
    return pl.pallas_call(
        kernel,
        out_shape=[jax.ShapeDtypeStruct(s, F32) for s in outs],
        in_specs=[SMEM] * scalars + [VMEM] * (len(args) - scalars),
        out_specs=[VMEM] * len(outs),
        name=name,
    )(*args)


EXT_SHAPE = (4, TALL, 2 * WIN)
BAND = (4, EXT // 2, WIN)
HALF = (4, WIN, WIN)


def moved(x, axis, size, distance):
    route = [(i, i + distance) for i in range(size) if 0 <= i + distance < size]
    return lax.ppermute(x, axis, route)


def swap_cores(x):
    return lax.ppermute(x, "core", [(0, 1), (1, 0)])


def summed_half(keep, send):
    total = keep + swap_cores(send)
    parts = lax.all_to_all(total.reshape(N_CHIPS, -1, WIN), CHIPS, 0, 0, tiled=True)
    own = jnp.sum(parts, axis=0)
    whole = lax.all_to_all(
        jnp.broadcast_to(own[None], (N_CHIPS, *own.shape)), CHIPS, 0, 0, tiled=True
    )
    return whole.reshape(HALF)


def exchanged(grad, left, right):
    west = moved(right, COL, N_COL, 1)
    east = moved(left, COL, N_COL, -1)
    grad, up, down = call(middle_kernel, [EXT_SHAPE, BAND, BAND], grad, west, east, name="middle")
    north = moved(down, ROW, N_ROW, 1)
    south = moved(up, ROW, N_ROW, -1)
    return grad, north, south


def per_device(object_field, probe, kernel_phase, amplitudes, offsets):
    rate = PROBE_RATE / math.sqrt(N_ROW * N_COL)
    tables = jnp.asarray(dft_tables())
    kernel = jnp.stack([jnp.cos(kernel_phase), jnp.sin(kernel_phase)])
    row = lax.axis_index(ROW)
    col = lax.axis_index(COL)
    core = lax.axis_index("core")
    edges = jnp.stack([
        jnp.where(row == 0, OVL, 0),
        jnp.where(row == N_ROW - 1, EXT - OVL, EXT),
        jnp.where(col == 0, OVL, 0),
        jnp.where(col == N_COL - 1, EXT - OVL, EXT),
        core,
    ]).astype(jnp.int32)
    infos = [jnp.concatenate([offsets[b, 0, 0], edges]) for b in range(3)]
    measured = amplitudes[:, 0, 0]
    obj = object_field.reshape(4, WIN, WIN)
    probe = probe.reshape(2 * MODES, WIN, WIN)

    north = moved(obj[:, WIN - OVL :], ROW, N_ROW, 1)
    south = moved(obj[:, :OVL], ROW, N_ROW, -1)
    left, right = call(halo_kernel, [(4, 48, WIN)] * 2, obj, north, south, name="halo")
    west = moved(right, COL, N_COL, 1)
    east = moved(left, COL, N_COL, -1)

    step_outs = [EXT_SHAPE, EXT_SHAPE, BAND, BAND, HALF, HALF]
    extended, grad, left, right, keep0, send0 = call(
        first_kernel, step_outs, infos[0], obj, north, south, west, east, probe, kernel,
        measured[0], tables, scalars=1, name="step0",
    )
    grad, north, south = exchanged(grad, left, right)
    mine0 = summed_half(keep0, send0)
    other0 = swap_cores(mine0)
    extended, grad, left, right, keep1, send1 = call(
        second_kernel, step_outs, infos[1], extended, grad, north, south, probe, kernel,
        measured[1], tables, scalars=1, name="step1",
    )
    grad, north, south = exchanged(grad, left, right)
    extended, grad, left, right, keep2, send2, probe = call(
        lambda *refs: third_kernel(rate, *refs), step_outs + [(2 * MODES, WIN, WIN)],
        infos[2], extended, grad, north, south, probe, mine0, other0, keep1, send1, kernel,
        measured[2], tables, scalars=1, name="step2",
    )
    grad, north, south = exchanged(grad, left, right)
    mine = summed_half(keep2, send2)
    other = swap_cores(mine)
    (obj,) = call(object_kernel, [HALF], extended, grad, north, south, name="object")
    (probe,) = call(
        lambda *refs: probe_kernel(rate, *refs), [(2 * MODES, WIN, WIN)],
        infos[2], probe, mine, other, scalars=1, name="probe",
    )
    return obj.reshape(2, 2, WIN, WIN), probe.reshape(MODES, 2, WIN, WIN)


def solution(mesh):
    fine = Mesh(mesh.devices.reshape(SIZES), AXES)
    in_specs = (
        P(None, None, ROW, COL),
        P(),
        P(),
        P(None, ROW, COL, None, None),
        P(None, ROW, COL, None),
    )
    out_specs = (P(None, None, ROW, COL), P())
    return jax.shard_map(
        per_device, mesh=fine, in_specs=in_specs, out_specs=out_specs, check_vma=False
    )
```

time: 716 us -> 217 us (0.30)
  the two profiles are of different devices: /device:TPU:4 before, /device:TPU:1 now
where the time goes in v1:
time: 217 us; the launch traced here: 216 us
  starting transfers between devices  83.2 us (38%)
  waiting for transfers between devices  49.1 us (23%)
  Pallas kernels  37.7 us (17%)
  blocking collectives  29.5 us (14%)
  local copies, waits for them, and re-layouts  12.2 us (6%)
  other arithmetic  3.64 us (2%)
    ppermute x16, starting transfers between devices, moved(): return lax.ppermute(x, axis, route)  45.3 us
    pallas_call x9, Pallas kernels, call(): pl.pallas_call(kernel, out_shape=[jax.ShapeDtypeStruct(s, F32) for s in o...  37.7 us
    all_to_all x1, blocking collectives, summed_half(): lax.all_to_all(total.reshape(N_CHIPS, -1, WIN), CHIPS, 0, 0, tiled=True)  29.5 us
    ppermute x16, waiting for transfers between devices, moved(): return lax.ppermute(x, axis, route)  28.6 us
    all_to_all x1, starting transfers between devices, summed_half(): lax.all_to_all(total.reshape(N_CHIPS, -1, WIN), CHIPS, 0, 0, tiled=True)  20.1 us
    all_to_all x2, starting transfers between devices, summed_half(): lax.all_to_all(jnp.broadcast_to(own[None], (N_CHIPS, *own.shape)), CHIPS,...  14.2 us
    all_to_all x1, waiting for transfers between devices, summed_half(): lax.all_to_all(total.reshape(N_CHIPS, -1, WIN), CHIPS, 0, 0, tiled=True)  8.87 us
    all_to_all x2, waiting for transfers between devices, summed_half(): lax.all_to_all(jnp.broadcast_to(own[None], (N_CHIPS, *own.shape)), CHIPS,...  8.15 us
  transfers between devices with their start and end apart: 23, of which 13 were waited for; matrix products, arithmetic and copies ran while one was open for 2% of the time, Pallas kernels for 8%

profile of v1, /device:TPU:1, one launch (start us, length us, event | category | flops | bytes accessed | tf_op | source)
XLA Modules:
  0.0 216.4 jit_solution(7944005782156730688)
XLA Ops:
  0.6 0.9 fusion
  1.6 5.1 %collective-permute-start.1 = (f32[4,32,128]{2,1,0:T(8,128)S(1)}, f32[4,32,128]{2,1,0:T(8,128)S(1)}, u32[]{:S(2)}, u32[]{:S(2)}) collective-permute-start(f32[4,32,128]{2,1,0:T(8,128)S(1)} %get-tuple-element.65), channel_id=1, source_target_pairs={{8,0},{16,8},{24,16},{32,24},{40,32},{48,40},{56,48},{64,56},{72,6... | collective-permute-start | bytes 196616 | tf_op jit(solution)/shard_map/ppermute | solution.py:321
  6.7 2.8 %collective-permute-start = (f32[4,32,128]{2,1,0:T(8,128)S(1)}, f32[4,32,128]{2,1,0:T(8,128)S(1)}, u32[]{:S(2)}, u32[]{:S(2)}) collective-permute-start(f32[4,32,128]{2,1,0:T(8,128)S(1)} %get-tuple-element.66), channel_id=1, source_target_pairs={{0,8},{8,16},{16,24},{24,32},{32,40},{40,48},{48,56},{56,64},{64,7... | collective-permute-start | bytes 196616 | tf_op jit(solution)/shard_map/ppermute | solution.py:321
  9.6 0.2 cosine_bitcast_fusion
  9.9 0.7 slice_bitcast_fusion
  10.6 0.2 slice_reduce_fusion
  10.7 0.6 concatenate.14.info
  11.3 0.6 copy-done.3
  12.0 0.6 copy-done.4
  12.6 1.9 halo.1
  14.5 3.0 %collective-permute-start.2 = (f32[4,48,128]{2,1,0:T(8,128)}, f32[4,48,128]{2,1,0:T(8,128)S(1)}, u32[]{:S(2)}, u32[]{:S(2)}) collective-permute-start(f32[4,48,128]{2,1,0:T(8,128)} %get-tuple-element.32), channel_id=1, source_target_pairs={{0,1},{1,2},{2,3},{3,4},{4,5},{5,6},{6,7},{8,9},{9,10},{10,11},{11... | collective-permute-start | bytes 294920 | tf_op jit(solution)/shard_map/ppermute | solution.py:321
  17.5 1.3 collective-permute-start.3
  18.8 0.7 pad_maximum_fusion.kernel.refs_10_
  19.5 3.7 %collective-permute-done.3.east = f32[4,48,128]{2,1,0:T(8,128)S(1)} collective-permute-done((f32[4,48,128]{2,1,0:T(8,128)}, f32[4,48,128]{2,1,0:T(8,128)S(1)}, u32[]{:S(2)}, u32[]{:S(2)}) %collective-permute-start.3) | collective-permute-done | bytes 98336 | tf_op jit(solution)/shard_map/ppermute | solution.py:321
  23.1 0.6 copy-done.20
  23.8 7.6 %step0.1 = (f32[4,200,256]{2,1,0:T(8,128)}, f32[4,200,256]{2,1,0:T(8,128)}, f32[4,96,128]{2,1,0:T(8,128)}, f32[4,96,128]{2,1,0:T(8,128)}, f32[4,128,128]{2,1,0:T(8,128)}, /*index=5*/f32[4,128,128]{2,1,0:T(8,128)}) custom-call(s32[7]{0:T(128)} %concatenate.14.info, f32[4,128,128]{2,1,0:T(8,128)} %bitcast.28, f32[4,32,128]{2,1,0:T(8,128)} %copy-done.4, ...), custom_call_target="tpu_custom_call" | custom-call | tf_op jit(solution)/shard_map/step0/pallas_call | solution.py:305
  31.4 1.7 collective-permute-done.12
  33.1 1.7 add.18
  34.8 20.1 %all-to-all-start = ((f32[128,4,128]{2,1,0:T(4,128)}), f32[128,4,128]{2,1,0:T(4,128)S(1)}, u32[]{:S(2)}, u32[]{:S(2)}) async-start(f32[128,4,128]{2,1,0:T(4,128)} %bitcast.11), calls=%async_computation | async-start | bytes 524288 | tf_op jit(solution)/shard_map/all_to_all | solution.py:330
  54.9 2.5 %collective-permute-start.4 = (f32[4,96,128]{2,1,0:T(8,128)S(1)}, f32[4,96,128]{2,1,0:T(8,128)S(1)}, u32[]{:S(2)}, u32[]{:S(2)}) collective-permute-start(f32[4,96,128]{2,1,0:T(8,128)S(1)} %copy-done.26), channel_id=1, source_target_pairs={{0,1},{1,2},{2,3},{3,4},{4,5},{5,6},{6,7},{8,9},{9,10},{10,11},{11... | collective-permute-start | bytes 589832 | tf_op jit(solution)/shard_map/ppermute | solution.py:321
  57.4 1.3 collective-permute-start.5
  58.7 8.9 %all-to-all-done = f32[128,4,128]{2,1,0:T(4,128)S(1)} async-done(((f32[128,4,128]{2,1,0:T(4,128)}), f32[128,4,128]{2,1,0:T(4,128)S(1)}, u32[]{:S(2)}, u32[]{:S(2)}) %all-to-all-start) | async-done | bytes 262176 | tf_op jit(solution)/shard_map/all_to_all | solution.py:330
  67.7 0.7 broadcast_in_dim.4
  68.4 7.1 %all-to-all-start.1 = ((f32[128,4,128]{2,1,0:T(4,128)}), f32[128,4,128]{2,1,0:T(4,128)S(1)}, u32[]{:S(2)}, u32[]{:S(2)}) async-start(f32[128,4,128]{2,1,0:T(4,128)} %broadcast_in_dim.4), calls=%async_computation.1 | async-start | bytes 524288 | tf_op jit(solution)/shard_map/all_to_all | solution.py:332
  75.6 0.6 copy-done.8
  76.3 2.5 %middle.3 = (f32[4,200,256]{2,1,0:T(8,128)}, f32[4,96,128]{2,1,0:T(8,128)}, f32[4,96,128]{2,1,0:T(8,128)}) custom-call(f32[4,200,256]{2,1,0:T(8,128)} %get-tuple-element.35.g_in, f32[4,96,128]{2,1,0:T(8,128)} %copy-done.8, f32[4,96,128]{2,1,0:T(8,128)} %copy-done.9), custom_call_target="tpu_custom_call" | custom-call | tf_op jit(solution)/shard_map/middle/pallas_call | solution.py:305
  78.9 6.0 %collective-permute-start.6 = (f32[4,96,128]{2,1,0:T(8,128)}, f32[4,96,128]{2,1,0:T(8,128)S(1)}, u32[]{:S(2)}, u32[]{:S(2)}) collective-permute-start(f32[4,96,128]{2,1,0:T(8,128)} %get-tuple-element.39), channel_id=1, source_target_pairs={{0,8},{8,16},{16,24},{24,32},{32,40},{40,48},{48,56},{56,64},{64,7... | collective-permute-start | bytes 589832 | tf_op jit(solution)/shard_map/ppermute | solution.py:321
  84.9 2.1 collective-permute-start.7
  87.0 0.6 concatenate.13.info
  87.8 5.8 %collective-permute-done.7.south = f32[4,96,128]{2,1,0:T(8,128)S(1)} collective-permute-done((f32[4,96,128]{2,1,0:T(8,128)}, f32[4,96,128]{2,1,0:T(8,128)S(1)}, u32[]{:S(2)}, u32[]{:S(2)}) %collective-permute-start.7) | collective-permute-done | bytes 196640 | tf_op jit(solution)/shard_map/ppermute | solution.py:321
  93.6 0.7 copy-done.18
  94.2 7.7 %step1.1 = (f32[4,200,256]{2,1,0:T(8,128)}, f32[4,200,256]{2,1,0:T(8,128)}, f32[4,96,128]{2,1,0:T(8,128)}, f32[4,96,128]{2,1,0:T(8,128)}, f32[4,128,128]{2,1,0:T(8,128)}, /*index=5*/f32[4,128,128]{2,1,0:T(8,128)}) custom-call(s32[7]{0:T(128)} %concatenate.13.info, f32[4,200,256]{2,1,0:T(8,128)} %get-tuple-element.34.old, ...), custom_call_target="tpu_custom_call" | custom-call | tf_op jit(solution)/shard_map/step1/pallas_call | solution.py:305
  101.9 2.2 %collective-permute-start.8 = (f32[4,96,128]{2,1,0:T(8,128)}, f32[4,96,128]{2,1,0:T(8,128)S(1)}, u32[]{:S(2)}, u32[]{:S(2)}) collective-permute-start(f32[4,96,128]{2,1,0:T(8,128)} %get-tuple-element.43), channel_id=1, source_target_pairs={{0,1},{1,2},{2,3},{3,4},{4,5},{5,6},{6,7},{8,9},{9,10},{10,11},{11... | collective-permute-start | bytes 589832 | tf_op jit(solution)/shard_map/ppermute | solution.py:321
  104.1 1.3 collective-permute-start.9
  105.5 1.5 collective-permute-done.8.west
  107.0 4.5 %collective-permute-done.9.east = f32[4,96,128]{2,1,0:T(8,128)S(1)} collective-permute-done((f32[4,96,128]{2,1,0:T(8,128)}, f32[4,96,128]{2,1,0:T(8,128)S(1)}, u32[]{:S(2)}, u32[]{:S(2)}) %collective-permute-start.9) | collective-permute-done | bytes 196640 | tf_op jit(solution)/shard_map/ppermute | solution.py:321
  111.6 0.7 copy-done.12
  112.2 2.5 %middle.4 = (f32[4,200,256]{2,1,0:T(8,128)}, f32[4,96,128]{2,1,0:T(8,128)}, f32[4,96,128]{2,1,0:T(8,128)}) custom-call(f32[4,200,256]{2,1,0:T(8,128)} %get-tuple-element.42.g_in, f32[4,96,128]{2,1,0:T(8,128)} %copy-done.10, f32[4,96,128]{2,1,0:T(8,128)} %copy-done.12), custom_call_target="tpu_custom_call" | custom-call | tf_op jit(solution)/shard_map/middle/pallas_call | solution.py:305
  114.8 5.7 %collective-permute-start.10 = (f32[4,96,128]{2,1,0:T(8,128)}, f32[4,96,128]{2,1,0:T(8,128)S(1)}, u32[]{:S(2)}, u32[]{:S(2)}) collective-permute-start(f32[4,96,128]{2,1,0:T(8,128)} %get-tuple-element.46), channel_id=1, source_target_pairs={{0,8},{8,16},{16,24},{24,32},{32,40},{40,48},{48,56},{56,64},{64,7... | collective-permute-start | bytes 589832 | tf_op jit(solution)/shard_map/ppermute | solution.py:321
  120.4 1.9 collective-permute-start.11
  122.4 0.6 concatenate.12.refs_0_
  123.0 0.4 collective-permute-done.10.refs_3_
  123.4 5.8 %collective-permute-done.11.refs_4_ = f32[4,96,128]{2,1,0:T(8,128)S(1)} collective-permute-done((f32[4,96,128]{2,1,0:T(8,128)}, f32[4,96,128]{2,1,0:T(8,128)S(1)}, u32[]{:S(2)}, u32[]{:S(2)}) %collective-permute-start.11) | collective-permute-done | bytes 196640 | tf_op jit(solution)/shard_map/ppermute | solution.py:321
  129.2 0.7 copy-done.7
  129.9 8.4 %step2.1 = (f32[4,200,256]{2,1,0:T(8,128)}, f32[4,200,256]{2,1,0:T(8,128)}, f32[4,96,128]{2,1,0:T(8,128)}, f32[4,96,128]{2,1,0:T(8,128)}, f32[4,128,128]{2,1,0:T...) custom-call(s32[7]{0:T(128)} %concatenate.12.refs_0_, f32[4,200,256]{2,1,0:T(8,128)} %get-tuple-element.41.refs_1_, ...), custom_call_target="tpu_custom_call" | custom-call | tf_op jit(solution)/shard_map/step2/pallas_call | solution.py:305
  138.5 1.7 collective-permute-done.18
  140.2 1.0 add.19
  141.2 29.5 %all_to_all.20 = f32[128,4,128]{2,1,0:T(4,128)S(1)} all-to-all(f32[128,4,128]{2,1,0:T(4,128)S(1)} %bitcast.31), channel_id=1, replica_groups=mesh['z'=8,'xh'=2,'core'=2,'y'=4,'xl'=2] {'z','xh','y','xl'}, dimensions={0} | all-to-all | bytes 524288 | tf_op jit(solution)/shard_map/all_to_all | solution.py:330
  170.8 0.7 broadcast_in_dim.5
  171.6 7.1 %all-to-all-start.3 = ((f32[128,4,128]{2,1,0:T(4,128)}), f32[128,4,128]{2,1,0:T(4,128)S(1)}, u32[]{:S(2)}, u32[]{:S(2)}) async-start(f32[128,4,128]{2,1,0:T(4,128)} %broadcast_in_dim.5), calls=%async_computation.3 | async-start | bytes 524288 | tf_op jit(solution)/shard_map/all_to_all | solution.py:332
  178.6 2.5 %collective-permute-start.14 = (f32[4,96,128]{2,1,0:T(8,128)S(1)}, f32[4,96,128]{2,1,0:T(8,128)S(1)}, u32[]{:S(2)}, u32[]{:S(2)}) collective-permute-start(f32[4,96,128]{2,1,0:T(8,128)S(1)} %copy-done.24), channel_id=1, source_target_pairs={{0,1},{1,2},{2,3},{3,4},{4,5},{5,6},{6,7},{8,9},{9,10},{10,11},{11... | collective-permute-start | bytes 589832 | tf_op jit(solution)/shard_map/ppermute | solution.py:321
  181.1 1.3 collective-permute-start.15
  182.4 8.1 %all-to-all-done.3 = f32[128,4,128]{2,1,0:T(4,128)S(1)} async-done(((f32[128,4,128]{2,1,0:T(4,128)}), f32[128,4,128]{2,1,0:T(4,128)S(1)}, u32[]{:S(2)}, u32[]{:S(2)}) %all-to-all-start.3) | async-done | bytes 262176 | tf_op jit(solution)/shard_map/all_to_all | solution.py:332
  190.6 3.5 %collective-permute-start.19 = (f32[4,128,128]{2,1,0:T(8,128)S(1)}, f32[4,128,128]{2,1,0:T(8,128)S(1)}, u32[]{:S(2)}, u32[]{:S(2)}) collective-permute-start(f32[4,128,128]{2,1,0:T(8,128)S(1)} %bitcast.32), channel_id=1, source_target_pairs={{0,8},{8,0},{1,9},{9,1},{2,10},{10,2},{3,11},{11,3},{4,12},{12,4},... | collective-permute-start | bytes 786440 | tf_op jit(solution)/shard_map/ppermute | solution.py:325
  194.1 0.7 copy-done.11
  194.8 2.5 %middle.5 = (f32[4,200,256]{2,1,0:T(8,128)}, f32[4,96,128]{2,1,0:T(8,128)}, f32[4,96,128]{2,1,0:T(8,128)}) custom-call(f32[4,200,256]{2,1,0:T(8,128)} %get-tuple-element.53.g_in, f32[4,96,128]{2,1,0:T(8,128)} %copy-done.11, f32[4,96,128]{2,1,0:T(8,128)} %copy-done.13), custom_call_target="tpu_custom_call" | custom-call | tf_op jit(solution)/shard_map/middle/pallas_call | solution.py:305
  197.4 4.4 %collective-permute-start.16 = (f32[4,96,128]{2,1,0:T(8,128)}, f32[4,96,128]{2,1,0:T(8,128)S(1)}, u32[]{:S(2)}, u32[]{:S(2)}) collective-permute-start(f32[4,96,128]{2,1,0:T(8,128)} %get-tuple-element.57), channel_id=1, source_target_pairs={{0,8},{8,16},{16,24},{24,32},{32,40},{40,48},{48,56},{56,64},{64,7... | collective-permute-start | bytes 589832 | tf_op jit(solution)/shard_map/ppermute | solution.py:321
  201.8 1.9 collective-permute-start.17
  203.7 1.0 collective-permute-done.16.north
  204.7 5.8 %collective-permute-done.17.south = f32[4,96,128]{2,1,0:T(8,128)S(1)} collective-permute-done((f32[4,96,128]{2,1,0:T(8,128)}, f32[4,96,128]{2,1,0:T(8,128)S(1)}, u32[]{:S(2)}, u32[]{:S(2)}) %collective-permute-start.17) | collective-permute-done | bytes 196640 | tf_op jit(solution)/shard_map/ppermute | solution.py:321
  210.5 0.7 copy-done.15
  211.2 2.5 %object.1 = f32[4,128,128]{2,1,0:T(8,128)} custom-call(f32[4,200,256]{2,1,0:T(8,128)} %get-tuple-element.52.old, f32[4,200,256]{2,1,0:T(8,128)} %get-tuple-element.56.grad, f32[4,96,128]{2,1,0:T(8,128)} %copy-done.14, f32[4,96,128]{2,1,0:T(8,128)} %copy-done.15), custom_call_target="tpu_custom_call" | custom-call | tf_op jit(solution)/shard_map/object/pallas_call | solution.py:305
  213.7 0.7 copy-done.5
  214.4 2.0 probe.1
  (60 shorter events, 1.0 us)
Async XLA Ops:
  0.6 8.9 %copy-start.21 = (f32[128,128]{1,0:T(8,128)S(1)}, f32[128,128]{1,0:T(8,128)}, u32[]{:S(2)}) copy-start(f32[128,128]{1,0:T(8,128)} %param.8) | copy-start | bytes 196612
  0.6 9.2 %copy-start.16 = (f32[3,1,1,128,128]{4,3,2,1,0:T(8,128)S(1)}, f32[3,1,1,128,128]{4,3,2,1,0:T(8,128)}, u32[]{:S(2)}) copy-start(f32[3,1,1,128,128]{4,3,2,1,0:T(8,128)} %param.9) | copy-start | bytes 589828
  1.6 9.8 %collective-permute-start.1 = (f32[4,32,128]{2,1,0:T(8,128)S(1)}, f32[4,32,128]{2,1,0:T(8,128)S(1)}, u32[]{:S(2)}, u32[]{:S(2)}) collective-permute-start(f32[4,32,128]{2,1,0:T(8,128)S(1)} %get-tuple-element.65), channel_id=1, source_target_pairs={{8,0},{16,8},{24,16},{32,24},{40,32},{48,40},{56,48},{64,56},{72,6... | collective-permute-start | bytes 196616 | tf_op jit(solution)/shard_map/ppermute | solution.py:321
  6.7 4.6 %collective-permute-start = (f32[4,32,128]{2,1,0:T(8,128)S(1)}, f32[4,32,128]{2,1,0:T(8,128)S(1)}, u32[]{:S(2)}, u32[]{:S(2)}) collective-permute-start(f32[4,32,128]{2,1,0:T(8,128)S(1)} %get-tuple-element.66), channel_id=1, source_target_pairs={{0,8},{8,16},{16,24},{24,32},{32,40},{40,48},{48,56},{56,64},{64,7... | collective-permute-start | bytes 196616 | tf_op jit(solution)/shard_map/ppermute | solution.py:321
  9.8 0.7 copy-start.22
  11.3 0.6 copy-start.3
  12.0 0.6 copy-start.4
  14.5 5.0 %collective-permute-start.2 = (f32[4,48,128]{2,1,0:T(8,128)}, f32[4,48,128]{2,1,0:T(8,128)S(1)}, u32[]{:S(2)}, u32[]{:S(2)}) collective-permute-start(f32[4,48,128]{2,1,0:T(8,128)} %get-tuple-element.32), channel_id=1, source_target_pairs={{0,1},{1,2},{2,3},{3,4},{4,5},{5,6},{6,7},{8,9},{9,10},{10,11},{11... | collective-permute-start | bytes 294920 | tf_op jit(solution)/shard_map/ppermute | solution.py:321
  17.5 5.6 %collective-permute-start.3 = (f32[4,48,128]{2,1,0:T(8,128)}, f32[4,48,128]{2,1,0:T(8,128)S(1)}, u32[]{:S(2)}, u32[]{:S(2)}) collective-permute-start(f32[4,48,128]{2,1,0:T(8,128)} %get-tuple-element.33), channel_id=1, source_target_pairs={{1,0},{2,1},{3,2},{4,3},{5,4},{6,5},{7,6},{9,8},{10,9},{11,10},{12... | collective-permute-start | bytes 294920 | tf_op jit(solution)/shard_map/ppermute | solution.py:321
  19.5 3.7 %copy-start.19 = (f32[4,48,128]{2,1,0:T(8,128)}, f32[4,48,128]{2,1,0:T(8,128)S(1)}, u32[]{:S(2)}) copy-start(f32[4,48,128]{2,1,0:T(8,128)S(1)} %collective-permute-done.2.west) | copy-start | bytes 294916
  23.1 0.6 copy-start.20
  31.3 1.7 collective-permute-start.12
  34.8 20.1 %copy-start.26 = (f32[4,96,128]{2,1,0:T(8,128)S(1)}, f32[4,96,128]{2,1,0:T(8,128)}, u32[]{:S(2)}) copy-start(f32[4,96,128]{2,1,0:T(8,128)} %get-tuple-element.36) | copy-start | bytes 589828
  34.8 22.6 %copy-start.25 = (f32[4,96,128]{2,1,0:T(8,128)S(1)}, f32[4,96,128]{2,1,0:T(8,128)}, u32[]{:S(2)}) copy-start(f32[4,96,128]{2,1,0:T(8,128)} %get-tuple-element.37) | copy-start | bytes 589828
  34.8 32.8 %all-to-all-start = ((f32[128,4,128]{2,1,0:T(4,128)}), f32[128,4,128]{2,1,0:T(4,128)S(1)}, u32[]{:S(2)}, u32[]{:S(2)}) async-start(f32[128,4,128]{2,1,0:T(4,128)} %bitcast.11), calls=%async_computation | async-start | bytes 524288 | tf_op jit(solution)/shard_map/all_to_all | solution.py:330
  54.9 20.7 %collective-permute-start.4 = (f32[4,96,128]{2,1,0:T(8,128)S(1)}, f32[4,96,128]{2,1,0:T(8,128)S(1)}, u32[]{:S(2)}, u32[]{:S(2)}) collective-permute-start(f32[4,96,128]{2,1,0:T(8,128)S(1)} %copy-done.26), channel_id=1, source_target_pairs={{0,1},{1,2},{2,3},{3,4},{4,5},{5,6},{6,7},{8,9},{9,10},{10,11},{11... | collective-permute-start | bytes 589832 | tf_op jit(solution)/shard_map/ppermute | solution.py:321
  57.4 18.2 %collective-permute-start.5 = (f32[4,96,128]{2,1,0:T(8,128)S(1)}, f32[4,96,128]{2,1,0:T(8,128)S(1)}, u32[]{:S(2)}, u32[]{:S(2)}) collective-permute-start(f32[4,96,128]{2,1,0:T(8,128)S(1)} %copy-done.25), channel_id=1, source_target_pairs={{1,0},{2,1},{3,2},{4,3},{5,4},{6,5},{7,6},{9,8},{10,9},{11,10},{12... | collective-permute-start | bytes 589832 | tf_op jit(solution)/shard_map/ppermute | solution.py:321
  68.4 37.0 %all-to-all-start.1 = ((f32[128,4,128]{2,1,0:T(4,128)}), f32[128,4,128]{2,1,0:T(4,128)S(1)}, u32[]{:S(2)}, u32[]{:S(2)}) async-start(f32[128,4,128]{2,1,0:T(4,128)} %broadcast_in_dim.4), calls=%async_computation.1 | async-start | bytes 524288 | tf_op jit(solution)/shard_map/all_to_all | solution.py:332
  75.6 0.7 copy-start.8
  75.6 0.7 copy-start.9
  78.9 8.9 %collective-permute-start.6 = (f32[4,96,128]{2,1,0:T(8,128)}, f32[4,96,128]{2,1,0:T(8,128)S(1)}, u32[]{:S(2)}, u32[]{:S(2)}) collective-permute-start(f32[4,96,128]{2,1,0:T(8,128)} %get-tuple-element.39), channel_id=1, source_target_pairs={{0,8},{8,16},{16,24},{24,32},{32,40},{40,48},{48,56},{56,64},{64,7... | collective-permute-start | bytes 589832 | tf_op jit(solution)/shard_map/ppermute | solution.py:321
  84.9 8.7 %collective-permute-start.7 = (f32[4,96,128]{2,1,0:T(8,128)}, f32[4,96,128]{2,1,0:T(8,128)S(1)}, u32[]{:S(2)}, u32[]{:S(2)}) collective-permute-start(f32[4,96,128]{2,1,0:T(8,128)} %get-tuple-element.40), channel_id=1, source_target_pairs={{8,0},{16,8},{24,16},{32,24},{40,32},{48,40},{56,48},{64,56},{72,6... | collective-permute-start | bytes 589832 | tf_op jit(solution)/shard_map/ppermute | solution.py:321
  87.8 5.8 %copy-start.17 = (f32[4,96,128]{2,1,0:T(8,128)}, f32[4,96,128]{2,1,0:T(8,128)S(1)}, u32[]{:S(2)}) copy-start(f32[4,96,128]{2,1,0:T(8,128)S(1)} %collective-permute-done.6.north) | copy-start | bytes 589828
  93.6 0.7 copy-start.18
  101.9 5.1 %collective-permute-start.8 = (f32[4,96,128]{2,1,0:T(8,128)}, f32[4,96,128]{2,1,0:T(8,128)S(1)}, u32[]{:S(2)}, u32[]{:S(2)}) collective-permute-start(f32[4,96,128]{2,1,0:T(8,128)} %get-tuple-element.43), channel_id=1, source_target_pairs={{0,1},{1,2},{2,3},{3,4},{4,5},{5,6},{6,7},{8,9},{9,10},{10,11},{11... | collective-permute-start | bytes 589832 | tf_op jit(solution)/shard_map/ppermute | solution.py:321
  104.1 7.4 %collective-permute-start.9 = (f32[4,96,128]{2,1,0:T(8,128)}, f32[4,96,128]{2,1,0:T(8,128)S(1)}, u32[]{:S(2)}, u32[]{:S(2)}) collective-permute-start(f32[4,96,128]{2,1,0:T(8,128)} %get-tuple-element.44), channel_id=1, source_target_pairs={{1,0},{2,1},{3,2},{4,3},{5,4},{6,5},{7,6},{9,8},{10,9},{11,10},{12... | collective-permute-start | bytes 589832 | tf_op jit(solution)/shard_map/ppermute | solution.py:321
  105.4 9.4 %copy-start = (f32[128,4,128]{2,1,0:T(4,128)}, f32[128,4,128]{2,1,0:T(4,128)S(1)}, u32[]{:S(2)}) copy-start(f32[128,4,128]{2,1,0:T(4,128)S(1)} %all-to-all-done.1) | copy-start | bytes 786436
  105.4 23.7 %collective-permute-start.13 = (f32[4,128,128]{2,1,0:T(8,128)S(1)}, f32[4,128,128]{2,1,0:T(8,128)S(1)}, u32[]{:S(2)}, u32[]{:S(2)}) collective-permute-start(f32[4,128,128]{2,1,0:T(8,128)S(1)} %bitcast.29), channel_id=1, source_target_pairs={{0,8},{8,0},{1,9},{9,1},{2,10},{10,2},{3,11},{11,3},{4,12},{12,4},... | collective-permute-start | bytes 786440 | tf_op jit(solution)/shard_map/ppermute | solution.py:325
  107.0 4.5 %copy-start.10 = (f32[4,96,128]{2,1,0:T(8,128)}, f32[4,96,128]{2,1,0:T(8,128)S(1)}, u32[]{:S(2)}) copy-start(f32[4,96,128]{2,1,0:T(8,128)S(1)} %collective-permute-done.8.west) | copy-start | bytes 589828
  111.5 0.7 copy-start.12
  114.8 8.6 %collective-permute-start.10 = (f32[4,96,128]{2,1,0:T(8,128)}, f32[4,96,128]{2,1,0:T(8,128)S(1)}, u32[]{:S(2)}, u32[]{:S(2)}) collective-permute-start(f32[4,96,128]{2,1,0:T(8,128)} %get-tuple-element.46), channel_id=1, source_target_pairs={{0,8},{8,16},{16,24},{24,32},{32,40},{40,48},{48,56},{56,64},{64,7... | collective-permute-start | bytes 589832 | tf_op jit(solution)/shard_map/ppermute | solution.py:321
  120.4 8.7 %collective-permute-start.11 = (f32[4,96,128]{2,1,0:T(8,128)}, f32[4,96,128]{2,1,0:T(8,128)S(1)}, u32[]{:S(2)}, u32[]{:S(2)}) collective-permute-start(f32[4,96,128]{2,1,0:T(8,128)} %get-tuple-element.47), channel_id=1, source_target_pairs={{8,0},{16,8},{24,16},{32,24},{40,32},{48,40},{56,48},{64,56},{72,6... | collective-permute-start | bytes 589832 | tf_op jit(solution)/shard_map/ppermute | solution.py:321
  123.4 5.8 %copy-start.6 = (f32[4,96,128]{2,1,0:T(8,128)}, f32[4,96,128]{2,1,0:T(8,128)S(1)}, u32[]{:S(2)}) copy-start(f32[4,96,128]{2,1,0:T(8,128)S(1)} %collective-permute-done.10.refs_3_) | copy-start | bytes 589828
  129.1 0.7 copy-start.7
  129.2 0.8 copy-start.2
  138.4 1.8 collective-permute-start.18
  171.5 7.1 %copy-start.24 = (f32[4,96,128]{2,1,0:T(8,128)S(1)}, f32[4,96,128]{2,1,0:T(8,128)}, u32[]{:S(2)}) copy-start(f32[4,96,128]{2,1,0:T(8,128)} %get-tuple-element.54) | copy-start | bytes 589828
  171.6 9.6 %copy-start.23 = (f32[4,96,128]{2,1,0:T(8,128)S(1)}, f32[4,96,128]{2,1,0:T(8,128)}, u32[]{:S(2)}) copy-start(f32[4,96,128]{2,1,0:T(8,128)} %get-tuple-element.55) | copy-start | bytes 589828
  171.6 19.0 %all-to-all-start.3 = ((f32[128,4,128]{2,1,0:T(4,128)}), f32[128,4,128]{2,1,0:T(4,128)S(1)}, u32[]{:S(2)}, u32[]{:S(2)}) async-start(f32[128,4,128]{2,1,0:T(4,128)} %broadcast_in_dim.5), calls=%async_computation.3 | async-start | bytes 524288 | tf_op jit(solution)/shard_map/all_to_all | solution.py:332
  178.6 15.4 %collective-permute-start.14 = (f32[4,96,128]{2,1,0:T(8,128)S(1)}, f32[4,96,128]{2,1,0:T(8,128)S(1)}, u32[]{:S(2)}, u32[]{:S(2)}) collective-permute-start(f32[4,96,128]{2,1,0:T(8,128)S(1)} %copy-done.24), channel_id=1, source_target_pairs={{0,1},{1,2},{2,3},{3,4},{4,5},{5,6},{6,7},{8,9},{9,10},{10,11},{11... | collective-permute-start | bytes 589832 | tf_op jit(solution)/shard_map/ppermute | solution.py:321
  181.1 12.9 %collective-permute-start.15 = (f32[4,96,128]{2,1,0:T(8,128)S(1)}, f32[4,96,128]{2,1,0:T(8,128)S(1)}, u32[]{:S(2)}, u32[]{:S(2)}) collective-permute-start(f32[4,96,128]{2,1,0:T(8,128)S(1)} %copy-done.23), channel_id=1, source_target_pairs={{1,0},{2,1},{3,2},{4,3},{5,4},{6,5},{7,6},{9,8},{10,9},{11,10},{12... | collective-permute-start | bytes 589832 | tf_op jit(solution)/shard_map/ppermute | solution.py:321
  190.6 6.8 %copy-start.1 = (f32[128,4,128]{2,1,0:T(4,128)}, f32[128,4,128]{2,1,0:T(4,128)S(1)}, u32[]{:S(2)}) copy-start(f32[128,4,128]{2,1,0:T(4,128)S(1)} %all-to-all-done.3) | copy-start | bytes 786436
  190.6 23.1 %collective-permute-start.19 = (f32[4,128,128]{2,1,0:T(8,128)S(1)}, f32[4,128,128]{2,1,0:T(8,128)S(1)}, u32[]{:S(2)}, u32[]{:S(2)}) collective-permute-start(f32[4,128,128]{2,1,0:T(8,128)S(1)} %bitcast.32), channel_id=1, source_target_pairs={{0,8},{8,0},{1,9},{9,1},{2,10},{10,2},{3,11},{11,3},{4,12},{12,4},... | collective-permute-start | bytes 786440 | tf_op jit(solution)/shard_map/ppermute | solution.py:325
  194.1 0.7 copy-start.11
  194.1 0.7 copy-start.13
  197.4 7.3 %collective-permute-start.16 = (f32[4,96,128]{2,1,0:T(8,128)}, f32[4,96,128]{2,1,0:T(8,128)S(1)}, u32[]{:S(2)}, u32[]{:S(2)}) collective-permute-start(f32[4,96,128]{2,1,0:T(8,128)} %get-tuple-element.57), channel_id=1, source_target_pairs={{0,8},{8,16},{16,24},{24,32},{32,40},{40,48},{48,56},{56,64},{64,7... | collective-permute-start | bytes 589832 | tf_op jit(solution)/shard_map/ppermute | solution.py:321
  201.8 8.7 %collective-permute-start.17 = (f32[4,96,128]{2,1,0:T(8,128)}, f32[4,96,128]{2,1,0:T(8,128)S(1)}, u32[]{:S(2)}, u32[]{:S(2)}) collective-permute-start(f32[4,96,128]{2,1,0:T(8,128)} %get-tuple-element.58), channel_id=1, source_target_pairs={{8,0},{16,8},{24,16},{32,24},{40,32},{48,40},{56,48},{64,56},{72,6... | collective-permute-start | bytes 589832 | tf_op jit(solution)/shard_map/ppermute | solution.py:321
  204.7 5.8 %copy-start.14 = (f32[4,96,128]{2,1,0:T(8,128)}, f32[4,96,128]{2,1,0:T(8,128)S(1)}, u32[]{:S(2)}) copy-start(f32[4,96,128]{2,1,0:T(8,128)S(1)} %collective-permute-done.16.north) | copy-start | bytes 589828
  210.5 0.7 copy-start.15
  213.6 0.7 copy-start.5

commit v2 on v1

--- a/solution.py
+++ b/solution.py
@@ -7,6 +7,7 @@
 from jax.experimental import pallas as pl
 from jax.experimental.pallas import tpu as pltpu
 from jax.sharding import Mesh, PartitionSpec as P
+
 
 WIN = 128
 OVL = 32
@@ -25,6 +26,7 @@
 N_ROW = 32
 N_COL = 8
 N_CHIPS = 128
+CORE = 10
 
 F32 = jnp.float32
 BF16 = jnp.bfloat16
@@ -172,8 +174,8 @@
 def update_extended(e_ref, info, old, grad, north, south):
     row = lax.broadcasted_iota(jnp.int32, (EXT, WIN), 0)
     lane = lanes((EXT, WIN))
-    in_rows = (row >= info[2]) & (row < info[3])
-    keep = (in_rows & (lane >= info[4]), in_rows & (lane + WIN < info[5]))
+    in_rows = (row >= info[6]) & (row < info[7])
+    keep = (in_rows & (lane >= info[8]), in_rows & (lane + WIN < info[9]))
     gap = jnp.zeros((64, WIN), F32)
     for a in range(4):
         n_parts = unpack_rows(north[a])
@@ -185,12 +187,12 @@
             e_ref[a, :EXT, cols] = jnp.where(keep[t], value, 0.0)
 
 
-def step_core(info, e_ref, probe, kernel, measured, tables, g_ref, left, right):
-    oy, ox = info[0], info[1]
+def step_core(info, b, e_ref, probe, kernel, measured, tables, g_ref, left, right):
+    oy, ox = info[2 * b], info[2 * b + 1]
     a_high, a_low, b_high, b_low = (tables[i] for i in range(4))
     o1 = [place_window(e_ref, oy, ox, 0), place_window(e_ref, oy, ox, 1)]
     o2 = [place_window(e_ref, oy, ox, 2), place_window(e_ref, oy, ox, 3)]
-    phase = [kernel[0], kernel[1]]
+    phase = [kernel[0][...], kernel[1][...]]
     x = per_mode(probe, lambda p, m: product(p, o1))
     x = apply_left(apply_right(x, a_high, a_low), b_high, b_low)
     x = per_mode(x, lambda v, m: product(phase, v))
@@ -198,7 +200,7 @@
     x = per_mode(phi, lambda v, m: product(v, o2))
     x = apply_left(apply_right(x, a_high, a_low), b_high, b_low)
     intensity = sum(x[m // 2][m % 2][c] * x[m // 2][m % 2][c] for m in range(MODES) for c in range(2))
-    factor = 1.0 - measured / jnp.sqrt(intensity + FLOOR)
+    factor = 1.0 - measured[b] / jnp.sqrt(intensity + FLOOR)
     x = per_mode(x, lambda v, m: [v[0] * factor, v[1] * factor])
     chi2 = apply_right(apply_left(x, a_high, a_low), b_high, b_low)
     terms2 = [conj_product(phi[m // 2][m % 2], chi2[m // 2][m % 2]) for m in range(MODES)]
@@ -228,7 +230,7 @@
 
 
 def write_halves(info, grads, keep, send, add=None):
-    first = info[6] == 0
+    first = info[CORE] == 0
     for i in range(4):
         low = grads[0][i // 2][i % 2]
         high = grads[1][i // 2][i % 2]
@@ -241,30 +243,34 @@
         send[i] = sent
 
 
-def first_kernel(info, obj, north, south, west, east, probe, kernel, measured, tables,
+def first_kernel(info, obj, north, south, west, east, probe, kcos, ksin, measured, tables,
                  e_ref, g_ref, left, right, keep, send):
     build_extended(e_ref, obj, north, south, west, east)
-    grads = step_core(info, e_ref, probe_blocks(probe), kernel, measured[...], tables, g_ref, left, right)
+    grads = step_core(info, 0, e_ref, probe_blocks(probe), (kcos, ksin), measured, tables, g_ref, left, right)
     write_halves(info, grads, keep, send)
 
 
-def second_kernel(info, old, grad, north, south, probe, kernel, measured, tables,
+def second_kernel(info, old, grad, north, south, probe, kcos, ksin, measured, tables,
                   e_ref, g_ref, left, right, keep, send):
     update_extended(e_ref, info, old, grad, north, south)
-    grads = step_core(info, e_ref, probe_blocks(probe), kernel, measured[...], tables, g_ref, left, right)
+    grads = step_core(info, 1, e_ref, probe_blocks(probe), (kcos, ksin), measured, tables, g_ref, left, right)
     write_halves(info, grads, keep, send)
 
 
 def third_kernel(rate, info, old, grad, north, south, probe, mine, other, keep_add, send_add,
-                 kernel, measured, tables,
+                 kcos, ksin, measured, tables,
                  e_ref, g_ref, left, right, keep, send, p_ref):
     update_extended(e_ref, info, old, grad, north, south)
-    first = info[6] == 0
+    update_probe(rate, info, probe, mine, other, p_ref)
+    grads = step_core(info, 2, e_ref, probe_blocks(p_ref), (kcos, ksin), measured, tables, g_ref, left, right)
+    write_halves(info, grads, keep, send, (keep_add, send_add))
+
+
+def update_probe(rate, info, probe, mine, other, out):
+    first = info[CORE] == 0
     for i in range(4):
-        p_ref[i] = probe[i] - rate * jnp.where(first, mine[i], other[i])
-        p_ref[4 + i] = probe[4 + i] - rate * jnp.where(first, other[i], mine[i])
-    grads = step_core(info, e_ref, probe_blocks(p_ref), kernel, measured[...], tables, g_ref, left, right)
-    write_halves(info, grads, keep, send, (keep_add, send_add))
+        out[i] = probe[i] - rate * jnp.where(first, mine[i], other[i])
+        out[4 + i] = probe[4 + i] - rate * jnp.where(first, other[i], mine[i])
 
 
 def middle_kernel(g_in, west, east, g_ref, up, down):
@@ -290,24 +296,20 @@
         out[a] = jnp.where(lane < WIN - OVL, parts[0], parts[1])
 
 
-def probe_kernel(rate, info, probe, mine, other, out):
-    first = info[6] == 0
-    for i in range(4):
-        out[i] = probe[i] - rate * jnp.where(first, mine[i], other[i])
-        out[4 + i] = probe[4 + i] - rate * jnp.where(first, other[i], mine[i])
-
-
 SMEM = pl.BlockSpec(memory_space=pltpu.SMEM)
 VMEM = pl.BlockSpec(memory_space=pltpu.VMEM)
 
 
-def call(kernel, outs, *args, scalars=0, name=None):
+def call(kernel, outs, *args, scalars=0, on_chip=True):
+    args = list(args[:scalars]) + [
+        pltpu.with_memory_space_constraint(x, pltpu.VMEM) for x in args[scalars:]
+    ]
     return pl.pallas_call(
         kernel,
-        out_shape=[jax.ShapeDtypeStruct(s, F32) for s in outs],
+        out_shape=[pltpu.VMEM(s, F32) if on_chip else jax.ShapeDtypeStruct(s, F32) for s in outs],
         in_specs=[SMEM] * scalars + [VMEM] * (len(args) - scalars),
         out_specs=[VMEM] * len(outs),
-        name=name,
+        compiler_params=pltpu.CompilerParams(vmem_limit_bytes=32 << 20),
     )(*args)
 
 
@@ -325,29 +327,31 @@
     return lax.ppermute(x, "core", [(0, 1), (1, 0)])
 
 
+def chip_exchange(x):
+    return lax.all_to_all(x, CHIPS, 0, 0, tiled=True)
+
+
 def summed_half(keep, send):
     total = keep + swap_cores(send)
-    parts = lax.all_to_all(total.reshape(N_CHIPS, -1, WIN), CHIPS, 0, 0, tiled=True)
+    parts = chip_exchange(total.reshape(N_CHIPS, -1, WIN))
     own = jnp.sum(parts, axis=0)
-    whole = lax.all_to_all(
-        jnp.broadcast_to(own[None], (N_CHIPS, *own.shape)), CHIPS, 0, 0, tiled=True
-    )
-    return whole.reshape(HALF)
+    spread = jnp.broadcast_to(own[None], (N_CHIPS, *own.shape))
+    return chip_exchange(spread).reshape(HALF)
 
 
 def exchanged(grad, left, right):
     west = moved(right, COL, N_COL, 1)
     east = moved(left, COL, N_COL, -1)
-    grad, up, down = call(middle_kernel, [EXT_SHAPE, BAND, BAND], grad, west, east, name="middle")
+    grad, up, down = call(middle_kernel, [EXT_SHAPE, BAND, BAND], grad, west, east)
     north = moved(down, ROW, N_ROW, 1)
     south = moved(up, ROW, N_ROW, -1)
     return grad, north, south
 
 
-def per_device(object_field, probe, kernel_phase, amplitudes, offsets):
+def steps(object_field, probe, kernel_phase, amplitudes, offsets):
     rate = PROBE_RATE / math.sqrt(N_ROW * N_COL)
     tables = jnp.asarray(dft_tables())
-    kernel = jnp.stack([jnp.cos(kernel_phase), jnp.sin(kernel_phase)])
+    kcos, ksin = jnp.cos(kernel_phase), jnp.sin(kernel_phase)
     row = lax.axis_index(ROW)
     col = lax.axis_index(COL)
     core = lax.axis_index("core")
@@ -358,42 +362,42 @@
         jnp.where(col == N_COL - 1, EXT - OVL, EXT),
         core,
     ]).astype(jnp.int32)
-    infos = [jnp.concatenate([offsets[b, 0, 0], edges]) for b in range(3)]
+    info = jnp.concatenate([offsets.reshape(-1), edges])
     measured = amplitudes[:, 0, 0]
     obj = object_field.reshape(4, WIN, WIN)
     probe = probe.reshape(2 * MODES, WIN, WIN)
 
     north = moved(obj[:, WIN - OVL :], ROW, N_ROW, 1)
     south = moved(obj[:, :OVL], ROW, N_ROW, -1)
-    left, right = call(halo_kernel, [(4, 48, WIN)] * 2, obj, north, south, name="halo")
+    left, right = call(halo_kernel, [(4, 48, WIN)] * 2, obj, north, south)
     west = moved(right, COL, N_COL, 1)
     east = moved(left, COL, N_COL, -1)
 
     step_outs = [EXT_SHAPE, EXT_SHAPE, BAND, BAND, HALF, HALF]
     extended, grad, left, right, keep0, send0 = call(
-        first_kernel, step_outs, infos[0], obj, north, south, west, east, probe, kernel,
-        measured[0], tables, scalars=1, name="step0",
+        first_kernel, step_outs, info, obj, north, south, west, east, probe, kcos, ksin,
+        measured, tables, scalars=1,
     )
     grad, north, south = exchanged(grad, left, right)
     mine0 = summed_half(keep0, send0)
     other0 = swap_cores(mine0)
     extended, grad, left, right, keep1, send1 = call(
-        second_kernel, step_outs, infos[1], extended, grad, north, south, probe, kernel,
-        measured[1], tables, scalars=1, name="step1",
+        second_kernel, step_outs, info, extended, grad, north, south, probe, kcos, ksin,
+        measured, tables, scalars=1,
     )
     grad, north, south = exchanged(grad, left, right)
     extended, grad, left, right, keep2, send2, probe = call(
         lambda *refs: third_kernel(rate, *refs), step_outs + [(2 * MODES, WIN, WIN)],
-        infos[2], extended, grad, north, south, probe, mine0, other0, keep1, send1, kernel,
-        measured[2], tables, scalars=1, name="step2",
+        info, extended, grad, north, south, probe, mine0, other0, keep1, send1, kcos, ksin,
+        measured, tables, scalars=1,
     )
     grad, north, south = exchanged(grad, left, right)
     mine = summed_half(keep2, send2)
     other = swap_cores(mine)
-    (obj,) = call(object_kernel, [HALF], extended, grad, north, south, name="object")
+    (obj,) = call(object_kernel, [HALF], extended, grad, north, south, on_chip=False)
     (probe,) = call(
-        lambda *refs: probe_kernel(rate, *refs), [(2 * MODES, WIN, WIN)],
-        infos[2], probe, mine, other, scalars=1, name="probe",
+        lambda *refs: update_probe(rate, *refs), [(2 * MODES, WIN, WIN)],
+        info, probe, mine, other, scalars=1, on_chip=False,
     )
     return obj.reshape(2, 2, WIN, WIN), probe.reshape(MODES, 2, WIN, WIN)
 
@@ -408,6 +412,4 @@
         P(None, ROW, COL, None),
     )
     out_specs = (P(None, None, ROW, COL), P())
-    return jax.shard_map(
-        per_device, mesh=fine, in_specs=in_specs, out_specs=out_specs, check_vma=False
-    )
+    return jax.shard_map(steps, mesh=fine, in_specs=in_specs, out_specs=out_specs, check_vma=False)

time: 217 us -> 201 us (0.926)
  Pallas kernels: 37.7 us -> 21.3 us
  other arithmetic: 3.64 us -> 1.06 us
    pallas_call x9, Pallas kernels: 37.7 us -> 21.3 us  [call(): pl.pallas_call(kernel, out_shape=[pltpu.VMEM(s, F32) if on_chip else jax....]
    unnamed x54 -> x45, local copies, waits for them, and re-layouts: 6.89 us -> 9.81 us
  transfers between devices with their start and end apart: 23 -> 23, of which waited for: 13 -> 14; matrix products, arithmetic and copies ran while one was open for 2% -> 1% of each run, Pallas kernels for 8% -> 4%
where the time goes in v2:
time: 201 us; the launch traced here: 200 us
  starting transfers between devices  84.1 us (42%)
  waiting for transfers between devices  49.8 us (25%)
  blocking collectives  29.8 us (15%)
  Pallas kernels  21.3 us (11%)
  local copies, waits for them, and re-layouts  12.6 us (6%)
    ppermute x16, starting transfers between devices, moved(): return lax.ppermute(x, axis, route)  45.3 us
    all_to_all x3, starting transfers between devices, chip_exchange(): return lax.all_to_all(x, CHIPS, 0, 0, tiled=True)  35.2 us
    all_to_all x1, blocking collectives, chip_exchange(): return lax.all_to_all(x, CHIPS, 0, 0, tiled=True)  29.8 us
    ppermute x16, waiting for transfers between devices, moved(): return lax.ppermute(x, axis, route)  29.7 us
    pallas_call x9, Pallas kernels, call(): pl.pallas_call(kernel, out_shape=[pltpu.VMEM(s, F32) if on_chip else jax....  21.3 us
    all_to_all x3, waiting for transfers between devices, chip_exchange(): return lax.all_to_all(x, CHIPS, 0, 0, tiled=True)  17 us
    unnamed x45, local copies, waits for them, and re-layouts  9.81 us
  transfers between devices with their start and end apart: 23, of which 14 were waited for; matrix products, arithmetic and copies ran while one was open for 1% of the time, Pallas kernels for 4%

profile of v2, /device:TPU:1, one launch (start us, length us, event | category | flops | bytes accessed | tf_op | source)
XLA Modules:
  0.0 199.7 jit_solution(2178743930278055286)
XLA Ops:
  0.6 0.9 fusion
  1.6 5.1 %collective-permute-start.1 = (f32[4,32,128]{2,1,0:T(8,128)S(1)}, f32[4,32,128]{2,1,0:T(8,128)S(1)}, u32[]{:S(2)}, u32[]{:S(2)}) collective-permute-start(f32[4,32,128]{2,1,0:T(8,128)S(1)} %get-tuple-element.62), channel_id=1, source_target_pairs={{8,0},{16,8},{24,16},{32,24},{40,32},{48,40},{56,48},{64,56},{72,6... | collective-permute-start | bytes 196616 | tf_op jit(solution)/shard_map/ppermute | solution.py:323
  6.7 2.8 %collective-permute-start = (f32[4,32,128]{2,1,0:T(8,128)S(1)}, f32[4,32,128]{2,1,0:T(8,128)S(1)}, u32[]{:S(2)}, u32[]{:S(2)}) collective-permute-start(f32[4,32,128]{2,1,0:T(8,128)S(1)} %get-tuple-element.63), channel_id=1, source_target_pairs={{0,8},{8,16},{16,24},{24,32},{32,40},{40,48},{48,56},{56,64},{64,7... | collective-permute-start | bytes 196616 | tf_op jit(solution)/shard_map/ppermute | solution.py:323
  9.6 1.3 collective-permute-done.north
  10.9 0.9 copy-done.4
  11.8 0.2 shard_map.77
  12.0 3.2 %collective-permute-start.2 = (f32[4,48,128]{2,1,0:T(8,128)S(1)}, f32[4,48,128]{2,1,0:T(8,128)S(1)}, u32[]{:S(2)}, u32[]{:S(2)}) collective-permute-start(f32[4,48,128]{2,1,0:T(8,128)S(1)} %get-tuple-element.32), channel_id=1, source_target_pairs={{0,1},{1,2},{2,3},{3,4},{4,5},{5,6},{6,7},{8,9},{9,10},{10,11},{11... | collective-permute-start | bytes 294920 | tf_op jit(solution)/shard_map/ppermute | solution.py:323
  15.2 1.3 collective-permute-start.3
  16.6 0.2 fusion.1
  16.8 0.7 copy-done.21
  17.5 0.1 copy.9
  17.8 2.9 %collective-permute-done.3.east = f32[4,48,128]{2,1,0:T(8,128)S(1)} collective-permute-done((f32[4,48,128]{2,1,0:T(8,128)S(1)}, f32[4,48,128]{2,1,0:T(8,128)S(1)}, u32[]{:S(2)}, u32[]{:S(2)}) %collective-permute-start.3) | collective-permute-done | bytes 98336 | tf_op jit(solution)/shard_map/ppermute | solution.py:323
  20.7 1.0 copy-done.1
  21.7 0.9 copy-done.5
  22.7 6.3 %shard_map.78 = (f32[4,200,256]{2,1,0:T(8,128)S(1)}, f32[4,200,256]{2,1,0:T(8,128)S(1)}, f32[4,96,128]{2,1,0:T(8,128)S(1)}, f32[4,96,128]{2,1,0:T(8,128)}, f32[4...) custom-call(s32[11]{0:T(128)S(1)} %concatenate.3.info.refs_0_, f32[4,128,128]{2,1,0:T(8,128)S(1)} %bitcast.24, ...), custom_call_target="tpu_custom_call" | custom-call | tf_op jit(solution)/shard_map/pallas_call | solution.py:307
  29.0 1.5 collective-permute-done.12
  30.5 0.7 add.18
  31.2 21.0 %all-to-all-start = ((f32[128,4,128]{2,1,0:T(4,128)}), f32[128,4,128]{2,1,0:T(4,128)S(1)}, u32[]{:S(2)}, u32[]{:S(2)}) async-start(f32[128,4,128]{2,1,0:T(4,128)} %bitcast.8), calls=%async_computation | async-start | bytes 524288 | tf_op jit(solution)/shard_map/all_to_all | solution.py:331
  52.3 2.5 %collective-permute-start.4 = (f32[4,96,128]{2,1,0:T(8,128)}, f32[4,96,128]{2,1,0:T(8,128)S(1)}, u32[]{:S(2)}, u32[]{:S(2)}) collective-permute-start(f32[4,96,128]{2,1,0:T(8,128)} %get-tuple-element.36), channel_id=1, source_target_pairs={{0,1},{1,2},{2,3},{3,4},{4,5},{5,6},{6,7},{8,9},{9,10},{10,11},{11... | collective-permute-start | bytes 589832 | tf_op jit(solution)/shard_map/ppermute | solution.py:323
  54.8 1.3 collective-permute-start.5
  56.1 8.9 %all-to-all-done = f32[128,4,128]{2,1,0:T(4,128)S(1)} async-done(((f32[128,4,128]{2,1,0:T(4,128)}), f32[128,4,128]{2,1,0:T(4,128)S(1)}, u32[]{:S(2)}, u32[]{:S(2)}) %all-to-all-start) | async-done | bytes 262176 | tf_op jit(solution)/shard_map/all_to_all | solution.py:331
  65.0 0.1 reduce_sum.18
  65.1 0.7 broadcast_in_dim.4
  65.8 7.1 %all-to-all-start.1 = ((f32[128,4,128]{2,1,0:T(4,128)}), f32[128,4,128]{2,1,0:T(4,128)S(1)}, u32[]{:S(2)}, u32[]{:S(2)}) async-start(f32[128,4,128]{2,1,0:T(4,128)} %broadcast_in_dim.4), calls=%async_computation.1 | async-start | bytes 524288 | tf_op jit(solution)/shard_map/all_to_all | solution.py:331
  73.0 0.7 copy-done.14
  73.7 0.9 copy-done.15
  74.6 0.2 shard_map.79
  74.9 6.0 %collective-permute-start.6 = (f32[4,96,128]{2,1,0:T(8,128)S(1)}, f32[4,96,128]{2,1,0:T(8,128)S(1)}, u32[]{:S(2)}, u32[]{:S(2)}) collective-permute-start(f32[4,96,128]{2,1,0:T(8,128)S(1)} %get-tuple-element.39), channel_id=1, source_target_pairs={{0,8},{8,16},{16,24},{24,32},{32,40},{40,48},{48,56},{56,64},{64,7... | collective-permute-start | bytes 589832 | tf_op jit(solution)/shard_map/ppermute | solution.py:323
  80.9 2.1 %collective-permute-start.7 = (f32[4,96,128]{2,1,0:T(8,128)S(1)}, f32[4,96,128]{2,1,0:T(8,128)S(1)}, u32[]{:S(2)}, u32[]{:S(2)}) collective-permute-start(f32[4,96,128]{2,1,0:T(8,128)S(1)} %get-tuple-element.40), channel_id=1, source_target_pairs={{8,0},{16,8},{24,16},{32,24},{40,32},{48,40},{56,48},{64,56},{72,6... | collective-permute-start | bytes 589832 | tf_op jit(solution)/shard_map/ppermute | solution.py:323
  83.0 0.6 collective-permute-done.6.north
  83.6 5.8 %collective-permute-done.7.south = f32[4,96,128]{2,1,0:T(8,128)S(1)} collective-permute-done((f32[4,96,128]{2,1,0:T(8,128)S(1)}, f32[4,96,128]{2,1,0:T(8,128)S(1)}, u32[]{:S(2)}, u32[]{:S(2)}) %collective-permute-start.7) | collective-permute-done | bytes 196640 | tf_op jit(solution)/shard_map/ppermute | solution.py:323
  89.4 6.1 %shard_map.80 = (f32[4,200,256]{2,1,0:T(8,128)S(1)}, f32[4,200,256]{2,1,0:T(8,128)S(1)}, f32[4,96,128]{2,1,0:T(8,128)}, f32[4,96,128]{2,1,0:T(8,128)}, f32[4,128...) custom-call(s32[11]{0:T(128)S(1)} %concatenate.3.info.refs_0_, f32[4,200,256]{2,1,0:T(8,128)S(1)} %get-tuple-element.34.old, ...), custom_call_target="tpu_custom_call" | custom-call | tf_op jit(solution)/shard_map/pallas_call | solution.py:307
  95.5 0.9 copy-done.8
  96.4 0.7 copy-done.12
  97.1 2.2 %collective-permute-start.8 = (f32[4,96,128]{2,1,0:T(8,128)}, f32[4,96,128]{2,1,0:T(8,128)S(1)}, u32[]{:S(2)}, u32[]{:S(2)}) collective-permute-start(f32[4,96,128]{2,1,0:T(8,128)} %get-tuple-element.43), channel_id=1, source_target_pairs={{0,1},{1,2},{2,3},{3,4},{4,5},{5,6},{6,7},{8,9},{9,10},{10,11},{11... | collective-permute-start | bytes 589832 | tf_op jit(solution)/shard_map/ppermute | solution.py:323
  99.3 1.3 collective-permute-start.9
  100.6 0.1 collective-permute-start.13
  100.7 1.5 collective-permute-done.8.west
  102.2 4.5 %collective-permute-done.9.east = f32[4,96,128]{2,1,0:T(8,128)S(1)} collective-permute-done((f32[4,96,128]{2,1,0:T(8,128)}, f32[4,96,128]{2,1,0:T(8,128)S(1)}, u32[]{:S(2)}, u32[]{:S(2)}) %collective-permute-start.9) | collective-permute-done | bytes 196640 | tf_op jit(solution)/shard_map/ppermute | solution.py:323
  106.7 1.1 copy-done.9
  107.9 0.2 shard_map.81
  108.1 5.4 %collective-permute-start.10 = (f32[4,96,128]{2,1,0:T(8,128)S(1)}, f32[4,96,128]{2,1,0:T(8,128)S(1)}, u32[]{:S(2)}, u32[]{:S(2)}) collective-permute-start(f32[4,96,128]{2,1,0:T(8,128)S(1)} %get-tuple-element.46), channel_id=1, source_target_pairs={{0,8},{8,16},{16,24},{24,32},{32,40},{40,48},{48,56},{56,64},{64,7... | collective-permute-start | bytes 589832 | tf_op jit(solution)/shard_map/ppermute | solution.py:323
  113.5 1.9 collective-permute-start.11
  115.5 0.7 collective-permute-done.10.refs_3_
  116.1 5.9 %collective-permute-done.11.refs_4_ = f32[4,96,128]{2,1,0:T(8,128)S(1)} collective-permute-done((f32[4,96,128]{2,1,0:T(8,128)S(1)}, f32[4,96,128]{2,1,0:T(8,128)S(1)}, u32[]{:S(2)}, u32[]{:S(2)}) %collective-permute-start.11) | collective-permute-done | bytes 196640 | tf_op jit(solution)/shard_map/ppermute | solution.py:323
  122.0 5.5 %shard_map.82 = (f32[4,200,256]{2,1,0:T(8,128)S(1)}, f32[4,200,256]{2,1,0:T(8,128)S(1)}, f32[4,96,128]{2,1,0:T(8,128)S(1)}, f32[4,96,128]{2,1,0:T(8,128)S(1)}, f...) custom-call(s32[11]{0:T(128)S(1)} %concatenate.3.info.refs_0_, ...), custom_call_target="tpu_custom_call" | custom-call | tf_op jit(solution)/shard_map/pallas_call | solution.py:307
  127.5 0.9 copy-done.6
  128.4 0.8 copy-done.10
  129.2 1.5 collective-permute-done.18
  130.8 29.8 %all_to_all.20 = f32[128,4,128]{2,1,0:T(4,128)S(1)} all-to-all(f32[128,4,128]{2,1,0:T(4,128)S(1)} %bitcast.29), channel_id=1, replica_groups=mesh['z'=8,'xh'=2,'core'=2,'y'=4,'xl'=2] {'z','xh','y','xl'}, dimensions={0} | all-to-all | bytes 524288 | tf_op jit(solution)/shard_map/all_to_all | solution.py:331
  160.6 0.1 reduce_sum.19
  160.8 0.7 broadcast_in_dim.5
  161.5 7.1 %all-to-all-start.3 = ((f32[128,4,128]{2,1,0:T(4,128)}), f32[128,4,128]{2,1,0:T(4,128)S(1)}, u32[]{:S(2)}, u32[]{:S(2)}) async-start(f32[128,4,128]{2,1,0:T(4,128)} %broadcast_in_dim.5), calls=%async_computation.3 | async-start | bytes 524288 | tf_op jit(solution)/shard_map/all_to_all | solution.py:331
  168.6 2.5 %collective-permute-start.14 = (f32[4,96,128]{2,1,0:T(8,128)S(1)}, f32[4,96,128]{2,1,0:T(8,128)S(1)}, u32[]{:S(2)}, u32[]{:S(2)}) collective-permute-start(f32[4,96,128]{2,1,0:T(8,128)S(1)} %copy-done.19), channel_id=1, source_target_pairs={{0,1},{1,2},{2,3},{3,4},{4,5},{5,6},{6,7},{8,9},{9,10},{10,11},{11... | collective-permute-start | bytes 589832 | tf_op jit(solution)/shard_map/ppermute | solution.py:323
  171.1 1.3 collective-permute-start.15
  172.4 8.1 %all-to-all-done.3 = f32[128,4,128]{2,1,0:T(4,128)S(1)} async-done(((f32[128,4,128]{2,1,0:T(4,128)}), f32[128,4,128]{2,1,0:T(4,128)S(1)}, u32[]{:S(2)}, u32[]{:S(2)}) %all-to-all-start.3) | async-done | bytes 262176 | tf_op jit(solution)/shard_map/all_to_all | solution.py:331
  180.6 3.5 %collective-permute-start.19 = (f32[4,128,128]{2,1,0:T(8,128)S(1)}, f32[4,128,128]{2,1,0:T(8,128)S(1)}, u32[]{:S(2)}, u32[]{:S(2)}) collective-permute-start(f32[4,128,128]{2,1,0:T(8,128)S(1)} %bitcast.27), channel_id=1, source_target_pairs={{0,8},{8,0},{1,9},{9,1},{2,10},{10,2},{3,11},{11,3},{4,12},{12,4},... | collective-permute-start | bytes 786440 | tf_op jit(solution)/shard_map/ppermute | solution.py:327
  184.1 0.2 shard_map.83
  184.3 4.5 %collective-permute-start.16 = (f32[4,96,128]{2,1,0:T(8,128)S(1)}, f32[4,96,128]{2,1,0:T(8,128)S(1)}, u32[]{:S(2)}, u32[]{:S(2)}) collective-permute-start(f32[4,96,128]{2,1,0:T(8,128)S(1)} %get-tuple-element.57), channel_id=1, source_target_pairs={{0,8},{8,16},{16,24},{24,32},{32,40},{40,48},{48,56},{56,64},{64,7... | collective-permute-start | bytes 589832 | tf_op jit(solution)/shard_map/ppermute | solution.py:323
  188.8 1.9 collective-permute-start.17
  190.7 0.7 collective-permute-done.16.north
  191.4 5.9 %collective-permute-done.17.south = f32[4,96,128]{2,1,0:T(8,128)S(1)} collective-permute-done((f32[4,96,128]{2,1,0:T(8,128)S(1)}, f32[4,96,128]{2,1,0:T(8,128)S(1)}, u32[]{:S(2)}, u32[]{:S(2)}) %collective-permute-start.17) | collective-permute-done | bytes 196640 | tf_op jit(solution)/shard_map/ppermute | solution.py:323
  197.3 1.0 shard_map.84
  198.3 1.4 shard_map.85
  (47 shorter events, 0.3 us)
Async XLA Ops:
  0.6 20.0 %copy-start = (f32[4,2,128,128]{3,2,1,0:T(8,128)S(1)}, f32[4,2,128,128]{3,2,1,0:T(8,128)}, u32[]{:S(2)}) copy-start(f32[4,2,128,128]{3,2,1,0:T(8,128)} %param.7) | copy-start | bytes 1572868
  1.6 8.0 %collective-permute-start.1 = (f32[4,32,128]{2,1,0:T(8,128)S(1)}, f32[4,32,128]{2,1,0:T(8,128)S(1)}, u32[]{:S(2)}, u32[]{:S(2)}) collective-permute-start(f32[4,32,128]{2,1,0:T(8,128)S(1)} %get-tuple-element.62), channel_id=1, source_target_pairs={{8,0},{16,8},{24,16},{32,24},{40,32},{48,40},{56,48},{64,56},{72,6... | collective-permute-start | bytes 196616 | tf_op jit(solution)/shard_map/ppermute | solution.py:323
  6.7 4.2 %collective-permute-start = (f32[4,32,128]{2,1,0:T(8,128)S(1)}, f32[4,32,128]{2,1,0:T(8,128)S(1)}, u32[]{:S(2)}, u32[]{:S(2)}) collective-permute-start(f32[4,32,128]{2,1,0:T(8,128)S(1)} %get-tuple-element.63), channel_id=1, source_target_pairs={{0,8},{8,16},{16,24},{24,32},{32,40},{40,48},{48,56},{56,64},{64,7... | collective-permute-start | bytes 196616 | tf_op jit(solution)/shard_map/ppermute | solution.py:323
  10.9 0.9 copy-start.4
  11.8 4.7 %copy-start.20 = (f32[128,128]{1,0:T(8,128)S(1)}, f32[128,128]{1,0:T(8,128)}, u32[]{:S(2)}) copy-start(f32[128,128]{1,0:T(8,128)} %param.8) | copy-start | bytes 196612
  12.0 8.6 %copy-start.3 = (f32[3,1,1,128,128]{4,3,2,1,0:T(8,128)S(1)}, f32[3,1,1,128,128]{4,3,2,1,0:T(8,128)}, u32[]{:S(2)}) copy-start(f32[3,1,1,128,128]{4,3,2,1,0:T(8,128)} %param.9) | copy-start | bytes 589828
  12.0 5.7 %collective-permute-start.2 = (f32[4,48,128]{2,1,0:T(8,128)S(1)}, f32[4,48,128]{2,1,0:T(8,128)S(1)}, u32[]{:S(2)}, u32[]{:S(2)}) collective-permute-start(f32[4,48,128]{2,1,0:T(8,128)S(1)} %get-tuple-element.32), channel_id=1, source_target_pairs={{0,1},{1,2},{2,3},{3,4},{4,5},{5,6},{6,7},{8,9},{9,10},{10,11},{11... | collective-permute-start | bytes 294920 | tf_op jit(solution)/shard_map/ppermute | solution.py:323
  15.2 5.4 %collective-permute-start.3 = (f32[4,48,128]{2,1,0:T(8,128)S(1)}, f32[4,48,128]{2,1,0:T(8,128)S(1)}, u32[]{:S(2)}, u32[]{:S(2)}) collective-permute-start(f32[4,48,128]{2,1,0:T(8,128)S(1)} %get-tuple-element.33), channel_id=1, source_target_pairs={{1,0},{2,1},{3,2},{4,3},{5,4},{6,5},{7,6},{9,8},{10,9},{11,10},{12... | collective-permute-start | bytes 294920 | tf_op jit(solution)/shard_map/ppermute | solution.py:323
  16.8 0.7 copy-start.21
  20.7 1.0 copy-start.1
  21.7 0.9 copy-start.5
  29.0 1.5 collective-permute-start.12
  31.2 33.7 %all-to-all-start = ((f32[128,4,128]{2,1,0:T(4,128)}), f32[128,4,128]{2,1,0:T(4,128)S(1)}, u32[]{:S(2)}, u32[]{:S(2)}) async-start(f32[128,4,128]{2,1,0:T(4,128)} %bitcast.8), calls=%async_computation | async-start | bytes 524288 | tf_op jit(solution)/shard_map/all_to_all | solution.py:331
  52.3 20.7 %collective-permute-start.4 = (f32[4,96,128]{2,1,0:T(8,128)}, f32[4,96,128]{2,1,0:T(8,128)S(1)}, u32[]{:S(2)}, u32[]{:S(2)}) collective-permute-start(f32[4,96,128]{2,1,0:T(8,128)} %get-tuple-element.36), channel_id=1, source_target_pairs={{0,1},{1,2},{2,3},{3,4},{4,5},{5,6},{6,7},{8,9},{9,10},{10,11},{11... | collective-permute-start | bytes 589832 | tf_op jit(solution)/shard_map/ppermute | solution.py:323
  54.8 18.2 %collective-permute-start.5 = (f32[4,96,128]{2,1,0:T(8,128)S(1)}, f32[4,96,128]{2,1,0:T(8,128)S(1)}, u32[]{:S(2)}, u32[]{:S(2)}) collective-permute-start(f32[4,96,128]{2,1,0:T(8,128)S(1)} %get-tuple-element.37), channel_id=1, source_target_pairs={{1,0},{2,1},{3,2},{4,3},{5,4},{6,5},{7,6},{9,8},{10,9},{11,10},{12... | collective-permute-start | bytes 589832 | tf_op jit(solution)/shard_map/ppermute | solution.py:323
  65.8 34.7 %all-to-all-start.1 = ((f32[128,4,128]{2,1,0:T(4,128)}), f32[128,4,128]{2,1,0:T(4,128)S(1)}, u32[]{:S(2)}, u32[]{:S(2)}) async-start(f32[128,4,128]{2,1,0:T(4,128)} %broadcast_in_dim.4), calls=%async_computation.1 | async-start | bytes 524288 | tf_op jit(solution)/shard_map/all_to_all | solution.py:331
  73.0 0.7 copy-start.14
  73.7 0.9 copy-start.15
  74.6 14.7 %copy-start.2 = (bf16[4,256,256]{2,1,0:T(8,128)(2,1)S(1)}, bf16[4,256,256]{2,1,0:T(8,128)(2,1)}, u32[]{:S(2)}) copy-start(bf16[4,256,256]{2,1,0:T(8,128)(2,1)} %constant.40.clone.tables.refs_13_) | copy-start | bytes 1572868
  74.9 8.7 %collective-permute-start.6 = (f32[4,96,128]{2,1,0:T(8,128)S(1)}, f32[4,96,128]{2,1,0:T(8,128)S(1)}, u32[]{:S(2)}, u32[]{:S(2)}) collective-permute-start(f32[4,96,128]{2,1,0:T(8,128)S(1)} %get-tuple-element.39), channel_id=1, source_target_pairs={{0,8},{8,16},{16,24},{24,32},{32,40},{40,48},{48,56},{56,64},{64,7... | collective-permute-start | bytes 589832 | tf_op jit(solution)/shard_map/ppermute | solution.py:323
  80.9 8.5 %collective-permute-start.7 = (f32[4,96,128]{2,1,0:T(8,128)S(1)}, f32[4,96,128]{2,1,0:T(8,128)S(1)}, u32[]{:S(2)}, u32[]{:S(2)}) collective-permute-start(f32[4,96,128]{2,1,0:T(8,128)S(1)} %get-tuple-element.40), channel_id=1, source_target_pairs={{8,0},{16,8},{24,16},{32,24},{40,32},{48,40},{56,48},{64,56},{72,6... | collective-permute-start | bytes 589832 | tf_op jit(solution)/shard_map/ppermute | solution.py:323
  95.5 0.9 copy-start.8
  96.4 0.7 copy-start.12
  97.1 5.1 %collective-permute-start.8 = (f32[4,96,128]{2,1,0:T(8,128)}, f32[4,96,128]{2,1,0:T(8,128)S(1)}, u32[]{:S(2)}, u32[]{:S(2)}) collective-permute-start(f32[4,96,128]{2,1,0:T(8,128)} %get-tuple-element.43), channel_id=1, source_target_pairs={{0,1},{1,2},{2,3},{3,4},{4,5},{5,6},{6,7},{8,9},{9,10},{10,11},{11... | collective-permute-start | bytes 589832 | tf_op jit(solution)/shard_map/ppermute | solution.py:323
  99.3 7.4 %collective-permute-start.9 = (f32[4,96,128]{2,1,0:T(8,128)}, f32[4,96,128]{2,1,0:T(8,128)S(1)}, u32[]{:S(2)}, u32[]{:S(2)}) collective-permute-start(f32[4,96,128]{2,1,0:T(8,128)} %get-tuple-element.44), channel_id=1, source_target_pairs={{1,0},{2,1},{3,2},{4,3},{5,4},{6,5},{7,6},{9,8},{10,9},{11,10},{12... | collective-permute-start | bytes 589832 | tf_op jit(solution)/shard_map/ppermute | solution.py:323
  100.6 21.4 %collective-permute-start.13 = (f32[4,128,128]{2,1,0:T(8,128)S(1)}, f32[4,128,128]{2,1,0:T(8,128)S(1)}, u32[]{:S(2)}, u32[]{:S(2)}) collective-permute-start(f32[4,128,128]{2,1,0:T(8,128)S(1)} %bitcast.25), channel_id=1, source_target_pairs={{0,8},{8,0},{1,9},{9,1},{2,10},{10,2},{3,11},{11,3},{4,12},{12,4},... | collective-permute-start | bytes 786440 | tf_op jit(solution)/shard_map/ppermute | solution.py:327
  106.7 1.1 copy-start.9
  107.9 14.2 %copy-start.13 = (f32[4,128,128]{2,1,0:T(8,128)S(1)}, f32[4,128,128]{2,1,0:T(8,128)}, u32[]{:S(2)}) copy-start(f32[4,128,128]{2,1,0:T(8,128)} %copy-done.12) | copy-start | bytes 786436
  108.1 8.0 %collective-permute-start.10 = (f32[4,96,128]{2,1,0:T(8,128)S(1)}, f32[4,96,128]{2,1,0:T(8,128)S(1)}, u32[]{:S(2)}, u32[]{:S(2)}) collective-permute-start(f32[4,96,128]{2,1,0:T(8,128)S(1)} %get-tuple-element.46), channel_id=1, source_target_pairs={{0,8},{8,16},{16,24},{24,32},{32,40},{40,48},{48,56},{56,64},{64,7... | collective-permute-start | bytes 589832 | tf_op jit(solution)/shard_map/ppermute | solution.py:323
  113.5 8.5 %collective-permute-start.11 = (f32[4,96,128]{2,1,0:T(8,128)S(1)}, f32[4,96,128]{2,1,0:T(8,128)S(1)}, u32[]{:S(2)}, u32[]{:S(2)}) collective-permute-start(f32[4,96,128]{2,1,0:T(8,128)S(1)} %get-tuple-element.47), channel_id=1, source_target_pairs={{8,0},{16,8},{24,16},{32,24},{40,32},{48,40},{56,48},{64,56},{72,6... | collective-permute-start | bytes 589832 | tf_op jit(solution)/shard_map/ppermute | solution.py:323
  127.5 0.9 copy-start.6
  128.4 0.8 copy-start.10
  129.2 1.6 copy-start.16
  129.2 1.6 copy-start.18
  129.2 1.5 collective-permute-start.18
  130.8 53.2 %copy-start.7 = (f32[4,200,256]{2,1,0:T(8,128)S(1)}, f32[4,200,256]{2,1,0:T(8,128)}, u32[]{:S(2)}) copy-start(f32[4,200,256]{2,1,0:T(8,128)} %copy-done.6) | copy-start | bytes 2457604
  161.5 7.1 %copy-start.19 = (f32[4,96,128]{2,1,0:T(8,128)S(1)}, f32[4,96,128]{2,1,0:T(8,128)}, u32[]{:S(2)}) copy-start(f32[4,96,128]{2,1,0:T(8,128)} %copy-done.18) | copy-start | bytes 589828
  161.5 9.6 %copy-start.17 = (f32[4,96,128]{2,1,0:T(8,128)S(1)}, f32[4,96,128]{2,1,0:T(8,128)}, u32[]{:S(2)}) copy-start(f32[4,96,128]{2,1,0:T(8,128)} %copy-done.16) | copy-start | bytes 589828
  161.5 19.0 %all-to-all-start.3 = ((f32[128,4,128]{2,1,0:T(4,128)}), f32[128,4,128]{2,1,0:T(4,128)S(1)}, u32[]{:S(2)}, u32[]{:S(2)}) async-start(f32[128,4,128]{2,1,0:T(4,128)} %broadcast_in_dim.5), calls=%async_computation.3 | async-start | bytes 524288 | tf_op jit(solution)/shard_map/all_to_all | solution.py:331
  168.6 15.4 %collective-permute-start.14 = (f32[4,96,128]{2,1,0:T(8,128)S(1)}, f32[4,96,128]{2,1,0:T(8,128)S(1)}, u32[]{:S(2)}, u32[]{:S(2)}) collective-permute-start(f32[4,96,128]{2,1,0:T(8,128)S(1)} %copy-done.19), channel_id=1, source_target_pairs={{0,1},{1,2},{2,3},{3,4},{4,5},{5,6},{6,7},{8,9},{9,10},{10,11},{11... | collective-permute-start | bytes 589832 | tf_op jit(solution)/shard_map/ppermute | solution.py:323
  171.1 12.9 %collective-permute-start.15 = (f32[4,96,128]{2,1,0:T(8,128)S(1)}, f32[4,96,128]{2,1,0:T(8,128)S(1)}, u32[]{:S(2)}, u32[]{:S(2)}) collective-permute-start(f32[4,96,128]{2,1,0:T(8,128)S(1)} %copy-done.17), channel_id=1, source_target_pairs={{1,0},{2,1},{3,2},{4,3},{5,4},{6,5},{7,6},{9,8},{10,9},{11,10},{12... | collective-permute-start | bytes 589832 | tf_op jit(solution)/shard_map/ppermute | solution.py:323
  180.6 17.7 %collective-permute-start.19 = (f32[4,128,128]{2,1,0:T(8,128)S(1)}, f32[4,128,128]{2,1,0:T(8,128)S(1)}, u32[]{:S(2)}, u32[]{:S(2)}) collective-permute-start(f32[4,128,128]{2,1,0:T(8,128)S(1)} %bitcast.27), channel_id=1, source_target_pairs={{0,8},{8,0},{1,9},{9,1},{2,10},{10,2},{3,11},{11,3},{4,12},{12,4},... | collective-permute-start | bytes 786440 | tf_op jit(solution)/shard_map/ppermute | solution.py:327
  184.3 7.1 %collective-permute-start.16 = (f32[4,96,128]{2,1,0:T(8,128)S(1)}, f32[4,96,128]{2,1,0:T(8,128)S(1)}, u32[]{:S(2)}, u32[]{:S(2)}) collective-permute-start(f32[4,96,128]{2,1,0:T(8,128)S(1)} %get-tuple-element.57), channel_id=1, source_target_pairs={{0,8},{8,16},{16,24},{24,32},{32,40},{40,48},{48,56},{56,64},{64,7... | collective-permute-start | bytes 589832 | tf_op jit(solution)/shard_map/ppermute | solution.py:323
  188.8 8.5 %collective-permute-start.17 = (f32[4,96,128]{2,1,0:T(8,128)S(1)}, f32[4,96,128]{2,1,0:T(8,128)S(1)}, u32[]{:S(2)}, u32[]{:S(2)}) collective-permute-start(f32[4,96,128]{2,1,0:T(8,128)S(1)} %get-tuple-element.58), channel_id=1, source_target_pairs={{8,0},{16,8},{24,16},{32,24},{40,32},{48,40},{56,48},{64,56},{72,6... | collective-permute-start | bytes 589832 | tf_op jit(solution)/shard_map/ppermute | solution.py:323
  197.3 1.0 copy-start.11

commit v3 on v2

v3 whole, which is shorter than its diff:
```python
import math

import jax
import jax.numpy as jnp
import numpy as np
from jax import lax
from jax.experimental import pallas as pl
from jax.experimental.pallas import tpu as pltpu
from jax.sharding import Mesh, PartitionSpec as P


WIN = 128
OVL = 32
EXT = WIN + 2 * OVL
TALL = EXT + 8
MODES = 4
OBJECT_RATE = 0.5
PROBE_RATE = 0.5
FLOOR = 0.1

AXES = ("z", "xh", "core", "y", "xl")
SIZES = (8, 2, 2, 4, 2)
ROW = ("z", "xh", "core")
COL = ("y", "xl")
CHIPS = ("z", "xh", "y", "xl")
N_ROW = 32
N_COL = 8
N_CHIPS = 128
CORE = 10
XLOW = 11

F32 = jnp.float32
BF16 = jnp.bfloat16


def dft_tables():
    counter = np.arange(WIN, dtype=np.int64)
    phase = (counter[:, None] * counter[None, :] % WIN).astype(np.float64) * (-2.0 * math.pi / WIN)
    out = []
    for table in (np.cos(phase) / math.sqrt(WIN), np.sin(phase) / math.sqrt(WIN)):
        high = table.astype(np.float32).astype(jnp.bfloat16)
        low = (table - high.astype(np.float64)).astype(np.float32).astype(jnp.bfloat16)
        out += [high, low]
    return np.stack(out)


def full_tables(refs):
    out = []
    for part in range(2):
        cosine, sine = refs[part], refs[2 + part]
        out.append(grid_of([[cosine, sine], [-sine, cosine]]))
        out.append(grid_of([[cosine, -sine], [sine, cosine]]))
    return out


def lanes(shape):
    return lax.broadcasted_iota(jnp.int32, shape, len(shape) - 1)


def split(x):
    high = x.astype(BF16)
    return high, (x - high.astype(F32)).astype(BF16)


def dot(a, b):
    return lax.dot_general(a, b, (((1,), (0,)), ((), ())), preferred_element_type=F32)


def grid_of(blocks):
    return jnp.concatenate([jnp.concatenate(line, axis=1) for line in blocks], axis=0)


def blocks_of(x):
    half = WIN
    return [[x[:half, :half], x[:half, half:]], [x[half:, :half], x[half:, half:]]]


def transposed(blocks):
    return [[blocks[0][0], blocks[1][0]], [blocks[0][1], blocks[1][1]]]


def apply_right(pairs, high, low):
    out = []
    for blocks in pairs:
        xh, xl = split(grid_of(blocks))
        out.append(blocks_of(dot(xh, high) + dot(xh, low) + dot(xl, high)))
    return out


def apply_left(pairs, high, low):
    out = []
    for blocks in pairs:
        xh, xl = split(grid_of(transposed(blocks)))
        out.append(transposed(blocks_of(dot(high, xh) + dot(low, xh) + dot(high, xl))))
    return out


def product(a, b):
    return [a[0] * b[0] - a[1] * b[1], a[0] * b[1] + a[1] * b[0]]


def conj_product(a, b):
    return [a[0] * b[0] + a[1] * b[1], a[0] * b[1] - a[1] * b[0]]


def per_mode(pairs, fn):
    return [[fn(pairs[m // 2][m % 2], m) for m in (2 * k, 2 * k + 1)] for k in range(2)]


def place_window(e_ref, oy, ox, which):
    base = pl.multiple_of(oy // 8 * 8, 8)
    up = (WIN + 8 - oy % 8) % (WIN + 8)
    back = (WIN - ox) % WIN
    parts = []
    for t in range(2):
        rows = e_ref[which, pl.ds(base, WIN + 8), t * WIN : (t + 1) * WIN]
        parts.append(pltpu.roll(pltpu.roll(rows, up, 0)[:WIN], back, 1))
    first, second = parts
    return jnp.where(lanes((WIN, WIN)) < WIN - ox, first, second)


def pack_cols(tile):
    half = EXT // 2
    lane = lanes((half, WIN))
    return jnp.where(lane < 64, tile[:half], pltpu.roll(tile[half:], 64, 1))


def unpack_cols(packed):
    low = lanes(packed.shape) < 64
    return jnp.concatenate(
        [jnp.where(low, packed, 0.0), jnp.where(low, pltpu.roll(packed, 64, 1), 0.0)], axis=0
    )


def pack_rows(first, second):
    lane = lanes((32, WIN))
    rest = jnp.where(lane < 64, second[:32], pltpu.roll(second[32:], 64, 1))
    return jnp.concatenate([first, rest], axis=0)


def unpack_rows(packed):
    rest = packed[64:]
    low = lanes(rest.shape) < 64
    second = jnp.concatenate(
        [jnp.where(low, rest, 0.0), jnp.where(low, pltpu.roll(rest, 64, 1), 0.0)], axis=0
    )
    return packed[:64], second


def by_parity(odd, pair, near, far, a):
    first, last = pair
    near[a] = jnp.where(odd, first, last)
    far[a] = jnp.where(odd, last, first)


def sides(odd, near, far, a):
    return jnp.where(odd, near[a], far[a]), jnp.where(odd, far[a], near[a])


def cut_kernel(info, obj, near, far):
    for a in range(4):
        by_parity(info[CORE - 6] == 1, (obj[a, :OVL], obj[a, WIN - OVL :]), near, far, a)


def halo_kernel(info, obj, row_near, row_far, near, far):
    lane = lanes((48, WIN)) // 32
    for a in range(4):
        north, south = sides(info[CORE] == 1, row_near, row_far, a)
        column = jnp.concatenate([north, obj[a], south], axis=0)
        strips = []
        for base in (0, 32):
            out = jnp.zeros((48, WIN), F32)
            for i in range(4):
                part = column[48 * i : 48 * i + 48]
                shift = (32 * i + base) % WIN
                part = pltpu.roll(part, shift, 1) if shift else part
                out = jnp.where(lane == i, part, out)
            strips.append(out)
        by_parity(info[XLOW] == 1, strips, near, far, a)


def build_extended(e_ref, info, obj, row_near, row_far, col_near, col_far):
    lane = lanes((EXT, WIN))
    for a in range(4):
        north, south = sides(info[CORE] == 1, row_near, row_far, a)
        west, east = sides(info[XLOW] == 1, col_near, col_far, a)
        column = jnp.concatenate([north, obj[a], south], axis=0)
        column = pltpu.roll(column, 32, 1)
        lefts, rights = [], []
        for i in range(4):
            shift = (WIN - 32 * i) % WIN
            lefts.append(pltpu.roll(west, shift, 1) if shift else west)
            shift = (32 - 32 * i) % WIN
            rights.append(pltpu.roll(east, shift, 1) if shift else east)
        e_ref[a, :EXT, :WIN] = jnp.where(lane < 32, jnp.concatenate(lefts, axis=0), column)
        e_ref[a, :EXT, WIN:] = jnp.where(
            lane < 32, column, jnp.where(lane < 64, jnp.concatenate(rights, axis=0), 0.0)
        )


def place_gradient(info, b, grads, g_ref):
    oy, ox = info[2 * b], info[2 * b + 1]
    lane = lanes((WIN, WIN))
    base = pl.multiple_of(oy // 8 * 8, 8)
    gap = jnp.zeros((8, WIN), F32)
    for a in range(4):
        g_ref[a] = jnp.zeros((TALL, 2 * WIN), F32)
        turned = pltpu.roll(grads[a], ox, 1)
        for t in range(2):
            part = jnp.where(lane >= ox if t == 0 else lane < ox, turned, 0.0)
            part = pltpu.roll(jnp.concatenate([part, gap], axis=0), oy % 8, 0)
            g_ref[a, pl.ds(base, WIN + 8), t * WIN : (t + 1) * WIN] = part


def row_bands(info, rn, rf, a):
    north, south = (unpack_rows(x) for x in sides(info[CORE] == 1, rn, rf, a))
    gap = jnp.zeros((64, WIN), F32)
    return [jnp.concatenate([north[t], gap, south[t]], axis=0) for t in range(2)]


def total_gradient(info, g_ref, rows, cols, a):
    west_east = sides(info[XLOW] == 1, *cols, a)
    bands = row_bands(info, *rows, a)
    return [
        g_ref[a, :EXT, t * WIN : (t + 1) * WIN] + unpack_cols(west_east[t]) + bands[t]
        for t in range(2)
    ]


def pack_extended(e_ref, out):
    for a in range(4):
        out[a, :EXT] = e_ref[a, :EXT, :WIN]
        out[a, EXT:] = pack_cols(e_ref[a, :EXT, WIN:])


def own_part(parts):
    lane = lanes((WIN, WIN))
    turned = [pltpu.roll(x[OVL : OVL + WIN], WIN - OVL, 1) for x in parts]
    return jnp.where(lane < WIN - OVL, turned[0], turned[1])


def update_extended(e_ref, g_ref, info, b, old, grads, rows, cols):
    place_gradient(info, b - 1, grads, g_ref)
    row = lax.broadcasted_iota(jnp.int32, (EXT, WIN), 0)
    lane = lanes((EXT, WIN))
    in_rows = (row >= info[6]) & (row < info[7])
    keep = (in_rows & (lane >= info[8]), in_rows & (lane + WIN < info[9]))
    for a in range(4):
        grad = total_gradient(info, g_ref, rows, cols, a)
        before = (old[a, :EXT], unpack_cols(old[a, EXT:]))
        for t in range(2):
            value = before[t] - OBJECT_RATE * grad[t]
            e_ref[a, :EXT, t * WIN : (t + 1) * WIN] = jnp.where(keep[t], value, 0.0)


def step_core(info, b, e_ref, probe, loads, kernel, measured, tables, g_ref, w_ref, near, far):
    oy, ox = info[2 * b], info[2 * b + 1]
    o1 = [place_window(e_ref, oy, ox, 0), place_window(e_ref, oy, ox, 1)]
    o2 = [place_window(e_ref, oy, ox, 2), place_window(e_ref, oy, ox, 3)]
    loads[1].wait()
    a_high, b_high, a_low, b_low = full_tables(tables)
    x = per_mode(probe, lambda p, m: product(p, o1))
    for load in loads[2:]:
        load.wait()
    phase = [kernel[0], kernel[1]]
    x = apply_left(apply_right(x, a_high, a_low), b_high, b_low)
    x = per_mode(x, lambda v, m: product(phase, v))
    phi = apply_right(apply_left(x, a_high, a_low), b_high, b_low)
    x = per_mode(phi, lambda v, m: product(v, o2))
    x = apply_left(apply_right(x, a_high, a_low), b_high, b_low)
    intensity = sum(x[m // 2][m % 2][c] * x[m // 2][m % 2][c] for m in range(MODES) for c in range(2))
    factor = 1.0 - measured[...] / jnp.sqrt(intensity + FLOOR)
    x = per_mode(x, lambda v, m: [v[0] * factor, v[1] * factor])
    chi2 = apply_right(apply_left(x, a_high, a_low), b_high, b_low)
    terms2 = [conj_product(phi[m // 2][m % 2], chi2[m // 2][m % 2]) for m in range(MODES)]
    x = per_mode(chi2, lambda v, m: conj_product(o2, v))
    x = apply_left(apply_right(x, a_high, a_low), b_high, b_low)
    x = per_mode(x, lambda v, m: conj_product(phase, v))
    chi1 = apply_right(apply_left(x, a_high, a_low), b_high, b_low)
    terms1 = [conj_product(probe[m // 2][m % 2], chi1[m // 2][m % 2]) for m in range(MODES)]
    grads = [sum(t[c] for t in terms1) for c in range(2)] + [sum(t[c] for t in terms2) for c in range(2)]
    for a in range(4):
        w_ref[a] = grads[a]
    place_gradient(info, b, grads, g_ref)
    for a in range(4):
        up = pack_rows(g_ref[a, :64, :WIN], g_ref[a, :64, WIN:])
        down = pack_rows(g_ref[a, 128:EXT, :WIN], g_ref[a, 128:EXT, WIN:])
        by_parity(info[CORE] == 1, (up, down), near, far, a)
    return per_mode(chi1, lambda v, m: conj_product(o1, v))


def probe_blocks(probe_ref):
    return [[[probe_ref[2 * m], probe_ref[2 * m + 1]] for m in (2 * k, 2 * k + 1)] for k in range(2)]


def write_halves(info, grads, keep, send):
    first = info[CORE] == 0
    for i in range(4):
        low = grads[0][i // 2][i % 2]
        high = grads[1][i // 2][i % 2]
        keep[i] = jnp.where(first, low, high)
        send[i] = jnp.where(first, high, low)


def loads_of(b, probe, tables, kcos, ksin, measured, p_s, t_s, k_s, m_s, sem):
    pairs = (
        (probe, p_s), (tables, t_s), (kcos, k_s.at[0]), (ksin, k_s.at[1]), (measured.at[b], m_s)
    )
    copies = [pltpu.make_async_copy(x, y, sem.at[i]) for i, (x, y) in enumerate(pairs)]
    for copy in copies:
        copy.start()
    return copies


def first_kernel(info, obj, row_near, row_far, col_near, col_far, probe, tables, kcos, ksin, measured,
                 e_out, w_ref, near, far, keep, send, e_s, g_s, p_s, t_s, k_s, m_s, sem):
    loads = loads_of(0, probe, tables, kcos, ksin, measured, p_s, t_s, k_s, m_s, sem)
    build_extended(e_s, info, obj, row_near, row_far, col_near, col_far)
    pack_extended(e_s, e_out)
    loads[0].wait()
    grads = step_core(info, 0, e_s, probe_blocks(p_s), loads, k_s, m_s, t_s, g_s, w_ref, near, far)
    write_halves(info, grads, keep, send)


def second_kernel(info, old, grad, rn, rf, cn, cf, probe, tables, kcos, ksin, measured,
                  e_out, w_ref, near, far, held, e_s, g_s, p_s, t_s, k_s, m_s, h_s, sem):
    loads = loads_of(1, probe, tables, kcos, ksin, measured, p_s, t_s, k_s, m_s, sem)
    update_extended(e_s, g_s, info, 1, old, grad, (rn, rf), (cn, cf))
    pack_extended(e_s, e_out)
    loads[0].wait()
    grads = step_core(info, 1, e_s, probe_blocks(p_s), loads, k_s, m_s, t_s, g_s, w_ref, near, far)
    for m in range(MODES):
        h_s[2 * m] = grads[m // 2][m % 2][0]
        h_s[2 * m + 1] = grads[m // 2][m % 2][1]
    store = pltpu.make_async_copy(h_s, held, sem.at[5])
    store.start()
    store.wait()


def third_kernel(rate, info, old, grad, rn, rf, cn, cf, mine, other,
                 probe, tables, kcos, ksin, measured, held,
                 own, w_ref, near, far, keep, send, p_out, e_s, g_s, p_s, t_s, k_s, m_s, h_s, sem):
    loads = loads_of(2, probe, tables, kcos, ksin, measured, p_s, t_s, k_s, m_s, sem)
    load_held = pltpu.make_async_copy(held, h_s, sem.at[5])
    load_held.start()
    update_extended(e_s, g_s, info, 2, old, grad, (rn, rf), (cn, cf))
    for a in range(4):
        own[a] = own_part((e_s[a, :, :WIN], e_s[a, :, WIN:]))
    loads[0].wait()
    update_probe(rate, info, p_s, mine, other, p_out)
    grads = step_core(info, 2, e_s, probe_blocks(p_out), loads, k_s, m_s, t_s, g_s, w_ref, near, far)
    load_held.wait()
    grads = per_mode(grads, lambda v, m: [v[c] + h_s[2 * m + c] for c in range(2)])
    write_halves(info, grads, keep, send)


def update_probe(rate, info, probe, mine, other, out):
    first = info[CORE] == 0
    for i in range(4):
        out[i] = probe[i] - rate * jnp.where(first, mine[i], other[i])
        out[4 + i] = probe[4 + i] - rate * jnp.where(first, other[i], mine[i])


def middle_kernel(b, info, grad, rn, rf, near, far, g_s):
    place_gradient(info, b, grad, g_s)
    for a in range(4):
        bands = row_bands(info, rn, rf, a)
        strips = [pack_cols(g_s[a, :EXT, t * WIN : (t + 1) * WIN] + bands[t]) for t in range(2)]
        by_parity(info[XLOW] == 1, strips, near, far, a)


def object_kernel(info, own, grad, rn, rf, cn, cf, out, g_s):
    place_gradient(info, 2, grad, g_s)
    for a in range(4):
        total = total_gradient(info, g_s, (rn, rf), (cn, cf), a)
        out[a] = own[a] - OBJECT_RATE * own_part(total)


SMEM = pl.BlockSpec(memory_space=pltpu.SMEM)
VMEM = pl.BlockSpec(memory_space=pltpu.VMEM)


def call(kernel, outs, info, *args, loads=(), stores=(), scratch=(), on_chip=True):
    args = [pltpu.with_memory_space_constraint(x, pltpu.VMEM) for x in args]
    head = [] if info is None else [info]
    loads = [pltpu.with_memory_space_constraint(x, pltpu.HBM) for x in loads]
    apart = pl.BlockSpec(memory_space=pltpu.HBM)
    return pl.pallas_call(
        kernel,
        out_shape=[
            pltpu.VMEM(s, F32) if on_chip else jax.ShapeDtypeStruct(s, F32) for s in outs
        ] + [pltpu.HBM(s, F32) for s in stores],
        in_specs=[SMEM] * len(head) + [VMEM] * len(args) + [apart] * len(loads),
        out_specs=[VMEM] * len(outs) + [apart] * len(stores),
        scratch_shapes=list(scratch),
        compiler_params=pltpu.CompilerParams(vmem_limit_bytes=32 << 20),
    )(*head, *args, *loads)


EXT_SHAPE = (4, EXT + EXT // 2, WIN)
BAND = (4, EXT // 2, WIN)
HALF = (4, WIN, WIN)
PLACE = pltpu.VMEM((4, TALL, 2 * WIN), F32)
STEP_SCRATCH = (
    PLACE,
    PLACE,
    pltpu.VMEM((2 * MODES, WIN, WIN), F32),
    pltpu.VMEM((4, WIN, WIN), BF16),
    pltpu.VMEM((2, WIN, WIN), F32),
    pltpu.VMEM((WIN, WIN), F32),
)
SEMS = (pltpu.SemaphoreType.DMA((6,)),)
HELD = (pltpu.VMEM((2 * MODES, WIN, WIN), F32),)


def swap_near(x, axis):
    return lax.ppermute(x, axis, [(0, 1), (1, 0)])


def swap_far(x, axes, size):
    pairs = [(i, i + 1) for i in range(1, size - 1, 2)]
    return lax.ppermute(x, axes, pairs + [(j, i) for i, j in pairs])


def rows_swapped(near, far):
    return swap_near(near, "core"), swap_far(far, ROW, N_ROW)


def cols_swapped(near, far):
    return swap_near(near, "xl"), swap_far(far, COL, N_COL)


def swap_cores(x):
    return lax.ppermute(x, "core", [(0, 1), (1, 0)])


def chip_exchange(x):
    return lax.all_to_all(x, CHIPS, 0, 0, tiled=True)


def join_kernel(keep, other, out):
    out[...] = keep[...] + other[...]


def spread_kernel(parts, out):
    total = jnp.sum(parts[...].reshape(-1, 8, WIN), axis=0)
    total = total + pltpu.roll(total, 4, 0)
    out[...] = jnp.broadcast_to(total[None], (HALF[0] * WIN // 8, 8, WIN)).reshape(HALF)


def summed_half(keep, send):
    (total,) = call(join_kernel, [HALF], None, keep, swap_cores(send))
    parts = chip_exchange(total.reshape(N_CHIPS, -1, WIN)).reshape(HALF)
    (spread,) = call(spread_kernel, [HALF], None, parts)
    return chip_exchange(spread.reshape(N_CHIPS, -1, WIN)).reshape(HALF)


def exchanged(info, grad, near, far, b):
    rows = rows_swapped(near, far)
    near, far = call(
        lambda *refs: middle_kernel(b, *refs), [BAND, BAND], info, grad, *rows,
        scratch=(PLACE,),
    )
    return grad, *rows, *cols_swapped(near, far)


def steps(object_field, probe, kernel_phase, amplitudes, offsets):
    rate = PROBE_RATE / math.sqrt(N_ROW * N_COL)
    tables = jnp.asarray(dft_tables())
    kcos, ksin = jnp.cos(kernel_phase), jnp.sin(kernel_phase)
    row = lax.axis_index(ROW)
    col = lax.axis_index(COL)
    core = lax.axis_index("core")
    edges = jnp.stack([
        jnp.where(row == 0, OVL, 0),
        jnp.where(row == N_ROW - 1, EXT - OVL, EXT),
        jnp.where(col == 0, OVL, 0),
        jnp.where(col == N_COL - 1, EXT - OVL, EXT),
        core,
        lax.axis_index("xl"),
    ]).astype(jnp.int32)
    info = jnp.concatenate([offsets.reshape(-1), edges])
    measured = amplitudes[:, 0, 0]
    obj = object_field.reshape(4, WIN, WIN)
    probe = probe.reshape(2 * MODES, WIN, WIN)
    loads = (probe, tables, kcos, ksin, measured)

    rows = call(cut_kernel, [(4, OVL, WIN)] * 2, edges, obj)
    rows = rows_swapped(*rows)
    cols = call(halo_kernel, [(4, 48, WIN)] * 2, info, obj, *rows)
    cols = cols_swapped(*cols)

    step_outs = [EXT_SHAPE, HALF, BAND, BAND]
    whole = (2 * MODES, WIN, WIN)
    extended, grad, near, far, keep0, send0 = call(
        first_kernel, step_outs + [HALF, HALF], info, obj, *rows, *cols,
        loads=loads, scratch=STEP_SCRATCH + SEMS,
    )
    moves = exchanged(info, grad, near, far, 0)
    mine0 = summed_half(keep0, send0)
    other0 = swap_cores(mine0)
    extended, grad, near, far, held = call(
        second_kernel, step_outs, info, extended, *moves,
        loads=loads, stores=(whole,), scratch=STEP_SCRATCH + HELD + SEMS,
    )
    moves = exchanged(info, grad, near, far, 1)
    own, grad, near, far, keep2, send2, probe = call(
        lambda *refs: third_kernel(rate, *refs), [HALF] + step_outs[1:] + [HALF, HALF, whole],
        info, extended, *moves, mine0, other0,
        loads=loads + (held,), scratch=STEP_SCRATCH + HELD + SEMS,
    )
    moves = exchanged(info, grad, near, far, 2)
    mine = summed_half(keep2, send2)
    other = swap_cores(mine)
    (obj,) = call(object_kernel, [HALF], info, own, *moves, scratch=(PLACE,), on_chip=False)
    (probe,) = call(
        lambda *refs: update_probe(rate, *refs), [(2 * MODES, WIN, WIN)],
        info, probe, mine, other, on_chip=False,
    )
    return obj.reshape(2, 2, WIN, WIN), probe.reshape(MODES, 2, WIN, WIN)


def solution(mesh):
    fine = Mesh(mesh.devices.reshape(SIZES), AXES)
    in_specs = (
        P(None, None, ROW, COL),
        P(),
        P(),
        P(None, ROW, COL, None, None),
        P(None, ROW, COL, None),
    )
    out_specs = (P(None, None, ROW, COL), P())
    return jax.shard_map(steps, mesh=fine, in_specs=in_specs, out_specs=out_specs, check_vma=False)
```

time: 201 us -> 182 us (0.905)
  the two profiles are of different devices: /device:TPU:1 before, /device:TPU:8 now
where the time goes in v3:
time: 182 us; the launch traced here: 181 us
  starting transfers between devices  62.7 us (34%)
  waiting for transfers between devices  55 us (30%)
  Pallas kernels  30.4 us (17%)
  blocking collectives  30.1 us (17%)
  local copies, waits for them, and re-layouts  2.2 us (1%)
    all_to_all x3, starting transfers between devices, chip_exchange(): return lax.all_to_all(x, CHIPS, 0, 0, tiled=True)  30.4 us
    pallas_call x14, Pallas kernels, call(): pl.pallas_call(kernel, out_shape=[pltpu.VMEM(s, F32) if on_chip else jax....  30.4 us
    all_to_all x1, blocking collectives, chip_exchange(): return lax.all_to_all(x, CHIPS, 0, 0, tiled=True)  30.1 us
    all_to_all x3, waiting for transfers between devices, chip_exchange(): return lax.all_to_all(x, CHIPS, 0, 0, tiled=True)  26.7 us
    ppermute x8, starting transfers between devices, swap_far(): return lax.ppermute(x, axes, pairs + [(j, i) for i, j in pairs])  15.8 us
    ppermute x8, waiting for transfers between devices, swap_far(): return lax.ppermute(x, axes, pairs + [(j, i) for i, j in pairs])  14.2 us
    ppermute x8, waiting for transfers between devices, swap_near(): return lax.ppermute(x, axis, [(0, 1), (1, 0)])  11.7 us
    ppermute x4, starting transfers between devices, swap_cores(): return lax.ppermute(x, 'core', [(0, 1), (1, 0)])  10.9 us
  transfers between devices with their start and end apart: 23, of which 12 were waited for; matrix products, arithmetic and copies ran while one was open for 1% of the time, Pallas kernels for 7%

profile of v3, /device:TPU:8, one launch (start us, length us, event | category | flops | bytes accessed | tf_op | source)
XLA Modules:
  0.0 181.2 jit_solution(14731531959054775187)
XLA Ops:
  0.7 0.1 stack.27.info
  0.7 1.0 copy-done
  1.7 0.6 shard_map.77
  2.3 0.0 copy-start.3
  2.3 0.1 collective-permute-start
  2.4 0.7 collective-permute-start.1
  3.1 0.1 copy.9
  3.1 0.1 reshape.43
  3.2 0.1 concatenate.4.info.refs_0_
  3.3 0.3 collective-permute-done.row_near
  3.6 0.0 collective-permute-done.1.row_far
  3.6 0.8 shard_map.78
  4.4 1.6 collective-permute-start.2
  6.0 4.0 %collective-permute-start.3 = (f32[4,48,128]{2,1,0:T(8,128)S(1)}, f32[4,48,128]{2,1,0:T(8,128)S(1)}, u32[]{:S(2)}, u32[]{:S(2)}) collective-permute-start(f32[4,48,128]{2,1,0:T(8,128)S(1)} %get-tuple-element.33), channel_id=1, source_target_pairs={{1,2},{3,4},{5,6},{2,1},{4,3},{6,5},{9,10},{11,12},{13,14},{10,9},... | collective-permute-start | bytes 294920 | tf_op jit(solution)/shard_map/ppermute | solution.py:422
  10.0 0.9 fusion
  10.9 0.0 collective-permute-done.2.col_near
  10.9 2.5 %collective-permute-done.3.col_far = f32[4,48,128]{2,1,0:T(8,128)S(1)} collective-permute-done((f32[4,48,128]{2,1,0:T(8,128)S(1)}, f32[4,48,128]{2,1,0:T(8,128)S(1)}, u32[]{:S(2)}, u32[]{:S(2)}) %collective-permute-start.3) | collective-permute-done | bytes 98336 | tf_op jit(solution)/shard_map/ppermute | solution.py:422
  13.4 6.7 %shard_map.79 = (f32[4,288,128]{2,1,0:T(8,128)S(1)}, f32[4,128,128]{2,1,0:T(8,128)S(1)}, f32[4,96,128]{2,1,0:T(8,128)S(1)}, f32[4,96,128]{2,1,0:T(8,128)S(1)}, f...) custom-call(s32[12]{0:T(128)S(1)} %concatenate.4.info.refs_0_, f32[4,128,128]{2,1,0:T(8,128)S(1)} %bitcast.23, ...), custom_call_target="tpu_custom_call" | custom-call | tf_op jit(solution)/shard_map/pallas_call | solution.py:388
  20.0 5.0 %collective-permute-start.12 = (f32[4,128,128]{2,1,0:T(8,128)S(1)}, f32[4,128,128]{2,1,0:T(8,128)S(1)}, u32[]{:S(2)}, u32[]{:S(2)}) collective-permute-start(f32[4,128,128]{2,1,0:T(8,128)S(1)} %get-tuple-element.47), channel_id=1, source_target_pairs={{0,8},{8,0},{1,9},{9,1},{2,10},{10,2},{3,11},{11,3},{4,12},{12,4},... | collective-permute-start | bytes 786440 | tf_op jit(solution)/shard_map/ppermute | solution.py:434
  25.0 1.2 collective-permute-done.12.other
  26.2 0.7 shard_map.83
  26.9 17.3 %all-to-all-start = ((f32[128,4,128]{2,1,0:T(4,128)}), f32[128,4,128]{2,1,0:T(4,128)S(1)}, u32[]{:S(2)}, u32[]{:S(2)}) async-start(f32[128,4,128]{2,1,0:T(4,128)} %bitcast.9), calls=%async_computation | async-start | bytes 524288 | tf_op jit(solution)/shard_map/all_to_all | solution.py:438
  44.2 0.1 collective-permute-start.4
  44.3 0.7 collective-permute-start.5
  45.0 14.2 %all-to-all-done = f32[128,4,128]{2,1,0:T(4,128)S(1)} async-done(((f32[128,4,128]{2,1,0:T(4,128)}), f32[128,4,128]{2,1,0:T(4,128)S(1)}, u32[]{:S(2)}, u32[]{:S(2)}) %all-to-all-start) | async-done | bytes 262176 | tf_op jit(solution)/shard_map/all_to_all | solution.py:438
  59.2 0.8 shard_map.84
  60.0 6.6 %all-to-all-start.1 = ((f32[128,4,128]{2,1,0:T(4,128)}), f32[128,4,128]{2,1,0:T(4,128)S(1)}, u32[]{:S(2)}, u32[]{:S(2)}) async-start(f32[128,4,128]{2,1,0:T(4,128)} %bitcast.11), calls=%async_computation.1 | async-start | bytes 524288 | tf_op jit(solution)/shard_map/all_to_all | solution.py:438
  66.6 0.0 collective-permute-done.4.refs_2_.rn
  66.6 0.0 collective-permute-done.5.refs_3_.rf
  66.6 1.0 shard_map.80
  67.6 1.6 collective-permute-start.6
  69.2 3.1 %collective-permute-start.7 = (f32[4,96,128]{2,1,0:T(8,128)S(1)}, f32[4,96,128]{2,1,0:T(8,128)S(1)}, u32[]{:S(2)}, u32[]{:S(2)}) collective-permute-start(f32[4,96,128]{2,1,0:T(8,128)S(1)} %get-tuple-element.39), channel_id=1, source_target_pairs={{1,2},{3,4},{5,6},{2,1},{4,3},{6,5},{9,10},{11,12},{13,14},{10,9},... | collective-permute-start | bytes 589832 | tf_op jit(solution)/shard_map/ppermute | solution.py:422
  72.2 4.3 %collective-permute-done.6.cn = f32[4,96,128]{2,1,0:T(8,128)S(1)} collective-permute-done((f32[4,96,128]{2,1,0:T(8,128)S(1)}, f32[4,96,128]{2,1,0:T(8,128)S(1)}, u32[]{:S(2)}, u32[]{:S(2)}) %collective-permute-start.6) | collective-permute-done | bytes 196640 | tf_op jit(solution)/shard_map/ppermute | solution.py:417
  76.6 3.0 %collective-permute-done.7.cf = f32[4,96,128]{2,1,0:T(8,128)S(1)} collective-permute-done((f32[4,96,128]{2,1,0:T(8,128)S(1)}, f32[4,96,128]{2,1,0:T(8,128)S(1)}, u32[]{:S(2)}, u32[]{:S(2)}) %collective-permute-start.7) | collective-permute-done | bytes 196640 | tf_op jit(solution)/shard_map/ppermute | solution.py:422
  79.6 7.1 %shard_map.81 = (f32[4,288,128]{2,1,0:T(8,128)S(1)}, f32[4,128,128]{2,1,0:T(8,128)S(1)}, f32[4,96,128]{2,1,0:T(8,128)S(1)}, f32[4,96,128]{2,1,0:T(8,128)S(1)}, f32[8,128,128]{2,1,0:T(8,128)}) custom-call(s32[12]{0:T(128)S(1)} %concatenate.4.info.refs_0_, f32[4,288,128]{2,1,0:T(8,128)S(1)} %get-tuple-element.34.old, ...), custom_call_target="tpu_custom_call" | custom-call | tf_op jit(solution)/shard_map/pallas_call | solution.py:388
  86.7 0.1 collective-permute-start.8
  86.8 0.7 collective-permute-start.9
  87.4 0.0 all-to-all-done.1
  87.5 3.9 %collective-permute-start.13 = (f32[4,128,128]{2,1,0:T(8,128)S(1)}, f32[4,128,128]{2,1,0:T(8,128)S(1)}, u32[]{:S(2)}, u32[]{:S(2)}) collective-permute-start(f32[4,128,128]{2,1,0:T(8,128)S(1)} %bitcast.29), channel_id=1, source_target_pairs={{0,8},{8,0},{1,9},{9,1},{2,10},{10,2},{3,11},{11,3},{4,12},{12,4},... | collective-permute-start | bytes 786440 | tf_op jit(solution)/shard_map/ppermute | solution.py:434
  91.4 0.0 collective-permute-done.8.refs_2_.refs_3_
  91.4 1.0 shard_map.82
  92.4 1.4 collective-permute-start.10
  93.8 2.0 %collective-permute-start.11 = (f32[4,96,128]{2,1,0:T(8,128)S(1)}, f32[4,96,128]{2,1,0:T(8,128)S(1)}, u32[]{:S(2)}, u32[]{:S(2)}) collective-permute-start(f32[4,96,128]{2,1,0:T(8,128)S(1)} %get-tuple-element.45), channel_id=1, source_target_pairs={{1,2},{3,4},{5,6},{2,1},{4,3},{6,5},{9,10},{11,12},{13,14},{10,9},... | collective-permute-start | bytes 589832 | tf_op jit(solution)/shard_map/ppermute | solution.py:422
  95.8 3.9 %collective-permute-done.10.refs_5_ = f32[4,96,128]{2,1,0:T(8,128)S(1)} collective-permute-done((f32[4,96,128]{2,1,0:T(8,128)S(1)}, f32[4,96,128]{2,1,0:T(8,128)S(1)}, u32[]{:S(2)}, u32[]{:S(2)}) %collective-permute-start.10) | collective-permute-done | bytes 196640 | tf_op jit(solution)/shard_map/ppermute | solution.py:417
  99.8 4.3 %collective-permute-done.11.refs_6_ = f32[4,96,128]{2,1,0:T(8,128)S(1)} collective-permute-done((f32[4,96,128]{2,1,0:T(8,128)S(1)}, f32[4,96,128]{2,1,0:T(8,128)S(1)}, u32[]{:S(2)}, u32[]{:S(2)}) %collective-permute-start.11) | collective-permute-done | bytes 196640 | tf_op jit(solution)/shard_map/ppermute | solution.py:422
  104.0 0.0 collective-permute-done.13.refs_8_
  104.1 6.6 %shard_map.85 = (f32[4,128,128]{2,1,0:T(8,128)S(1)}, f32[4,128,128]{2,1,0:T(8,128)S(1)}, f32[4,96,128]{2,1,0:T(8,128)S(1)}, f32[4,96,128]{2,1,0:T(8,128)S(1)}, f...) custom-call(s32[12]{0:T(128)S(1)} %concatenate.4.info.refs_0_, ...), custom_call_target="tpu_custom_call" | custom-call | tf_op jit(solution)/shard_map/pallas_call | solution.py:388
  110.7 2.0 %collective-permute-start.18 = (f32[4,128,128]{2,1,0:T(8,128)S(1)}, f32[4,128,128]{2,1,0:T(8,128)S(1)}, u32[]{:S(2)}, u32[]{:S(2)}) collective-permute-start(f32[4,128,128]{2,1,0:T(8,128)S(1)} %get-tuple-element.57), channel_id=1, source_target_pairs={{0,8},{8,0},{1,9},{9,1},{2,10},{10,2},{3,11},{11,3},{4,12},{12,4},... | collective-permute-start | bytes 786440 | tf_op jit(solution)/shard_map/ppermute | solution.py:434
  112.7 1.2 collective-permute-done.18.other
  113.9 30.1 %all_to_all.20 = f32[128,4,128]{2,1,0:T(4,128)S(1)} all-to-all(f32[128,4,128]{2,1,0:T(4,128)S(1)} %bitcast.24), channel_id=1, replica_groups=mesh['z'=8,'xh'=2,'core'=2,'y'=4,'xl'=2] {'z','xh','y','xl'}, dimensions={0} | all-to-all | bytes 524288 | tf_op jit(solution)/shard_map/all_to_all | solution.py:438
  144.0 0.8 shard_map.89
  144.8 6.6 %all-to-all-start.3 = ((f32[128,4,128]{2,1,0:T(4,128)}), f32[128,4,128]{2,1,0:T(4,128)S(1)}, u32[]{:S(2)}, u32[]{:S(2)}) async-start(f32[128,4,128]{2,1,0:T(4,128)} %bitcast.16), calls=%async_computation.3 | async-start | bytes 524288 | tf_op jit(solution)/shard_map/all_to_all | solution.py:438
  151.3 0.1 collective-permute-start.14
  151.4 0.7 collective-permute-start.15
  152.1 12.5 %all-to-all-done.3 = f32[128,4,128]{2,1,0:T(4,128)S(1)} async-done(((f32[128,4,128]{2,1,0:T(4,128)}), f32[128,4,128]{2,1,0:T(4,128)S(1)}, u32[]{:S(2)}, u32[]{:S(2)}) %all-to-all-start.3) | async-done | bytes 262176 | tf_op jit(solution)/shard_map/all_to_all | solution.py:438
  164.6 0.0 collective-permute-done.14.refs_2_.rn
  164.6 0.0 collective-permute-done.15.refs_3_.rf
  164.6 1.0 shard_map.86
  165.7 0.7 collective-permute-start.16
  166.4 4.0 %collective-permute-start.17 = (f32[4,96,128]{2,1,0:T(8,128)S(1)}, f32[4,96,128]{2,1,0:T(8,128)S(1)}, u32[]{:S(2)}, u32[]{:S(2)}) collective-permute-start(f32[4,96,128]{2,1,0:T(8,128)S(1)} %get-tuple-element.54), channel_id=1, source_target_pairs={{1,2},{3,4},{5,6},{2,1},{4,3},{6,5},{9,10},{11,12},{13,14},{10,9},... | collective-permute-start | bytes 589832 | tf_op jit(solution)/shard_map/ppermute | solution.py:422
  170.4 3.2 %collective-permute-done.16.cn = f32[4,96,128]{2,1,0:T(8,128)S(1)} collective-permute-done((f32[4,96,128]{2,1,0:T(8,128)S(1)}, f32[4,96,128]{2,1,0:T(8,128)S(1)}, u32[]{:S(2)}, u32[]{:S(2)}) %collective-permute-start.16) | collective-permute-done | bytes 196640 | tf_op jit(solution)/shard_map/ppermute | solution.py:417
  173.5 4.4 %collective-permute-done.17.cf = f32[4,96,128]{2,1,0:T(8,128)S(1)} collective-permute-done((f32[4,96,128]{2,1,0:T(8,128)S(1)}, f32[4,96,128]{2,1,0:T(8,128)S(1)}, u32[]{:S(2)}, u32[]{:S(2)}) %collective-permute-start.17) | collective-permute-done | bytes 196640 | tf_op jit(solution)/shard_map/ppermute | solution.py:422
  178.0 1.9 %shard_map.87 = f32[4,128,128]{2,1,0:T(8,128)} custom-call(s32[12]{0:T(128)S(1)} %concatenate.4.info.refs_0_, f32[4,128,128]{2,1,0:T(8,128)S(1)} %get-tuple-element.49.own, f32[4,128,128]{2,1,0:T(8,128)S(1)} %get-tuple-element.50.refs_1_.grad, f32[4,96,128]{2,1,0:T(8,128)S(1)} %collective-permute-done.14.refs_2_.rn, ...), custom_call_target="tpu_custom_call" | custom-call | tf_op jit(solution)/shard_map/pallas_call | solution.py:388
  179.8 1.4 shard_map.90
  (10 shorter events, 0.0 us)
Async XLA Ops:
  0.7 1.0 copy-start
  1.7 1.9 %copy-start.1 = (f32[2,2,128,128]{3,2,1,0:T(8,128)S(1)}, f32[2,2,128,128]{3,2,1,0:T(8,128)}, u32[]{:S(2)}) copy-start(f32[2,2,128,128]{3,2,1,0:T(8,128)} %param.6) | copy-start | bytes 786436
  2.3 0.8 copy-start.3
  2.3 1.3 collective-permute-start
  2.4 1.2 collective-permute-start.1
  3.3 6.7 %copy-start.2 = (f32[128,128]{1,0:T(8,128)S(1)}, f32[128,128]{1,0:T(8,128)}, u32[]{:S(2)}) copy-start(f32[128,128]{1,0:T(8,128)} %param.8) | copy-start | bytes 196612
  4.4 6.5 %collective-permute-start.2 = (f32[4,48,128]{2,1,0:T(8,128)S(1)}, f32[4,48,128]{2,1,0:T(8,128)S(1)}, u32[]{:S(2)}, u32[]{:S(2)}) collective-permute-start(f32[4,48,128]{2,1,0:T(8,128)S(1)} %get-tuple-element.32), channel_id=1, source_target_pairs={{0,1},{1,0},{2,3},{3,2},{4,5},{5,4},{6,7},{7,6},{8,9},{9,8},{10,11... | collective-permute-start | bytes 294920 | tf_op jit(solution)/shard_map/ppermute | solution.py:417
  6.0 7.4 %collective-permute-start.3 = (f32[4,48,128]{2,1,0:T(8,128)S(1)}, f32[4,48,128]{2,1,0:T(8,128)S(1)}, u32[]{:S(2)}, u32[]{:S(2)}) collective-permute-start(f32[4,48,128]{2,1,0:T(8,128)S(1)} %get-tuple-element.33), channel_id=1, source_target_pairs={{1,2},{3,4},{5,6},{2,1},{4,3},{6,5},{9,10},{11,12},{13,14},{10,9},... | collective-permute-start | bytes 294920 | tf_op jit(solution)/shard_map/ppermute | solution.py:422
  20.0 6.1 %collective-permute-start.12 = (f32[4,128,128]{2,1,0:T(8,128)S(1)}, f32[4,128,128]{2,1,0:T(8,128)S(1)}, u32[]{:S(2)}, u32[]{:S(2)}) collective-permute-start(f32[4,128,128]{2,1,0:T(8,128)S(1)} %get-tuple-element.47), channel_id=1, source_target_pairs={{0,8},{8,0},{1,9},{9,1},{2,10},{10,2},{3,11},{11,3},{4,12},{12,4},... | collective-permute-start | bytes 786440 | tf_op jit(solution)/shard_map/ppermute | solution.py:434
  26.9 32.3 %all-to-all-start = ((f32[128,4,128]{2,1,0:T(4,128)}), f32[128,4,128]{2,1,0:T(4,128)S(1)}, u32[]{:S(2)}, u32[]{:S(2)}) async-start(f32[128,4,128]{2,1,0:T(4,128)} %bitcast.9), calls=%async_computation | async-start | bytes 524288 | tf_op jit(solution)/shard_map/all_to_all | solution.py:438
  44.2 22.3 %collective-permute-start.4 = (f32[4,96,128]{2,1,0:T(8,128)S(1)}, f32[4,96,128]{2,1,0:T(8,128)S(1)}, u32[]{:S(2)}, u32[]{:S(2)}) collective-permute-start(f32[4,96,128]{2,1,0:T(8,128)S(1)} %get-tuple-element.36), channel_id=1, source_target_pairs={{0,8},{8,0},{1,9},{9,1},{2,10},{10,2},{3,11},{11,3},{4,12},{12,4},... | collective-permute-start | bytes 589832 | tf_op jit(solution)/shard_map/ppermute | solution.py:417
  44.3 22.3 %collective-permute-start.5 = (f32[4,96,128]{2,1,0:T(8,128)S(1)}, f32[4,96,128]{2,1,0:T(8,128)S(1)}, u32[]{:S(2)}, u32[]{:S(2)}) collective-permute-start(f32[4,96,128]{2,1,0:T(8,128)S(1)} %get-tuple-element.37), channel_id=1, source_target_pairs={{8,16},{24,32},{40,48},{56,64},{72,80},{88,96},{104,112},{120,128}... | collective-permute-start | bytes 589832 | tf_op jit(solution)/shard_map/ppermute | solution.py:422
  60.0 27.5 %all-to-all-start.1 = ((f32[128,4,128]{2,1,0:T(4,128)}), f32[128,4,128]{2,1,0:T(4,128)S(1)}, u32[]{:S(2)}, u32[]{:S(2)}) async-start(f32[128,4,128]{2,1,0:T(4,128)} %bitcast.11), calls=%async_computation.1 | async-start | bytes 524288 | tf_op jit(solution)/shard_map/all_to_all | solution.py:438
  67.6 8.9 %collective-permute-start.6 = (f32[4,96,128]{2,1,0:T(8,128)S(1)}, f32[4,96,128]{2,1,0:T(8,128)S(1)}, u32[]{:S(2)}, u32[]{:S(2)}) collective-permute-start(f32[4,96,128]{2,1,0:T(8,128)S(1)} %get-tuple-element.38), channel_id=1, source_target_pairs={{0,1},{1,0},{2,3},{3,2},{4,5},{5,4},{6,7},{7,6},{8,9},{9,8},{10,11... | collective-permute-start | bytes 589832 | tf_op jit(solution)/shard_map/ppermute | solution.py:417
  69.2 10.4 %collective-permute-start.7 = (f32[4,96,128]{2,1,0:T(8,128)S(1)}, f32[4,96,128]{2,1,0:T(8,128)S(1)}, u32[]{:S(2)}, u32[]{:S(2)}) collective-permute-start(f32[4,96,128]{2,1,0:T(8,128)S(1)} %get-tuple-element.39), channel_id=1, source_target_pairs={{1,2},{3,4},{5,6},{2,1},{4,3},{6,5},{9,10},{11,12},{13,14},{10,9},... | collective-permute-start | bytes 589832 | tf_op jit(solution)/shard_map/ppermute | solution.py:422
  86.7 4.7 %collective-permute-start.8 = (f32[4,96,128]{2,1,0:T(8,128)S(1)}, f32[4,96,128]{2,1,0:T(8,128)S(1)}, u32[]{:S(2)}, u32[]{:S(2)}) collective-permute-start(f32[4,96,128]{2,1,0:T(8,128)S(1)} %get-tuple-element.42), channel_id=1, source_target_pairs={{0,8},{8,0},{1,9},{9,1},{2,10},{10,2},{3,11},{11,3},{4,12},{12,4},... | collective-permute-start | bytes 589832 | tf_op jit(solution)/shard_map/ppermute | solution.py:417
  86.8 4.6 %collective-permute-start.9 = (f32[4,96,128]{2,1,0:T(8,128)S(1)}, f32[4,96,128]{2,1,0:T(8,128)S(1)}, u32[]{:S(2)}, u32[]{:S(2)}) collective-permute-start(f32[4,96,128]{2,1,0:T(8,128)S(1)} %get-tuple-element.43), channel_id=1, source_target_pairs={{8,16},{24,32},{40,48},{56,64},{72,80},{88,96},{104,112},{120,128}... | collective-permute-start | bytes 589832 | tf_op jit(solution)/shard_map/ppermute | solution.py:422
  87.5 16.6 %collective-permute-start.13 = (f32[4,128,128]{2,1,0:T(8,128)S(1)}, f32[4,128,128]{2,1,0:T(8,128)S(1)}, u32[]{:S(2)}, u32[]{:S(2)}) collective-permute-start(f32[4,128,128]{2,1,0:T(8,128)S(1)} %bitcast.29), channel_id=1, source_target_pairs={{0,8},{8,0},{1,9},{9,1},{2,10},{10,2},{3,11},{11,3},{4,12},{12,4},... | collective-permute-start | bytes 786440 | tf_op jit(solution)/shard_map/ppermute | solution.py:434
  92.4 7.3 %collective-permute-start.10 = (f32[4,96,128]{2,1,0:T(8,128)S(1)}, f32[4,96,128]{2,1,0:T(8,128)S(1)}, u32[]{:S(2)}, u32[]{:S(2)}) collective-permute-start(f32[4,96,128]{2,1,0:T(8,128)S(1)} %get-tuple-element.44), channel_id=1, source_target_pairs={{0,1},{1,0},{2,3},{3,2},{4,5},{5,4},{6,7},{7,6},{8,9},{9,8},{10,11... | collective-permute-start | bytes 589832 | tf_op jit(solution)/shard_map/ppermute | solution.py:417
  93.8 10.2 %collective-permute-start.11 = (f32[4,96,128]{2,1,0:T(8,128)S(1)}, f32[4,96,128]{2,1,0:T(8,128)S(1)}, u32[]{:S(2)}, u32[]{:S(2)}) collective-permute-start(f32[4,96,128]{2,1,0:T(8,128)S(1)} %get-tuple-element.45), channel_id=1, source_target_pairs={{1,2},{3,4},{5,6},{2,1},{4,3},{6,5},{9,10},{11,12},{13,14},{10,9},... | collective-permute-start | bytes 589832 | tf_op jit(solution)/shard_map/ppermute | solution.py:422
  110.7 3.2 %collective-permute-start.18 = (f32[4,128,128]{2,1,0:T(8,128)S(1)}, f32[4,128,128]{2,1,0:T(8,128)S(1)}, u32[]{:S(2)}, u32[]{:S(2)}) collective-permute-start(f32[4,128,128]{2,1,0:T(8,128)S(1)} %get-tuple-element.57), channel_id=1, source_target_pairs={{0,8},{8,0},{1,9},{9,1},{2,10},{10,2},{3,11},{11,3},{4,12},{12,4},... | collective-permute-start | bytes 786440 | tf_op jit(solution)/shard_map/ppermute | solution.py:434
  144.8 19.9 %all-to-all-start.3 = ((f32[128,4,128]{2,1,0:T(4,128)}), f32[128,4,128]{2,1,0:T(4,128)S(1)}, u32[]{:S(2)}, u32[]{:S(2)}) async-start(f32[128,4,128]{2,1,0:T(4,128)} %bitcast.16), calls=%async_computation.3 | async-start | bytes 524288 | tf_op jit(solution)/shard_map/all_to_all | solution.py:438
  151.3 13.3 %collective-permute-start.14 = (f32[4,96,128]{2,1,0:T(8,128)S(1)}, f32[4,96,128]{2,1,0:T(8,128)S(1)}, u32[]{:S(2)}, u32[]{:S(2)}) collective-permute-start(f32[4,96,128]{2,1,0:T(8,128)S(1)} %get-tuple-element.51), channel_id=1, source_target_pairs={{0,8},{8,0},{1,9},{9,1},{2,10},{10,2},{3,11},{11,3},{4,12},{12,4},... | collective-permute-start | bytes 589832 | tf_op jit(solution)/shard_map/ppermute | solution.py:417
  151.4 13.2 %collective-permute-start.15 = (f32[4,96,128]{2,1,0:T(8,128)S(1)}, f32[4,96,128]{2,1,0:T(8,128)S(1)}, u32[]{:S(2)}, u32[]{:S(2)}) collective-permute-start(f32[4,96,128]{2,1,0:T(8,128)S(1)} %get-tuple-element.52), channel_id=1, source_target_pairs={{8,16},{24,32},{40,48},{56,64},{72,80},{88,96},{104,112},{120,128}... | collective-permute-start | bytes 589832 | tf_op jit(solution)/shard_map/ppermute | solution.py:422
  164.6 15.2 %collective-permute-start.19 = (f32[4,128,128]{2,1,0:T(8,128)S(1)}, f32[4,128,128]{2,1,0:T(8,128)S(1)}, u32[]{:S(2)}, u32[]{:S(2)}) collective-permute-start(f32[4,128,128]{2,1,0:T(8,128)S(1)} %bitcast.27), channel_id=1, source_target_pairs={{0,8},{8,0},{1,9},{9,1},{2,10},{10,2},{3,11},{11,3},{4,12},{12,4},... | collective-permute-start | bytes 786440 | tf_op jit(solution)/shard_map/ppermute | solution.py:434
  165.7 7.9 %collective-permute-start.16 = (f32[4,96,128]{2,1,0:T(8,128)S(1)}, f32[4,96,128]{2,1,0:T(8,128)S(1)}, u32[]{:S(2)}, u32[]{:S(2)}) collective-permute-start(f32[4,96,128]{2,1,0:T(8,128)S(1)} %get-tuple-element.53), channel_id=1, source_target_pairs={{0,1},{1,0},{2,3},{3,2},{4,5},{5,4},{6,7},{7,6},{8,9},{9,8},{10,11... | collective-permute-start | bytes 589832 | tf_op jit(solution)/shard_map/ppermute | solution.py:417
  166.4 11.6 %collective-permute-start.17 = (f32[4,96,128]{2,1,0:T(8,128)S(1)}, f32[4,96,128]{2,1,0:T(8,128)S(1)}, u32[]{:S(2)}, u32[]{:S(2)}) collective-permute-start(f32[4,96,128]{2,1,0:T(8,128)S(1)} %get-tuple-element.54), channel_id=1, source_target_pairs={{1,2},{3,4},{5,6},{2,1},{4,3},{6,5},{9,10},{11,12},{13,14},{10,9},... | collective-permute-start | bytes 589832 | tf_op jit(solution)/shard_map/ppermute | solution.py:422

commit v4 on v3

--- a/solution.py
+++ b/solution.py
@@ -107,14 +107,30 @@
     return [[fn(pairs[m // 2][m % 2], m) for m in (2 * k, 2 * k + 1)] for k in range(2)]
 
 
+def rows_up(rows, by):
+    groups = rows.reshape(-1, 8, WIN)
+    turned = pltpu.roll(groups, (8 - by) % 8, 1)
+    line = lax.broadcasted_iota(jnp.int32, (WIN // 8, 8, WIN), 1)
+    return jnp.where(line < 8 - by, turned[:-1], turned[1:]).reshape(WIN, WIN)
+
+
+def rows_down(rows, by):
+    groups = rows.reshape(-1, 8, WIN)
+    turned = pltpu.roll(groups, by, 1)
+    zero = jnp.zeros((1, 8, WIN), F32)
+    line = lax.broadcasted_iota(jnp.int32, (WIN // 8 + 1, 8, WIN), 1)
+    first = jnp.concatenate([turned, zero], axis=0)
+    second = jnp.concatenate([zero, turned], axis=0)
+    return jnp.where(line >= by, first, second).reshape(WIN + 8, WIN)
+
+
 def place_window(e_ref, oy, ox, which):
     base = pl.multiple_of(oy // 8 * 8, 8)
-    up = (WIN + 8 - oy % 8) % (WIN + 8)
     back = (WIN - ox) % WIN
     parts = []
     for t in range(2):
         rows = e_ref[which, pl.ds(base, WIN + 8), t * WIN : (t + 1) * WIN]
-        parts.append(pltpu.roll(pltpu.roll(rows, up, 0)[:WIN], back, 1))
+        parts.append(pltpu.roll(rows_up(rows, oy % 8), back, 1))
     first, second = parts
     return jnp.where(lanes((WIN, WIN)) < WIN - ox, first, second)
 
@@ -157,9 +173,17 @@
     return jnp.where(odd, near[a], far[a]), jnp.where(odd, far[a], near[a])
 
 
-def cut_kernel(info, obj, near, far):
-    for a in range(4):
-        by_parity(info[CORE - 6] == 1, (obj[a, :OVL], obj[a, WIN - OVL :]), near, far, a)
+def cut_kernel(info, obj, near, far, sem):
+    edge = WIN - OVL
+    odd = info[CORE - 6]
+    copies = [
+        pltpu.make_async_copy(obj.at[:, pl.ds(pl.multiple_of(start * edge, 8), OVL), :], out, sem.at[i])
+        for i, (start, out) in enumerate(((1 - odd, near), (odd, far)))
+    ]
+    for copy in copies:
+        copy.start()
+    for copy in copies:
+        copy.wait()
 
 
 def halo_kernel(info, obj, row_near, row_far, near, far):
@@ -200,31 +224,26 @@
 
 def place_gradient(info, b, grads, g_ref):
     oy, ox = info[2 * b], info[2 * b + 1]
-    lane = lanes((WIN, WIN))
+    lane = lanes((WIN + 8, WIN))
     base = pl.multiple_of(oy // 8 * 8, 8)
-    gap = jnp.zeros((8, WIN), F32)
     for a in range(4):
         g_ref[a] = jnp.zeros((TALL, 2 * WIN), F32)
-        turned = pltpu.roll(grads[a], ox, 1)
+        turned = rows_down(pltpu.roll(grads[a], ox, 1), oy % 8)
         for t in range(2):
             part = jnp.where(lane >= ox if t == 0 else lane < ox, turned, 0.0)
-            part = pltpu.roll(jnp.concatenate([part, gap], axis=0), oy % 8, 0)
             g_ref[a, pl.ds(base, WIN + 8), t * WIN : (t + 1) * WIN] = part
 
 
-def row_bands(info, rn, rf, a):
-    north, south = (unpack_rows(x) for x in sides(info[CORE] == 1, rn, rf, a))
+def total_gradient(info, g_ref, cols, rows, a):
+    west_east = sides(info[XLOW] == 1, *cols, a)
+    north, south = (unpack_rows(x) for x in sides(info[CORE] == 1, *rows, a))
     gap = jnp.zeros((64, WIN), F32)
-    return [jnp.concatenate([north[t], gap, south[t]], axis=0) for t in range(2)]
-
-
-def total_gradient(info, g_ref, rows, cols, a):
-    west_east = sides(info[XLOW] == 1, *cols, a)
-    bands = row_bands(info, *rows, a)
-    return [
-        g_ref[a, :EXT, t * WIN : (t + 1) * WIN] + unpack_cols(west_east[t]) + bands[t]
-        for t in range(2)
-    ]
+    out = []
+    for t in range(2):
+        bands = jnp.concatenate([north[t], gap, south[t]], axis=0)
+        own = g_ref[a, :EXT, t * WIN : (t + 1) * WIN]
+        out.append(own + unpack_cols(west_east[t]) + bands)
+    return out
 
 
 def pack_extended(e_ref, out):
@@ -239,14 +258,14 @@
     return jnp.where(lane < WIN - OVL, turned[0], turned[1])
 
 
-def update_extended(e_ref, g_ref, info, b, old, grads, rows, cols):
+def update_extended(e_ref, g_ref, info, b, old, grads, cols, rows):
     place_gradient(info, b - 1, grads, g_ref)
     row = lax.broadcasted_iota(jnp.int32, (EXT, WIN), 0)
     lane = lanes((EXT, WIN))
     in_rows = (row >= info[6]) & (row < info[7])
     keep = (in_rows & (lane >= info[8]), in_rows & (lane + WIN < info[9]))
     for a in range(4):
-        grad = total_gradient(info, g_ref, rows, cols, a)
+        grad = total_gradient(info, g_ref, cols, rows, a)
         before = (old[a, :EXT], unpack_cols(old[a, EXT:]))
         for t in range(2):
             value = before[t] - OBJECT_RATE * grad[t]
@@ -283,9 +302,12 @@
         w_ref[a] = grads[a]
     place_gradient(info, b, grads, g_ref)
     for a in range(4):
-        up = pack_rows(g_ref[a, :64, :WIN], g_ref[a, :64, WIN:])
-        down = pack_rows(g_ref[a, 128:EXT, :WIN], g_ref[a, 128:EXT, WIN:])
-        by_parity(info[CORE] == 1, (up, down), near, far, a)
+        first, second = g_ref[a, :EXT, :WIN], g_ref[a, :EXT, WIN:]
+        if b < 2:
+            strips = (pack_cols(first), pack_cols(second))
+        else:
+            strips = (pack_strip(first, 0), pack_strip(second, OVL))
+        by_parity(info[XLOW] == 1, strips, near, far, a)
     return per_mode(chi1, lambda v, m: conj_product(o1, v))
 
 
@@ -322,10 +344,10 @@
     write_halves(info, grads, keep, send)
 
 
-def second_kernel(info, old, grad, rn, rf, cn, cf, probe, tables, kcos, ksin, measured,
+def second_kernel(info, old, grad, cn, cf, rn, rf, probe, tables, kcos, ksin, measured,
                   e_out, w_ref, near, far, held, e_s, g_s, p_s, t_s, k_s, m_s, h_s, sem):
     loads = loads_of(1, probe, tables, kcos, ksin, measured, p_s, t_s, k_s, m_s, sem)
-    update_extended(e_s, g_s, info, 1, old, grad, (rn, rf), (cn, cf))
+    update_extended(e_s, g_s, info, 1, old, grad, (cn, cf), (rn, rf))
     pack_extended(e_s, e_out)
     loads[0].wait()
     grads = step_core(info, 1, e_s, probe_blocks(p_s), loads, k_s, m_s, t_s, g_s, w_ref, near, far)
@@ -337,13 +359,13 @@
     store.wait()
 
 
-def third_kernel(rate, info, old, grad, rn, rf, cn, cf, mine, other,
+def third_kernel(rate, info, old, grad, cn, cf, rn, rf, mine, other,
                  probe, tables, kcos, ksin, measured, held,
                  own, w_ref, near, far, keep, send, p_out, e_s, g_s, p_s, t_s, k_s, m_s, h_s, sem):
     loads = loads_of(2, probe, tables, kcos, ksin, measured, p_s, t_s, k_s, m_s, sem)
     load_held = pltpu.make_async_copy(held, h_s, sem.at[5])
     load_held.start()
-    update_extended(e_s, g_s, info, 2, old, grad, (rn, rf), (cn, cf))
+    update_extended(e_s, g_s, info, 2, old, grad, (cn, cf), (rn, rf))
     for a in range(4):
         own[a] = own_part((e_s[a, :, :WIN], e_s[a, :, WIN:]))
     loads[0].wait()
@@ -361,19 +383,48 @@
         out[4 + i] = probe[4 + i] - rate * jnp.where(first, other[i], mine[i])
 
 
-def middle_kernel(b, info, grad, rn, rf, near, far, g_s):
+def middle_kernel(b, info, grad, cn, cf, near, far, g_s):
     place_gradient(info, b, grad, g_s)
     for a in range(4):
-        bands = row_bands(info, rn, rf, a)
-        strips = [pack_cols(g_s[a, :EXT, t * WIN : (t + 1) * WIN] + bands[t]) for t in range(2)]
-        by_parity(info[XLOW] == 1, strips, near, far, a)
-
-
-def object_kernel(info, own, grad, rn, rf, cn, cf, out, g_s):
+        west_east = [unpack_cols(x) for x in sides(info[XLOW] == 1, cn, cf, a)]
+        full = [g_s[a, :EXT, t * WIN : (t + 1) * WIN] + west_east[t] for t in range(2)]
+        up = pack_rows(full[0][:64], full[1][:64])
+        down = pack_rows(full[0][128:], full[1][128:])
+        by_parity(info[CORE] == 1, (up, down), near, far, a)
+
+
+def pack_strip(column, lane):
+    group = lanes((EXT // 4, WIN)) // OVL
+    out = jnp.zeros((EXT // 4, WIN), F32)
+    for i in range(4):
+        part = pltpu.roll(column[EXT // 4 * i : EXT // 4 * (i + 1)], (OVL * i - lane) % WIN, 1)
+        out = jnp.where(group == i, part, out)
+    return out
+
+
+def unpack_strip(packed, lane):
+    parts = [pltpu.roll(packed, (lane - OVL * i) % WIN, 1) for i in range(4)]
+    column = jnp.concatenate(parts, axis=0)
+    return jnp.where(lanes(column.shape) // OVL == lane // OVL, column, 0.0)
+
+
+def last_middle_kernel(info, grad, cn, cf, near, far, center, g_s):
     place_gradient(info, 2, grad, g_s)
-    for a in range(4):
-        total = total_gradient(info, g_s, (rn, rf), (cn, cf), a)
-        out[a] = own[a] - OBJECT_RATE * own_part(total)
+    lane = lanes((EXT, WIN))
+    for a in range(4):
+        west, east = sides(info[XLOW] == 1, cn, cf, a)
+        turned = [pltpu.roll(g_s[a, :EXT, t * WIN : (t + 1) * WIN], WIN - OVL, 1) for t in range(2)]
+        full = jnp.where(lane < WIN - OVL, turned[0], turned[1])
+        full = full + unpack_strip(west, 0) + unpack_strip(east, WIN - OVL)
+        center[a] = full[OVL : OVL + WIN]
+        by_parity(info[CORE] == 1, (full[:OVL], full[OVL + WIN :]), near, far, a)
+
+
+def object_kernel(info, own, center, rn, rf, out):
+    for a in range(4):
+        north, south = sides(info[CORE] == 1, rn, rf, a)
+        bands = jnp.concatenate([north, jnp.zeros((WIN - 2 * OVL, WIN), F32), south], axis=0)
+        out[a] = own[a] - OBJECT_RATE * (center[a] + bands)
 
 
 SMEM = pl.BlockSpec(memory_space=pltpu.SMEM)
@@ -399,6 +450,8 @@
 
 EXT_SHAPE = (4, EXT + EXT // 2, WIN)
 BAND = (4, EXT // 2, WIN)
+STRIP = (4, EXT // 4, WIN)
+EDGE = (4, OVL, WIN)
 HALF = (4, WIN, WIN)
 PLACE = pltpu.VMEM((4, TALL, 2 * WIN), F32)
 STEP_SCRATCH = (
@@ -456,12 +509,12 @@
 
 
 def exchanged(info, grad, near, far, b):
-    rows = rows_swapped(near, far)
+    cols = cols_swapped(near, far)
     near, far = call(
-        lambda *refs: middle_kernel(b, *refs), [BAND, BAND], info, grad, *rows,
+        lambda *refs: middle_kernel(b, *refs), [BAND, BAND], info, grad, *cols,
         scratch=(PLACE,),
     )
-    return grad, *rows, *cols_swapped(near, far)
+    return grad, *cols, *rows_swapped(near, far)
 
 
 def steps(object_field, probe, kernel_phase, amplitudes, offsets):
@@ -485,7 +538,10 @@
     probe = probe.reshape(2 * MODES, WIN, WIN)
     loads = (probe, tables, kcos, ksin, measured)
 
-    rows = call(cut_kernel, [(4, OVL, WIN)] * 2, edges, obj)
+    rows = call(
+        cut_kernel, [(4, OVL, WIN)] * 2, edges, loads=(obj,),
+        scratch=(pltpu.SemaphoreType.DMA((2,)),),
+    )
     rows = rows_swapped(*rows)
     cols = call(halo_kernel, [(4, 48, WIN)] * 2, info, obj, *rows)
     cols = cols_swapped(*cols)
@@ -505,14 +561,18 @@
     )
     moves = exchanged(info, grad, near, far, 1)
     own, grad, near, far, keep2, send2, probe = call(
-        lambda *refs: third_kernel(rate, *refs), [HALF] + step_outs[1:] + [HALF, HALF, whole],
+        lambda *refs: third_kernel(rate, *refs), [HALF, HALF, STRIP, STRIP, HALF, HALF, whole],
         info, extended, *moves, mine0, other0,
         loads=loads + (held,), scratch=STEP_SCRATCH + HELD + SEMS,
     )
-    moves = exchanged(info, grad, near, far, 2)
+    cols = cols_swapped(near, far)
+    near, far, center = call(
+        last_middle_kernel, [EDGE, EDGE, HALF], info, grad, *cols, scratch=(PLACE,)
+    )
+    rows = rows_swapped(near, far)
     mine = summed_half(keep2, send2)
     other = swap_cores(mine)
-    (obj,) = call(object_kernel, [HALF], info, own, *moves, scratch=(PLACE,), on_chip=False)
+    (obj,) = call(object_kernel, [HALF], info, own, center, *rows, on_chip=False)
     (probe,) = call(
         lambda *refs: update_probe(rate, *refs), [(2 * MODES, WIN, WIN)],
         info, probe, mine, other, on_chip=False,

time: 182 us -> 185 us (1.016)
  the two profiles are of different devices: /device:TPU:8 before, /device:TPU:3 now
where the time goes in v4:
time: 185 us
  starting transfers between devices  65.9 us (36%)
  blocking collectives  45.9 us (25%)
  waiting for transfers between devices  40.4 us (22%)
  Pallas kernels  30.2 us (16%)
    all_to_all x2, blocking collectives, chip_exchange(): return lax.all_to_all(x, CHIPS, 0, 0, tiled=True)  45.9 us
    pallas_call x14, Pallas kernels, call(): pl.pallas_call(kernel, out_shape=[pltpu.VMEM(s, F32) if on_chip else jax....  30.2 us
    ppermute x8, starting transfers between devices, swap_far(): return lax.ppermute(x, axes, pairs + [(j, i) for i, j in pairs])  29.5 us
    ppermute x8, waiting for transfers between devices, swap_far(): return lax.ppermute(x, axes, pairs + [(j, i) for i, j in pairs])  28.3 us
    all_to_all x2, starting transfers between devices, chip_exchange(): return lax.all_to_all(x, CHIPS, 0, 0, tiled=True)  23.2 us
    ppermute x8, starting transfers between devices, swap_near(): return lax.ppermute(x, axis, [(0, 1), (1, 0)])  9.35 us
    all_to_all x2, waiting for transfers between devices, chip_exchange(): return lax.all_to_all(x, CHIPS, 0, 0, tiled=True)  8.07 us
    ppermute x4, starting transfers between devices, swap_cores(): return lax.ppermute(x, 'core', [(0, 1), (1, 0)])  3.84 us
  transfers between devices with their start and end apart: 22, of which 12 were waited for; matrix products, arithmetic and copies ran while one was open for 1% of the time, Pallas kernels for 6%

profile of v4, /device:TPU:3, one launch (start us, length us, event | category | flops | bytes accessed | tf_op | source)
XLA Modules:
  0.0 184.5 jit_solution(12460631607288925747)
XLA Ops:
  0.6 0.0 copy-start
  0.7 0.1 stack.27.info
  0.8 1.4 shard_map.77
  2.2 0.0 copy-start.2
  2.2 0.8 collective-permute-start
  3.0 3.7 %collective-permute-start.1 = (f32[4,32,128]{2,1,0:T(8,128)S(1)}, f32[4,32,128]{2,1,0:T(8,128)S(1)}, u32[]{:S(2)}, u32[]{:S(2)}) collective-permute-start(f32[4,32,128]{2,1,0:T(8,128)S(1)} %get-tuple-element.32), channel_id=1, source_target_pairs={{8,16},{24,32},{40,48},{56,64},{72,80},{88,96},{104,112},{120,128}... | collective-permute-start | bytes 196616 | tf_op jit(solution)/shard_map/ppermute | solution.py:475
  6.6 0.1 copy.9
  6.7 0.1 reshape.43
  6.8 0.1 concatenate.4.info.refs_0_
  6.9 0.0 collective-permute-done.row_near
  6.9 3.1 %collective-permute-done.1.row_far = f32[4,32,128]{2,1,0:T(8,128)S(1)} collective-permute-done((f32[4,32,128]{2,1,0:T(8,128)S(1)}, f32[4,32,128]{2,1,0:T(8,128)S(1)}, u32[]{:S(2)}, u32[]{:S(2)}) %collective-permute-start.1) | collective-permute-done | bytes 65568 | tf_op jit(solution)/shard_map/ppermute | solution.py:475
  10.1 0.8 shard_map.78
  10.8 2.0 %collective-permute-start.2 = (f32[4,48,128]{2,1,0:T(8,128)S(1)}, f32[4,48,128]{2,1,0:T(8,128)S(1)}, u32[]{:S(2)}, u32[]{:S(2)}) collective-permute-start(f32[4,48,128]{2,1,0:T(8,128)S(1)} %get-tuple-element.33), channel_id=1, source_target_pairs={{0,1},{1,0},{2,3},{3,2},{4,5},{5,4},{6,7},{7,6},{8,9},{9,8},{10,11... | collective-permute-start | bytes 294920 | tf_op jit(solution)/shard_map/ppermute | solution.py:470
  12.9 2.4 %collective-permute-start.3 = (f32[4,48,128]{2,1,0:T(8,128)S(1)}, f32[4,48,128]{2,1,0:T(8,128)S(1)}, u32[]{:S(2)}, u32[]{:S(2)}) collective-permute-start(f32[4,48,128]{2,1,0:T(8,128)S(1)} %get-tuple-element.34), channel_id=1, source_target_pairs={{1,2},{3,4},{5,6},{2,1},{4,3},{6,5},{9,10},{11,12},{13,14},{10,9},... | collective-permute-start | bytes 294920 | tf_op jit(solution)/shard_map/ppermute | solution.py:475
  15.3 0.9 fusion
  16.2 0.0 collective-permute-done.2.col_near
  16.2 2.9 %collective-permute-done.3.col_far = f32[4,48,128]{2,1,0:T(8,128)S(1)} collective-permute-done((f32[4,48,128]{2,1,0:T(8,128)S(1)}, f32[4,48,128]{2,1,0:T(8,128)S(1)}, u32[]{:S(2)}, u32[]{:S(2)}) %collective-permute-start.3) | collective-permute-done | bytes 98336 | tf_op jit(solution)/shard_map/ppermute | solution.py:475
  19.1 6.7 %shard_map.79 = (f32[4,288,128]{2,1,0:T(8,128)S(1)}, f32[4,128,128]{2,1,0:T(8,128)S(1)}, f32[4,96,128]{2,1,0:T(8,128)S(1)}, f32[4,96,128]{2,1,0:T(8,128)S(1)}, f...) custom-call(s32[12]{0:T(128)S(1)} %concatenate.4.info.refs_0_, f32[4,128,128]{2,1,0:T(8,128)S(1)} %bitcast.23, ...), custom_call_target="tpu_custom_call" | custom-call | tf_op jit(solution)/shard_map/pallas_call | solution.py:439
  25.8 0.1 collective-permute-start.12
  25.9 1.5 collective-permute-done.12.other
  27.4 0.7 shard_map.83
  28.2 15.8 %all-to-all-start = ((f32[128,4,128]{2,1,0:T(4,128)}), f32[128,4,128]{2,1,0:T(4,128)S(1)}, u32[]{:S(2)}, u32[]{:S(2)}) async-start(f32[128,4,128]{2,1,0:T(4,128)} %bitcast.9), calls=%async_computation | async-start | bytes 524288 | tf_op jit(solution)/shard_map/all_to_all | solution.py:491
  44.0 1.0 collective-permute-start.4
  45.0 3.4 %collective-permute-start.5 = (f32[4,96,128]{2,1,0:T(8,128)S(1)}, f32[4,96,128]{2,1,0:T(8,128)S(1)}, u32[]{:S(2)}, u32[]{:S(2)}) collective-permute-start(f32[4,96,128]{2,1,0:T(8,128)S(1)} %get-tuple-element.38), channel_id=1, source_target_pairs={{1,2},{3,4},{5,6},{2,1},{4,3},{6,5},{9,10},{11,12},{13,14},{10,9},... | collective-permute-start | bytes 589832 | tf_op jit(solution)/shard_map/ppermute | solution.py:475
  48.4 8.1 %all-to-all-done = f32[128,4,128]{2,1,0:T(4,128)S(1)} async-done(((f32[128,4,128]{2,1,0:T(4,128)}), f32[128,4,128]{2,1,0:T(4,128)S(1)}, u32[]{:S(2)}, u32[]{:S(2)}) %all-to-all-start) | async-done | bytes 262176 | tf_op jit(solution)/shard_map/all_to_all | solution.py:491
  56.4 0.8 shard_map.84
  57.2 7.4 %all-to-all-start.1 = ((f32[128,4,128]{2,1,0:T(4,128)}), f32[128,4,128]{2,1,0:T(4,128)S(1)}, u32[]{:S(2)}, u32[]{:S(2)}) async-start(f32[128,4,128]{2,1,0:T(4,128)} %bitcast.11), calls=%async_computation.1 | async-start | bytes 524288 | tf_op jit(solution)/shard_map/all_to_all | solution.py:491
  64.6 0.0 collective-permute-done.4.refs_2_.cn
  64.6 0.0 collective-permute-done.5.refs_3_.cf
  64.7 0.9 shard_map.80
  65.6 2.2 %collective-permute-start.6 = (f32[4,96,128]{2,1,0:T(8,128)S(1)}, f32[4,96,128]{2,1,0:T(8,128)S(1)}, u32[]{:S(2)}, u32[]{:S(2)}) collective-permute-start(f32[4,96,128]{2,1,0:T(8,128)S(1)} %get-tuple-element.39), channel_id=1, source_target_pairs={{0,8},{8,0},{1,9},{9,1},{2,10},{10,2},{3,11},{11,3},{4,12},{12,4},... | collective-permute-start | bytes 589832 | tf_op jit(solution)/shard_map/ppermute | solution.py:470
  67.7 3.8 %collective-permute-start.7 = (f32[4,96,128]{2,1,0:T(8,128)S(1)}, f32[4,96,128]{2,1,0:T(8,128)S(1)}, u32[]{:S(2)}, u32[]{:S(2)}) collective-permute-start(f32[4,96,128]{2,1,0:T(8,128)S(1)} %get-tuple-element.40), channel_id=1, source_target_pairs={{8,16},{24,32},{40,48},{56,64},{72,80},{88,96},{104,112},{120,128}... | collective-permute-start | bytes 589832 | tf_op jit(solution)/shard_map/ppermute | solution.py:475
  71.6 0.0 collective-permute-done.6.rn
  71.6 5.4 %collective-permute-done.7.rf = f32[4,96,128]{2,1,0:T(8,128)S(1)} collective-permute-done((f32[4,96,128]{2,1,0:T(8,128)S(1)}, f32[4,96,128]{2,1,0:T(8,128)S(1)}, u32[]{:S(2)}, u32[]{:S(2)}) %collective-permute-start.7) | collective-permute-done | bytes 196640 | tf_op jit(solution)/shard_map/ppermute | solution.py:475
  77.0 7.0 %shard_map.81 = (f32[4,288,128]{2,1,0:T(8,128)S(1)}, f32[4,128,128]{2,1,0:T(8,128)S(1)}, f32[4,96,128]{2,1,0:T(8,128)S(1)}, f32[4,96,128]{2,1,0:T(8,128)S(1)}, f32[8,128,128]{2,1,0:T(8,128)}) custom-call(s32[12]{0:T(128)S(1)} %concatenate.4.info.refs_0_, f32[4,288,128]{2,1,0:T(8,128)S(1)} %get-tuple-element.35.old, ...), custom_call_target="tpu_custom_call" | custom-call | tf_op jit(solution)/shard_map/pallas_call | solution.py:439
  84.0 0.9 collective-permute-start.8
  84.9 3.4 %collective-permute-start.9 = (f32[4,96,128]{2,1,0:T(8,128)S(1)}, f32[4,96,128]{2,1,0:T(8,128)S(1)}, u32[]{:S(2)}, u32[]{:S(2)}) collective-permute-start(f32[4,96,128]{2,1,0:T(8,128)S(1)} %get-tuple-element.44), channel_id=1, source_target_pairs={{1,2},{3,4},{5,6},{2,1},{4,3},{6,5},{9,10},{11,12},{13,14},{10,9},... | collective-permute-start | bytes 589832 | tf_op jit(solution)/shard_map/ppermute | solution.py:475
  88.3 0.0 all-to-all-done.1
  88.3 0.1 collective-permute-start.13
  88.4 0.1 collective-permute-done.8.refs_2_.refs_3_
  88.6 3.6 %collective-permute-done.9.refs_3_.refs_4_ = f32[4,96,128]{2,1,0:T(8,128)S(1)} collective-permute-done((f32[4,96,128]{2,1,0:T(8,128)S(1)}, f32[4,96,128]{2,1,0:T(8,128)S(1)}, u32[]{:S(2)}, u32[]{:S(2)}) %collective-permute-start.9) | collective-permute-done | bytes 196640 | tf_op jit(solution)/shard_map/ppermute | solution.py:475
  92.2 0.9 shard_map.82
  93.1 0.1 collective-permute-start.10
  93.2 8.3 %collective-permute-start.11 = (f32[4,96,128]{2,1,0:T(8,128)S(1)}, f32[4,96,128]{2,1,0:T(8,128)S(1)}, u32[]{:S(2)}, u32[]{:S(2)}) collective-permute-start(f32[4,96,128]{2,1,0:T(8,128)S(1)} %get-tuple-element.46), channel_id=1, source_target_pairs={{8,16},{24,32},{40,48},{56,64},{72,80},{88,96},{104,112},{120,128}... | collective-permute-start | bytes 589832 | tf_op jit(solution)/shard_map/ppermute | solution.py:475
  101.4 0.0 collective-permute-done.10.refs_5_
  101.5 4.7 %collective-permute-done.11.refs_6_ = f32[4,96,128]{2,1,0:T(8,128)S(1)} collective-permute-done((f32[4,96,128]{2,1,0:T(8,128)S(1)}, f32[4,96,128]{2,1,0:T(8,128)S(1)}, u32[]{:S(2)}, u32[]{:S(2)}) %collective-permute-start.11) | collective-permute-done | bytes 196640 | tf_op jit(solution)/shard_map/ppermute | solution.py:475
  106.2 7.1 %shard_map.85 = (f32[4,128,128]{2,1,0:T(8,128)S(1)}, f32[4,128,128]{2,1,0:T(8,128)S(1)}, f32[4,48,128]{2,1,0:T(8,128)S(1)}, f32[4,48,128]{2,1,0:T(8,128)S(1)}, f...) custom-call(s32[12]{0:T(128)S(1)} %concatenate.4.info.refs_0_, ...), custom_call_target="tpu_custom_call" | custom-call | tf_op jit(solution)/shard_map/pallas_call | solution.py:439
  113.3 0.1 collective-permute-start.18
  113.4 1.5 collective-permute-done.18.other
  114.9 27.2 %all_to_all.20 = f32[128,4,128]{2,1,0:T(4,128)S(1)} all-to-all(f32[128,4,128]{2,1,0:T(4,128)S(1)} %bitcast.24), channel_id=1, replica_groups=mesh['z'=8,'xh'=2,'core'=2,'y'=4,'xl'=2] {'z','xh','y','xl'}, dimensions={0} | all-to-all | bytes 524288 | tf_op jit(solution)/shard_map/all_to_all | solution.py:491
  142.1 0.1 shard_map.89
  142.2 18.7 %all_to_all.21 = f32[128,4,128]{2,1,0:T(4,128)S(1)} all-to-all(f32[128,4,128]{2,1,0:T(4,128)S(1)} %bitcast.27), channel_id=1, replica_groups=mesh['z'=8,'xh'=2,'core'=2,'y'=4,'xl'=2] {'z','xh','y','xl'}, dimensions={0} | all-to-all | bytes 524288 | tf_op jit(solution)/shard_map/all_to_all | solution.py:491
  160.9 3.6 %collective-permute-start.19 = (f32[4,128,128]{2,1,0:T(8,128)S(1)}, f32[4,128,128]{2,1,0:T(8,128)S(1)}, u32[]{:S(2)}, u32[]{:S(2)}) collective-permute-start(f32[4,128,128]{2,1,0:T(8,128)S(1)} %bitcast.28), channel_id=1, source_target_pairs={{0,8},{8,0},{1,9},{9,1},{2,10},{10,2},{3,11},{11,3},{4,12},{12,4},... | collective-permute-start | bytes 786440 | tf_op jit(solution)/shard_map/ppermute | solution.py:487
  164.4 1.1 collective-permute-start.14
  165.6 2.4 %collective-permute-start.15 = (f32[4,48,128]{2,1,0:T(8,128)S(1)}, f32[4,48,128]{2,1,0:T(8,128)S(1)}, u32[]{:S(2)}, u32[]{:S(2)}) collective-permute-start(f32[4,48,128]{2,1,0:T(8,128)S(1)} %get-tuple-element.53), channel_id=1, source_target_pairs={{1,2},{3,4},{5,6},{2,1},{4,3},{6,5},{9,10},{11,12},{13,14},{10,9},... | collective-permute-start | bytes 294920 | tf_op jit(solution)/shard_map/ppermute | solution.py:475
  168.0 0.8 collective-permute-done.14.cn
  168.8 3.6 %collective-permute-done.15.cf = f32[4,48,128]{2,1,0:T(8,128)S(1)} collective-permute-done((f32[4,48,128]{2,1,0:T(8,128)S(1)}, f32[4,48,128]{2,1,0:T(8,128)S(1)}, u32[]{:S(2)}, u32[]{:S(2)}) %collective-permute-start.15) | collective-permute-done | bytes 98336 | tf_op jit(solution)/shard_map/ppermute | solution.py:475
  172.4 1.1 shard_map.86
  173.5 1.2 collective-permute-start.16
  174.8 2.1 %collective-permute-start.17 = (f32[4,32,128]{2,1,0:T(8,128)S(1)}, f32[4,32,128]{2,1,0:T(8,128)S(1)}, u32[]{:S(2)}, u32[]{:S(2)}) collective-permute-start(f32[4,32,128]{2,1,0:T(8,128)S(1)} %get-tuple-element.56), channel_id=1, source_target_pairs={{8,16},{24,32},{40,48},{56,64},{72,80},{88,96},{104,112},{120,128}... | collective-permute-start | bytes 196616 | tf_op jit(solution)/shard_map/ppermute | solution.py:475
  176.9 4.9 %collective-permute-done.17.rf = f32[4,32,128]{2,1,0:T(8,128)S(1)} collective-permute-done((f32[4,32,128]{2,1,0:T(8,128)S(1)}, f32[4,32,128]{2,1,0:T(8,128)S(1)}, u32[]{:S(2)}, u32[]{:S(2)}) %collective-permute-start.17) | collective-permute-done | bytes 65568 | tf_op jit(solution)/shard_map/ppermute | solution.py:475
  181.8 1.3 shard_map.87
  183.1 0.0 collective-permute-done.19.refs_3_
  183.1 1.4 shard_map.90
  (7 shorter events, 0.0 us)
Async XLA Ops:
  0.6 9.4 %copy-start = (f32[2,2,128,128]{3,2,1,0:T(8,128)S(1)}, f32[2,2,128,128]{3,2,1,0:T(8,128)}, u32[]{:S(2)}) copy-start(f32[2,2,128,128]{3,2,1,0:T(8,128)} %param.6) | copy-start | bytes 786436
  2.2 4.4 %copy-start.2 = (s32[3,1,1,2]{0,3,2,1:T(2,128)S(1)}, s32[3,1,1,2]{0,3,2,1:T(2,128)}, u32[]{:S(2)}) copy-start(s32[3,1,1,2]{0,3,2,1:T(2,128)} %param.10) | copy-start | bytes 76
  2.2 4.7 %collective-permute-start = (f32[4,32,128]{2,1,0:T(8,128)S(1)}, f32[4,32,128]{2,1,0:T(8,128)S(1)}, u32[]{:S(2)}, u32[]{:S(2)}) collective-permute-start(f32[4,32,128]{2,1,0:T(8,128)S(1)} %get-tuple-element.31), channel_id=1, source_target_pairs={{0,8},{8,0},{1,9},{9,1},{2,10},{10,2},{3,11},{11,3},{4,12},{12,4},... | collective-permute-start | bytes 196616 | tf_op jit(solution)/shard_map/ppermute | solution.py:470
  3.0 7.1 %collective-permute-start.1 = (f32[4,32,128]{2,1,0:T(8,128)S(1)}, f32[4,32,128]{2,1,0:T(8,128)S(1)}, u32[]{:S(2)}, u32[]{:S(2)}) collective-permute-start(f32[4,32,128]{2,1,0:T(8,128)S(1)} %get-tuple-element.32), channel_id=1, source_target_pairs={{8,16},{24,32},{40,48},{56,64},{72,80},{88,96},{104,112},{120,128}... | collective-permute-start | bytes 196616 | tf_op jit(solution)/shard_map/ppermute | solution.py:475
  6.9 8.4 %copy-start.1 = (f32[128,128]{1,0:T(8,128)S(1)}, f32[128,128]{1,0:T(8,128)}, u32[]{:S(2)}) copy-start(f32[128,128]{1,0:T(8,128)} %param.8) | copy-start | bytes 196612
  10.8 5.4 %collective-permute-start.2 = (f32[4,48,128]{2,1,0:T(8,128)S(1)}, f32[4,48,128]{2,1,0:T(8,128)S(1)}, u32[]{:S(2)}, u32[]{:S(2)}) collective-permute-start(f32[4,48,128]{2,1,0:T(8,128)S(1)} %get-tuple-element.33), channel_id=1, source_target_pairs={{0,1},{1,0},{2,3},{3,2},{4,5},{5,4},{6,7},{7,6},{8,9},{9,8},{10,11... | collective-permute-start | bytes 294920 | tf_op jit(solution)/shard_map/ppermute | solution.py:470
  12.9 6.2 %collective-permute-start.3 = (f32[4,48,128]{2,1,0:T(8,128)S(1)}, f32[4,48,128]{2,1,0:T(8,128)S(1)}, u32[]{:S(2)}, u32[]{:S(2)}) collective-permute-start(f32[4,48,128]{2,1,0:T(8,128)S(1)} %get-tuple-element.34), channel_id=1, source_target_pairs={{1,2},{3,4},{5,6},{2,1},{4,3},{6,5},{9,10},{11,12},{13,14},{10,9},... | collective-permute-start | bytes 294920 | tf_op jit(solution)/shard_map/ppermute | solution.py:475
  25.8 1.6 collective-permute-start.12
  28.2 28.3 %all-to-all-start = ((f32[128,4,128]{2,1,0:T(4,128)}), f32[128,4,128]{2,1,0:T(4,128)S(1)}, u32[]{:S(2)}, u32[]{:S(2)}) async-start(f32[128,4,128]{2,1,0:T(4,128)} %bitcast.9), calls=%async_computation | async-start | bytes 524288 | tf_op jit(solution)/shard_map/all_to_all | solution.py:491
  44.0 20.6 %collective-permute-start.4 = (f32[4,96,128]{2,1,0:T(8,128)S(1)}, f32[4,96,128]{2,1,0:T(8,128)S(1)}, u32[]{:S(2)}, u32[]{:S(2)}) collective-permute-start(f32[4,96,128]{2,1,0:T(8,128)S(1)} %get-tuple-element.37), channel_id=1, source_target_pairs={{0,1},{1,0},{2,3},{3,2},{4,5},{5,4},{6,7},{7,6},{8,9},{9,8},{10,11... | collective-permute-start | bytes 589832 | tf_op jit(solution)/shard_map/ppermute | solution.py:470
  45.0 19.7 %collective-permute-start.5 = (f32[4,96,128]{2,1,0:T(8,128)S(1)}, f32[4,96,128]{2,1,0:T(8,128)S(1)}, u32[]{:S(2)}, u32[]{:S(2)}) collective-permute-start(f32[4,96,128]{2,1,0:T(8,128)S(1)} %get-tuple-element.38), channel_id=1, source_target_pairs={{1,2},{3,4},{5,6},{2,1},{4,3},{6,5},{9,10},{11,12},{13,14},{10,9},... | collective-permute-start | bytes 589832 | tf_op jit(solution)/shard_map/ppermute | solution.py:475
  57.2 31.1 %all-to-all-start.1 = ((f32[128,4,128]{2,1,0:T(4,128)}), f32[128,4,128]{2,1,0:T(4,128)S(1)}, u32[]{:S(2)}, u32[]{:S(2)}) async-start(f32[128,4,128]{2,1,0:T(4,128)} %bitcast.11), calls=%async_computation.1 | async-start | bytes 524288 | tf_op jit(solution)/shard_map/all_to_all | solution.py:491
  65.6 6.0 %collective-permute-start.6 = (f32[4,96,128]{2,1,0:T(8,128)S(1)}, f32[4,96,128]{2,1,0:T(8,128)S(1)}, u32[]{:S(2)}, u32[]{:S(2)}) collective-permute-start(f32[4,96,128]{2,1,0:T(8,128)S(1)} %get-tuple-element.39), channel_id=1, source_target_pairs={{0,8},{8,0},{1,9},{9,1},{2,10},{10,2},{3,11},{11,3},{4,12},{12,4},... | collective-permute-start | bytes 589832 | tf_op jit(solution)/shard_map/ppermute | solution.py:470
  67.7 9.2 %collective-permute-start.7 = (f32[4,96,128]{2,1,0:T(8,128)S(1)}, f32[4,96,128]{2,1,0:T(8,128)S(1)}, u32[]{:S(2)}, u32[]{:S(2)}) collective-permute-start(f32[4,96,128]{2,1,0:T(8,128)S(1)} %get-tuple-element.40), channel_id=1, source_target_pairs={{8,16},{24,32},{40,48},{56,64},{72,80},{88,96},{104,112},{120,128}... | collective-permute-start | bytes 589832 | tf_op jit(solution)/shard_map/ppermute | solution.py:475
  84.0 4.6 %collective-permute-start.8 = (f32[4,96,128]{2,1,0:T(8,128)S(1)}, f32[4,96,128]{2,1,0:T(8,128)S(1)}, u32[]{:S(2)}, u32[]{:S(2)}) collective-permute-start(f32[4,96,128]{2,1,0:T(8,128)S(1)} %get-tuple-element.43), channel_id=1, source_target_pairs={{0,1},{1,0},{2,3},{3,2},{4,5},{5,4},{6,7},{7,6},{8,9},{9,8},{10,11... | collective-permute-start | bytes 589832 | tf_op jit(solution)/shard_map/ppermute | solution.py:470
  84.9 7.3 %collective-permute-start.9 = (f32[4,96,128]{2,1,0:T(8,128)S(1)}, f32[4,96,128]{2,1,0:T(8,128)S(1)}, u32[]{:S(2)}, u32[]{:S(2)}) collective-permute-start(f32[4,96,128]{2,1,0:T(8,128)S(1)} %get-tuple-element.44), channel_id=1, source_target_pairs={{1,2},{3,4},{5,6},{2,1},{4,3},{6,5},{9,10},{11,12},{13,14},{10,9},... | collective-permute-start | bytes 589832 | tf_op jit(solution)/shard_map/ppermute | solution.py:475
  88.3 17.8 %collective-permute-start.13 = (f32[4,128,128]{2,1,0:T(8,128)S(1)}, f32[4,128,128]{2,1,0:T(8,128)S(1)}, u32[]{:S(2)}, u32[]{:S(2)}) collective-permute-start(f32[4,128,128]{2,1,0:T(8,128)S(1)} %bitcast.30), channel_id=1, source_target_pairs={{0,8},{8,0},{1,9},{9,1},{2,10},{10,2},{3,11},{11,3},{4,12},{12,4},... | collective-permute-start | bytes 786440 | tf_op jit(solution)/shard_map/ppermute | solution.py:487
  93.1 8.4 %collective-permute-start.10 = (f32[4,96,128]{2,1,0:T(8,128)S(1)}, f32[4,96,128]{2,1,0:T(8,128)S(1)}, u32[]{:S(2)}, u32[]{:S(2)}) collective-permute-start(f32[4,96,128]{2,1,0:T(8,128)S(1)} %get-tuple-element.45), channel_id=1, source_target_pairs={{0,8},{8,0},{1,9},{9,1},{2,10},{10,2},{3,11},{11,3},{4,12},{12,4},... | collective-permute-start | bytes 589832 | tf_op jit(solution)/shard_map/ppermute | solution.py:470
  93.2 13.0 %collective-permute-start.11 = (f32[4,96,128]{2,1,0:T(8,128)S(1)}, f32[4,96,128]{2,1,0:T(8,128)S(1)}, u32[]{:S(2)}, u32[]{:S(2)}) collective-permute-start(f32[4,96,128]{2,1,0:T(8,128)S(1)} %get-tuple-element.46), channel_id=1, source_target_pairs={{8,16},{24,32},{40,48},{56,64},{72,80},{88,96},{104,112},{120,128}... | collective-permute-start | bytes 589832 | tf_op jit(solution)/shard_map/ppermute | solution.py:475
  113.3 1.6 collective-permute-start.18
  160.9 22.2 %collective-permute-start.19 = (f32[4,128,128]{2,1,0:T(8,128)S(1)}, f32[4,128,128]{2,1,0:T(8,128)S(1)}, u32[]{:S(2)}, u32[]{:S(2)}) collective-permute-start(f32[4,128,128]{2,1,0:T(8,128)S(1)} %bitcast.28), channel_id=1, source_target_pairs={{0,8},{8,0},{1,9},{9,1},{2,10},{10,2},{3,11},{11,3},{4,12},{12,4},... | collective-permute-start | bytes 786440 | tf_op jit(solution)/shard_map/ppermute | solution.py:487
  164.4 4.3 %collective-permute-start.14 = (f32[4,48,128]{2,1,0:T(8,128)S(1)}, f32[4,48,128]{2,1,0:T(8,128)S(1)}, u32[]{:S(2)}, u32[]{:S(2)}) collective-permute-start(f32[4,48,128]{2,1,0:T(8,128)S(1)} %get-tuple-element.52), channel_id=1, source_target_pairs={{0,1},{1,0},{2,3},{3,2},{4,5},{5,4},{6,7},{7,6},{8,9},{9,8},{10,11... | collective-permute-start | bytes 294920 | tf_op jit(solution)/shard_map/ppermute | solution.py:470
  165.6 6.8 %collective-permute-start.15 = (f32[4,48,128]{2,1,0:T(8,128)S(1)}, f32[4,48,128]{2,1,0:T(8,128)S(1)}, u32[]{:S(2)}, u32[]{:S(2)}) collective-permute-start(f32[4,48,128]{2,1,0:T(8,128)S(1)} %get-tuple-element.53), channel_id=1, source_target_pairs={{1,2},{3,4},{5,6},{2,1},{4,3},{6,5},{9,10},{11,12},{13,14},{10,9},... | collective-permute-start | bytes 294920 | tf_op jit(solution)/shard_map/ppermute | solution.py:475
  173.5 3.4 %collective-permute-start.16 = (f32[4,32,128]{2,1,0:T(8,128)S(1)}, f32[4,32,128]{2,1,0:T(8,128)S(1)}, u32[]{:S(2)}, u32[]{:S(2)}) collective-permute-start(f32[4,32,128]{2,1,0:T(8,128)S(1)} %get-tuple-element.55), channel_id=1, source_target_pairs={{0,8},{8,0},{1,9},{9,1},{2,10},{10,2},{3,11},{11,3},{4,12},{12,4},... | collective-permute-start | bytes 196616 | tf_op jit(solution)/shard_map/ppermute | solution.py:470
  174.8 7.1 %collective-permute-start.17 = (f32[4,32,128]{2,1,0:T(8,128)S(1)}, f32[4,32,128]{2,1,0:T(8,128)S(1)}, u32[]{:S(2)}, u32[]{:S(2)}) collective-permute-start(f32[4,32,128]{2,1,0:T(8,128)S(1)} %get-tuple-element.56), channel_id=1, source_target_pairs={{8,16},{24,32},{40,48},{56,64},{72,80},{88,96},{104,112},{120,128}... | collective-permute-start | bytes 196616 | tf_op jit(solution)/shard_map/ppermute | solution.py:475

commit v5 on v4

--- a/solution.py
+++ b/solution.py
@@ -171,19 +171,6 @@
 
 def sides(odd, near, far, a):
     return jnp.where(odd, near[a], far[a]), jnp.where(odd, far[a], near[a])
-
-
-def cut_kernel(info, obj, near, far, sem):
-    edge = WIN - OVL
-    odd = info[CORE - 6]
-    copies = [
-        pltpu.make_async_copy(obj.at[:, pl.ds(pl.multiple_of(start * edge, 8), OVL), :], out, sem.at[i])
-        for i, (start, out) in enumerate(((1 - odd, near), (odd, far)))
-    ]
-    for copy in copies:
-        copy.start()
-    for copy in copies:
-        copy.wait()
 
 
 def halo_kernel(info, obj, row_near, row_far, near, far):
@@ -538,10 +525,8 @@
     probe = probe.reshape(2 * MODES, WIN, WIN)
     loads = (probe, tables, kcos, ksin, measured)
 
-    rows = call(
-        cut_kernel, [(4, OVL, WIN)] * 2, edges, loads=(obj,),
-        scratch=(pltpu.SemaphoreType.DMA((2,)),),
-    )
+    top, bottom = obj[:, :OVL], obj[:, WIN - OVL :]
+    rows = jnp.where(core == 1, top, bottom), jnp.where(core == 1, bottom, top)
     rows = rows_swapped(*rows)
     cols = call(halo_kernel, [(4, 48, WIN)] * 2, info, obj, *rows)
     cols = cols_swapped(*cols)
@@ -573,10 +558,8 @@
     mine = summed_half(keep2, send2)
     other = swap_cores(mine)
     (obj,) = call(object_kernel, [HALF], info, own, center, *rows, on_chip=False)
-    (probe,) = call(
-        lambda *refs: update_probe(rate, *refs), [(2 * MODES, WIN, WIN)],
-        info, probe, mine, other, on_chip=False,
-    )
+    own_half = jnp.arange(2).reshape(2, 1, 1, 1) == core
+    probe = probe.reshape(2, *HALF) - rate * jnp.where(own_half, mine, other)
     return obj.reshape(2, 2, WIN, WIN), probe.reshape(MODES, 2, WIN, WIN)
 
 

time: 185 us -> 184 us (level)
  Pallas kernels: 30.2 us -> 27.4 us
  waiting for transfers between devices: 40.4 us -> 37.7 us
  other arithmetic: 0 us -> 1.87 us
    pallas_call x14 -> x12, Pallas kernels: 30.2 us -> 27.4 us  [call(): pl.pallas_call(kernel, out_shape=[pltpu.VMEM(s, F32) if on_chip else jax....]
    ppermute x8, starting transfers between devices: 9.35 us -> 7.02 us  [swap_near(): return lax.ppermute(x, axis, [(0, 1), (1, 0)])]
    ppermute x8, starting transfers between devices: 29.5 us -> 31.8 us  [swap_far(): return lax.ppermute(x, axes, pairs + [(j, i) for i, j in pairs])]
    ppermute x8, waiting for transfers between devices: 28.3 us -> 26 us  [swap_far(): return lax.ppermute(x, axes, pairs + [(j, i) for i, j in pairs])]
  transfers between devices with their start and end apart: 22 -> 22, of which waited for: 12 -> 12; matrix products, arithmetic and copies ran while one was open for 1% -> 1% of each run, Pallas kernels for 6% -> 7%
where the time goes in v5:
time: 184 us; the launch traced here: 183 us
  starting transfers between devices  67.2 us (37%)
  blocking collectives  45.9 us (25%)
  waiting for transfers between devices  37.7 us (20%)
  Pallas kernels  27.4 us (15%)
  local copies, waits for them, and re-layouts  2.06 us (1%)
  other arithmetic  1.87 us (1%)
    all_to_all x2, blocking collectives, chip_exchange(): return lax.all_to_all(x, CHIPS, 0, 0, tiled=True)  45.9 us
    ppermute x8, starting transfers between devices, swap_far(): return lax.ppermute(x, axes, pairs + [(j, i) for i, j in pairs])  31.8 us
    pallas_call x12, Pallas kernels, call(): pl.pallas_call(kernel, out_shape=[pltpu.VMEM(s, F32) if on_chip else jax....  27.4 us
    ppermute x8, waiting for transfers between devices, swap_far(): return lax.ppermute(x, axes, pairs + [(j, i) for i, j in pairs])  26 us
    all_to_all x2, starting transfers between devices, chip_exchange(): return lax.all_to_all(x, CHIPS, 0, 0, tiled=True)  23.8 us
    all_to_all x2, waiting for transfers between devices, chip_exchange(): return lax.all_to_all(x, CHIPS, 0, 0, tiled=True)  8.07 us
    ppermute x8, starting transfers between devices, swap_near(): return lax.ppermute(x, axis, [(0, 1), (1, 0)])  7.02 us
    ppermute x4, starting transfers between devices, swap_cores(): return lax.ppermute(x, 'core', [(0, 1), (1, 0)])  4.59 us
  transfers between devices with their start and end apart: 22, of which 12 were waited for; matrix products, arithmetic and copies ran while one was open for 1% of the time, Pallas kernels for 7%

profile of v5, /device:TPU:3, one launch (start us, length us, event | category | flops | bytes accessed | tf_op | source)
XLA Modules:
  0.0 183.1 jit_solution(16067031095787000457)
XLA Ops:
  0.6 0.9 slice_select_fusion
  1.6 4.3 %collective-permute-start.1 = (f32[4,32,128]{2,1,0:T(8,128)S(1)}, f32[4,32,128]{2,1,0:T(8,128)S(1)}, u32[]{:S(2)}, u32[]{:S(2)}) collective-permute-start(f32[4,32,128]{2,1,0:T(8,128)S(1)} %get-tuple-element.56), channel_id=1, source_target_pairs={{8,16},{24,32},{40,48},{56,64},{72,80},{88,96},{104,112},{120,128}... | collective-permute-start | bytes 196616 | tf_op jit(solution)/shard_map/ppermute | solution.py:462
  5.9 0.1 collective-permute-start
  6.0 0.0 copy-start.2
  6.0 0.7 copy-done.2
  6.7 0.1 copy.9
  6.8 0.1 reshape.54
  6.9 0.1 concatenate.3.info.refs_0_
  7.0 1.7 collective-permute-done.1.row_far
  8.7 0.0 collective-permute-done.row_near
  8.7 0.8 shard_map.77
  9.4 0.4 collective-permute-start.2
  9.8 4.1 %collective-permute-start.3 = (f32[4,48,128]{2,1,0:T(8,128)S(1)}, f32[4,48,128]{2,1,0:T(8,128)S(1)}, u32[]{:S(2)}, u32[]{:S(2)}) collective-permute-start(f32[4,48,128]{2,1,0:T(8,128)S(1)} %get-tuple-element.30), channel_id=1, source_target_pairs={{1,2},{3,4},{5,6},{2,1},{4,3},{6,5},{9,10},{11,12},{13,14},{10,9},... | collective-permute-start | bytes 294920 | tf_op jit(solution)/shard_map/ppermute | solution.py:462
  13.9 0.9 fusion
  14.8 0.0 collective-permute-done.2.col_near
  14.8 2.3 %collective-permute-done.3.col_far = f32[4,48,128]{2,1,0:T(8,128)S(1)} collective-permute-done((f32[4,48,128]{2,1,0:T(8,128)S(1)}, f32[4,48,128]{2,1,0:T(8,128)S(1)}, u32[]{:S(2)}, u32[]{:S(2)}) %collective-permute-start.3) | collective-permute-done | bytes 98336 | tf_op jit(solution)/shard_map/ppermute | solution.py:462
  17.1 6.7 %shard_map.78 = (f32[4,288,128]{2,1,0:T(8,128)S(1)}, f32[4,128,128]{2,1,0:T(8,128)S(1)}, f32[4,96,128]{2,1,0:T(8,128)S(1)}, f32[4,96,128]{2,1,0:T(8,128)S(1)}, f...) custom-call(s32[12]{0:T(128)S(1)} %concatenate.3.info.refs_0_, f32[4,128,128]{2,1,0:T(8,128)S(1)} %bitcast.25, ...), custom_call_target="tpu_custom_call" | custom-call | tf_op jit(solution)/shard_map/pallas_call | solution.py:426
  23.8 0.9 collective-permute-start.12
  24.6 1.2 collective-permute-done.12.other
  25.8 0.7 shard_map.82
  26.5 16.4 %all-to-all-start = ((f32[128,4,128]{2,1,0:T(4,128)}), f32[128,4,128]{2,1,0:T(4,128)S(1)}, u32[]{:S(2)}, u32[]{:S(2)}) async-start(f32[128,4,128]{2,1,0:T(4,128)} %bitcast.9), calls=%async_computation | async-start | bytes 524288 | tf_op jit(solution)/shard_map/all_to_all | solution.py:478
  42.9 1.0 collective-permute-start.4
  43.9 3.4 %collective-permute-start.5 = (f32[4,96,128]{2,1,0:T(8,128)S(1)}, f32[4,96,128]{2,1,0:T(8,128)S(1)}, u32[]{:S(2)}, u32[]{:S(2)}) collective-permute-start(f32[4,96,128]{2,1,0:T(8,128)S(1)} %get-tuple-element.34), channel_id=1, source_target_pairs={{1,2},{3,4},{5,6},{2,1},{4,3},{6,5},{9,10},{11,12},{13,14},{10,9},... | collective-permute-start | bytes 589832 | tf_op jit(solution)/shard_map/ppermute | solution.py:462
  47.3 8.1 %all-to-all-done = f32[128,4,128]{2,1,0:T(4,128)S(1)} async-done(((f32[128,4,128]{2,1,0:T(4,128)}), f32[128,4,128]{2,1,0:T(4,128)S(1)}, u32[]{:S(2)}, u32[]{:S(2)}) %all-to-all-start) | async-done | bytes 262176 | tf_op jit(solution)/shard_map/all_to_all | solution.py:478
  55.3 0.8 shard_map.83
  56.1 7.4 %all-to-all-start.1 = ((f32[128,4,128]{2,1,0:T(4,128)}), f32[128,4,128]{2,1,0:T(4,128)S(1)}, u32[]{:S(2)}, u32[]{:S(2)}) async-start(f32[128,4,128]{2,1,0:T(4,128)} %bitcast.11), calls=%async_computation.1 | async-start | bytes 524288 | tf_op jit(solution)/shard_map/all_to_all | solution.py:478
  63.5 0.0 collective-permute-done.4.refs_2_.cn
  63.5 0.0 collective-permute-done.5.refs_3_.cf
  63.6 0.9 shard_map.79
  64.5 2.2 %collective-permute-start.6 = (f32[4,96,128]{2,1,0:T(8,128)S(1)}, f32[4,96,128]{2,1,0:T(8,128)S(1)}, u32[]{:S(2)}, u32[]{:S(2)}) collective-permute-start(f32[4,96,128]{2,1,0:T(8,128)S(1)} %get-tuple-element.35), channel_id=1, source_target_pairs={{0,8},{8,0},{1,9},{9,1},{2,10},{10,2},{3,11},{11,3},{4,12},{12,4},... | collective-permute-start | bytes 589832 | tf_op jit(solution)/shard_map/ppermute | solution.py:457
  66.6 3.8 %collective-permute-start.7 = (f32[4,96,128]{2,1,0:T(8,128)S(1)}, f32[4,96,128]{2,1,0:T(8,128)S(1)}, u32[]{:S(2)}, u32[]{:S(2)}) collective-permute-start(f32[4,96,128]{2,1,0:T(8,128)S(1)} %get-tuple-element.36), channel_id=1, source_target_pairs={{8,16},{24,32},{40,48},{56,64},{72,80},{88,96},{104,112},{120,128}... | collective-permute-start | bytes 589832 | tf_op jit(solution)/shard_map/ppermute | solution.py:462
  70.5 0.0 collective-permute-done.6.rn
  70.5 5.4 %collective-permute-done.7.rf = f32[4,96,128]{2,1,0:T(8,128)S(1)} collective-permute-done((f32[4,96,128]{2,1,0:T(8,128)S(1)}, f32[4,96,128]{2,1,0:T(8,128)S(1)}, u32[]{:S(2)}, u32[]{:S(2)}) %collective-permute-start.7) | collective-permute-done | bytes 196640 | tf_op jit(solution)/shard_map/ppermute | solution.py:462
  75.9 7.0 %shard_map.80 = (f32[4,288,128]{2,1,0:T(8,128)S(1)}, f32[4,128,128]{2,1,0:T(8,128)S(1)}, f32[4,96,128]{2,1,0:T(8,128)S(1)}, f32[4,96,128]{2,1,0:T(8,128)S(1)}, f32[8,128,128]{2,1,0:T(8,128)}) custom-call(s32[12]{0:T(128)S(1)} %concatenate.3.info.refs_0_, f32[4,288,128]{2,1,0:T(8,128)S(1)} %get-tuple-element.31.old, ...), custom_call_target="tpu_custom_call" | custom-call | tf_op jit(solution)/shard_map/pallas_call | solution.py:426
  82.9 0.9 collective-permute-start.8
  83.8 3.4 %collective-permute-start.9 = (f32[4,96,128]{2,1,0:T(8,128)S(1)}, f32[4,96,128]{2,1,0:T(8,128)S(1)}, u32[]{:S(2)}, u32[]{:S(2)}) collective-permute-start(f32[4,96,128]{2,1,0:T(8,128)S(1)} %get-tuple-element.40), channel_id=1, source_target_pairs={{1,2},{3,4},{5,6},{2,1},{4,3},{6,5},{9,10},{11,12},{13,14},{10,9},... | collective-permute-start | bytes 589832 | tf_op jit(solution)/shard_map/ppermute | solution.py:462
  87.2 0.0 all-to-all-done.1
  87.2 0.1 collective-permute-start.13
  87.3 0.1 collective-permute-done.8.refs_2_.refs_3_
  87.5 3.6 %collective-permute-done.9.refs_3_.refs_4_ = f32[4,96,128]{2,1,0:T(8,128)S(1)} collective-permute-done((f32[4,96,128]{2,1,0:T(8,128)S(1)}, f32[4,96,128]{2,1,0:T(8,128)S(1)}, u32[]{:S(2)}, u32[]{:S(2)}) %collective-permute-start.9) | collective-permute-done | bytes 196640 | tf_op jit(solution)/shard_map/ppermute | solution.py:462
  91.1 0.9 shard_map.81
  92.0 0.1 collective-permute-start.10
  92.1 8.3 %collective-permute-start.11 = (f32[4,96,128]{2,1,0:T(8,128)S(1)}, f32[4,96,128]{2,1,0:T(8,128)S(1)}, u32[]{:S(2)}, u32[]{:S(2)}) collective-permute-start(f32[4,96,128]{2,1,0:T(8,128)S(1)} %get-tuple-element.42), channel_id=1, source_target_pairs={{8,16},{24,32},{40,48},{56,64},{72,80},{88,96},{104,112},{120,128}... | collective-permute-start | bytes 589832 | tf_op jit(solution)/shard_map/ppermute | solution.py:462
  100.3 0.0 collective-permute-done.10.refs_5_
  100.4 4.7 %collective-permute-done.11.refs_6_ = f32[4,96,128]{2,1,0:T(8,128)S(1)} collective-permute-done((f32[4,96,128]{2,1,0:T(8,128)S(1)}, f32[4,96,128]{2,1,0:T(8,128)S(1)}, u32[]{:S(2)}, u32[]{:S(2)}) %collective-permute-start.11) | collective-permute-done | bytes 196640 | tf_op jit(solution)/shard_map/ppermute | solution.py:462
  105.1 7.1 %shard_map.84 = (f32[4,128,128]{2,1,0:T(8,128)S(1)}, f32[4,128,128]{2,1,0:T(8,128)S(1)}, f32[4,48,128]{2,1,0:T(8,128)S(1)}, f32[4,48,128]{2,1,0:T(8,128)S(1)}, f...) custom-call(s32[12]{0:T(128)S(1)} %concatenate.3.info.refs_0_, ...), custom_call_target="tpu_custom_call" | custom-call | tf_op jit(solution)/shard_map/pallas_call | solution.py:426
  112.2 0.1 collective-permute-start.18
  112.3 1.5 collective-permute-done.18.other
  113.8 27.2 %all_to_all.20 = f32[128,4,128]{2,1,0:T(4,128)S(1)} all-to-all(f32[128,4,128]{2,1,0:T(4,128)S(1)} %bitcast.26), channel_id=1, replica_groups=mesh['z'=8,'xh'=2,'core'=2,'y'=4,'xl'=2] {'z','xh','y','xl'}, dimensions={0} | all-to-all | bytes 524288 | tf_op jit(solution)/shard_map/all_to_all | solution.py:478
  141.0 0.1 shard_map.88
  141.1 18.7 %all_to_all.21 = f32[128,4,128]{2,1,0:T(4,128)S(1)} all-to-all(f32[128,4,128]{2,1,0:T(4,128)S(1)} %bitcast.29), channel_id=1, replica_groups=mesh['z'=8,'xh'=2,'core'=2,'y'=4,'xl'=2] {'z','xh','y','xl'}, dimensions={0} | all-to-all | bytes 524288 | tf_op jit(solution)/shard_map/all_to_all | solution.py:478
  159.8 3.6 %collective-permute-start.19 = (f32[4,128,128]{2,1,0:T(8,128)S(1)}, f32[4,128,128]{2,1,0:T(8,128)S(1)}, u32[]{:S(2)}, u32[]{:S(2)}) collective-permute-start(f32[4,128,128]{2,1,0:T(8,128)S(1)} %bitcast.41), channel_id=1, source_target_pairs={{0,8},{8,0},{1,9},{9,1},{2,10},{10,2},{3,11},{11,3},{4,12},{12,4},... | collective-permute-start | bytes 786440 | tf_op jit(solution)/shard_map/ppermute | solution.py:474
  163.4 1.1 collective-permute-start.14
  164.5 2.4 %collective-permute-start.15 = (f32[4,48,128]{2,1,0:T(8,128)S(1)}, f32[4,48,128]{2,1,0:T(8,128)S(1)}, u32[]{:S(2)}, u32[]{:S(2)}) collective-permute-start(f32[4,48,128]{2,1,0:T(8,128)S(1)} %get-tuple-element.49), channel_id=1, source_target_pairs={{1,2},{3,4},{5,6},{2,1},{4,3},{6,5},{9,10},{11,12},{13,14},{10,9},... | collective-permute-start | bytes 294920 | tf_op jit(solution)/shard_map/ppermute | solution.py:462
  166.9 0.8 collective-permute-done.14.cn
  167.7 3.6 %collective-permute-done.15.cf = f32[4,48,128]{2,1,0:T(8,128)S(1)} collective-permute-done((f32[4,48,128]{2,1,0:T(8,128)S(1)}, f32[4,48,128]{2,1,0:T(8,128)S(1)}, u32[]{:S(2)}, u32[]{:S(2)}) %collective-permute-start.15) | collective-permute-done | bytes 98336 | tf_op jit(solution)/shard_map/ppermute | solution.py:462
  171.3 1.1 shard_map.85
  172.5 1.2 collective-permute-start.16
  173.7 2.1 %collective-permute-start.17 = (f32[4,32,128]{2,1,0:T(8,128)S(1)}, f32[4,32,128]{2,1,0:T(8,128)S(1)}, u32[]{:S(2)}, u32[]{:S(2)}) collective-permute-start(f32[4,32,128]{2,1,0:T(8,128)S(1)} %get-tuple-element.52), channel_id=1, source_target_pairs={{8,16},{24,32},{40,48},{56,64},{72,80},{88,96},{104,112},{120,128}... | collective-permute-start | bytes 196616 | tf_op jit(solution)/shard_map/ppermute | solution.py:462
  175.8 0.1 broadcast_in_dim.24
  175.9 0.1 broadcast_in_dim.25
  176.0 4.8 %collective-permute-done.17.rf = f32[4,32,128]{2,1,0:T(8,128)S(1)} collective-permute-done((f32[4,32,128]{2,1,0:T(8,128)S(1)}, f32[4,32,128]{2,1,0:T(8,128)S(1)}, u32[]{:S(2)}, u32[]{:S(2)}) %collective-permute-start.17) | collective-permute-done | bytes 65568 | tf_op jit(solution)/shard_map/ppermute | solution.py:462
  180.8 1.3 shard_map.86
  182.1 0.9 multiply_subtract_fusion
  (11 shorter events, 0.1 us)
Async XLA Ops:
  0.6 8.0 %copy-start = (f32[2,2,128,128]{3,2,1,0:T(8,128)S(1)}, f32[2,2,128,128]{3,2,1,0:T(8,128)}, u32[]{:S(2)}) copy-start(f32[2,2,128,128]{3,2,1,0:T(8,128)} %param.6) | copy-start | bytes 786436
  1.6 7.1 %collective-permute-start.1 = (f32[4,32,128]{2,1,0:T(8,128)S(1)}, f32[4,32,128]{2,1,0:T(8,128)S(1)}, u32[]{:S(2)}, u32[]{:S(2)}) collective-permute-start(f32[4,32,128]{2,1,0:T(8,128)S(1)} %get-tuple-element.56), channel_id=1, source_target_pairs={{8,16},{24,32},{40,48},{56,64},{72,80},{88,96},{104,112},{120,128}... | collective-permute-start | bytes 196616 | tf_op jit(solution)/shard_map/ppermute | solution.py:462
  5.9 2.8 %collective-permute-start = (f32[4,32,128]{2,1,0:T(8,128)S(1)}, f32[4,32,128]{2,1,0:T(8,128)S(1)}, u32[]{:S(2)}, u32[]{:S(2)}) collective-permute-start(f32[4,32,128]{2,1,0:T(8,128)S(1)} %get-tuple-element.57), channel_id=1, source_target_pairs={{0,8},{8,0},{1,9},{9,1},{2,10},{10,2},{3,11},{11,3},{4,12},{12,4},... | collective-permute-start | bytes 196616 | tf_op jit(solution)/shard_map/ppermute | solution.py:457
  6.0 0.7 copy-start.2
  7.0 6.9 %copy-start.1 = (f32[128,128]{1,0:T(8,128)S(1)}, f32[128,128]{1,0:T(8,128)}, u32[]{:S(2)}) copy-start(f32[128,128]{1,0:T(8,128)} %param.8) | copy-start | bytes 196612
  9.4 5.4 %collective-permute-start.2 = (f32[4,48,128]{2,1,0:T(8,128)S(1)}, f32[4,48,128]{2,1,0:T(8,128)S(1)}, u32[]{:S(2)}, u32[]{:S(2)}) collective-permute-start(f32[4,48,128]{2,1,0:T(8,128)S(1)} %get-tuple-element.29), channel_id=1, source_target_pairs={{0,1},{1,0},{2,3},{3,2},{4,5},{5,4},{6,7},{7,6},{8,9},{9,8},{10,11... | collective-permute-start | bytes 294920 | tf_op jit(solution)/shard_map/ppermute | solution.py:457
  9.8 7.2 %collective-permute-start.3 = (f32[4,48,128]{2,1,0:T(8,128)S(1)}, f32[4,48,128]{2,1,0:T(8,128)S(1)}, u32[]{:S(2)}, u32[]{:S(2)}) collective-permute-start(f32[4,48,128]{2,1,0:T(8,128)S(1)} %get-tuple-element.30), channel_id=1, source_target_pairs={{1,2},{3,4},{5,6},{2,1},{4,3},{6,5},{9,10},{11,12},{13,14},{10,9},... | collective-permute-start | bytes 294920 | tf_op jit(solution)/shard_map/ppermute | solution.py:462
  23.8 2.0 %collective-permute-start.12 = (f32[4,128,128]{2,1,0:T(8,128)S(1)}, f32[4,128,128]{2,1,0:T(8,128)S(1)}, u32[]{:S(2)}, u32[]{:S(2)}) collective-permute-start(f32[4,128,128]{2,1,0:T(8,128)S(1)} %get-tuple-element.44), channel_id=1, source_target_pairs={{0,8},{8,0},{1,9},{9,1},{2,10},{10,2},{3,11},{11,3},{4,12},{12,4},... | collective-permute-start | bytes 786440 | tf_op jit(solution)/shard_map/ppermute | solution.py:474
  26.5 28.8 %all-to-all-start = ((f32[128,4,128]{2,1,0:T(4,128)}), f32[128,4,128]{2,1,0:T(4,128)S(1)}, u32[]{:S(2)}, u32[]{:S(2)}) async-start(f32[128,4,128]{2,1,0:T(4,128)} %bitcast.9), calls=%async_computation | async-start | bytes 524288 | tf_op jit(solution)/shard_map/all_to_all | solution.py:478
  42.9 20.6 %collective-permute-start.4 = (f32[4,96,128]{2,1,0:T(8,128)S(1)}, f32[4,96,128]{2,1,0:T(8,128)S(1)}, u32[]{:S(2)}, u32[]{:S(2)}) collective-permute-start(f32[4,96,128]{2,1,0:T(8,128)S(1)} %get-tuple-element.33), channel_id=1, source_target_pairs={{0,1},{1,0},{2,3},{3,2},{4,5},{5,4},{6,7},{7,6},{8,9},{9,8},{10,11... | collective-permute-start | bytes 589832 | tf_op jit(solution)/shard_map/ppermute | solution.py:457
  43.9 19.7 %collective-permute-start.5 = (f32[4,96,128]{2,1,0:T(8,128)S(1)}, f32[4,96,128]{2,1,0:T(8,128)S(1)}, u32[]{:S(2)}, u32[]{:S(2)}) collective-permute-start(f32[4,96,128]{2,1,0:T(8,128)S(1)} %get-tuple-element.34), channel_id=1, source_target_pairs={{1,2},{3,4},{5,6},{2,1},{4,3},{6,5},{9,10},{11,12},{13,14},{10,9},... | collective-permute-start | bytes 589832 | tf_op jit(solution)/shard_map/ppermute | solution.py:462
  56.1 31.1 %all-to-all-start.1 = ((f32[128,4,128]{2,1,0:T(4,128)}), f32[128,4,128]{2,1,0:T(4,128)S(1)}, u32[]{:S(2)}, u32[]{:S(2)}) async-start(f32[128,4,128]{2,1,0:T(4,128)} %bitcast.11), calls=%async_computation.1 | async-start | bytes 524288 | tf_op jit(solution)/shard_map/all_to_all | solution.py:478
  64.5 6.0 %collective-permute-start.6 = (f32[4,96,128]{2,1,0:T(8,128)S(1)}, f32[4,96,128]{2,1,0:T(8,128)S(1)}, u32[]{:S(2)}, u32[]{:S(2)}) collective-permute-start(f32[4,96,128]{2,1,0:T(8,128)S(1)} %get-tuple-element.35), channel_id=1, source_target_pairs={{0,8},{8,0},{1,9},{9,1},{2,10},{10,2},{3,11},{11,3},{4,12},{12,4},... | collective-permute-start | bytes 589832 | tf_op jit(solution)/shard_map/ppermute | solution.py:457
  66.6 9.2 %collective-permute-start.7 = (f32[4,96,128]{2,1,0:T(8,128)S(1)}, f32[4,96,128]{2,1,0:T(8,128)S(1)}, u32[]{:S(2)}, u32[]{:S(2)}) collective-permute-start(f32[4,96,128]{2,1,0:T(8,128)S(1)} %get-tuple-element.36), channel_id=1, source_target_pairs={{8,16},{24,32},{40,48},{56,64},{72,80},{88,96},{104,112},{120,128}... | collective-permute-start | bytes 589832 | tf_op jit(solution)/shard_map/ppermute | solution.py:462
  82.9 4.6 %collective-permute-start.8 = (f32[4,96,128]{2,1,0:T(8,128)S(1)}, f32[4,96,128]{2,1,0:T(8,128)S(1)}, u32[]{:S(2)}, u32[]{:S(2)}) collective-permute-start(f32[4,96,128]{2,1,0:T(8,128)S(1)} %get-tuple-element.39), channel_id=1, source_target_pairs={{0,1},{1,0},{2,3},{3,2},{4,5},{5,4},{6,7},{7,6},{8,9},{9,8},{10,11... | collective-permute-start | bytes 589832 | tf_op jit(solution)/shard_map/ppermute | solution.py:457
  83.8 7.3 %collective-permute-start.9 = (f32[4,96,128]{2,1,0:T(8,128)S(1)}, f32[4,96,128]{2,1,0:T(8,128)S(1)}, u32[]{:S(2)}, u32[]{:S(2)}) collective-permute-start(f32[4,96,128]{2,1,0:T(8,128)S(1)} %get-tuple-element.40), channel_id=1, source_target_pairs={{1,2},{3,4},{5,6},{2,1},{4,3},{6,5},{9,10},{11,12},{13,14},{10,9},... | collective-permute-start | bytes 589832 | tf_op jit(solution)/shard_map/ppermute | solution.py:462
  87.2 17.8 %collective-permute-start.13 = (f32[4,128,128]{2,1,0:T(8,128)S(1)}, f32[4,128,128]{2,1,0:T(8,128)S(1)}, u32[]{:S(2)}, u32[]{:S(2)}) collective-permute-start(f32[4,128,128]{2,1,0:T(8,128)S(1)} %bitcast.30), channel_id=1, source_target_pairs={{0,8},{8,0},{1,9},{9,1},{2,10},{10,2},{3,11},{11,3},{4,12},{12,4},... | collective-permute-start | bytes 786440 | tf_op jit(solution)/shard_map/ppermute | solution.py:474
  92.0 8.4 %collective-permute-start.10 = (f32[4,96,128]{2,1,0:T(8,128)S(1)}, f32[4,96,128]{2,1,0:T(8,128)S(1)}, u32[]{:S(2)}, u32[]{:S(2)}) collective-permute-start(f32[4,96,128]{2,1,0:T(8,128)S(1)} %get-tuple-element.41), channel_id=1, source_target_pairs={{0,8},{8,0},{1,9},{9,1},{2,10},{10,2},{3,11},{11,3},{4,12},{12,4},... | collective-permute-start | bytes 589832 | tf_op jit(solution)/shard_map/ppermute | solution.py:457
  92.1 13.0 %collective-permute-start.11 = (f32[4,96,128]{2,1,0:T(8,128)S(1)}, f32[4,96,128]{2,1,0:T(8,128)S(1)}, u32[]{:S(2)}, u32[]{:S(2)}) collective-permute-start(f32[4,96,128]{2,1,0:T(8,128)S(1)} %get-tuple-element.42), channel_id=1, source_target_pairs={{8,16},{24,32},{40,48},{56,64},{72,80},{88,96},{104,112},{120,128}... | collective-permute-start | bytes 589832 | tf_op jit(solution)/shard_map/ppermute | solution.py:462
  112.2 1.6 collective-permute-start.18
  159.8 22.2 %collective-permute-start.19 = (f32[4,128,128]{2,1,0:T(8,128)S(1)}, f32[4,128,128]{2,1,0:T(8,128)S(1)}, u32[]{:S(2)}, u32[]{:S(2)}) collective-permute-start(f32[4,128,128]{2,1,0:T(8,128)S(1)} %bitcast.41), channel_id=1, source_target_pairs={{0,8},{8,0},{1,9},{9,1},{2,10},{10,2},{3,11},{11,3},{4,12},{12,4},... | collective-permute-start | bytes 786440 | tf_op jit(solution)/shard_map/ppermute | solution.py:474
  163.4 4.3 %collective-permute-start.14 = (f32[4,48,128]{2,1,0:T(8,128)S(1)}, f32[4,48,128]{2,1,0:T(8,128)S(1)}, u32[]{:S(2)}, u32[]{:S(2)}) collective-permute-start(f32[4,48,128]{2,1,0:T(8,128)S(1)} %get-tuple-element.48), channel_id=1, source_target_pairs={{0,1},{1,0},{2,3},{3,2},{4,5},{5,4},{6,7},{7,6},{8,9},{9,8},{10,11... | collective-permute-start | bytes 294920 | tf_op jit(solution)/shard_map/ppermute | solution.py:457
  164.5 6.8 %collective-permute-start.15 = (f32[4,48,128]{2,1,0:T(8,128)S(1)}, f32[4,48,128]{2,1,0:T(8,128)S(1)}, u32[]{:S(2)}, u32[]{:S(2)}) collective-permute-start(f32[4,48,128]{2,1,0:T(8,128)S(1)} %get-tuple-element.49), channel_id=1, source_target_pairs={{1,2},{3,4},{5,6},{2,1},{4,3},{6,5},{9,10},{11,12},{13,14},{10,9},... | collective-permute-start | bytes 294920 | tf_op jit(solution)/shard_map/ppermute | solution.py:462
  172.5 3.5 %collective-permute-start.16 = (f32[4,32,128]{2,1,0:T(8,128)S(1)}, f32[4,32,128]{2,1,0:T(8,128)S(1)}, u32[]{:S(2)}, u32[]{:S(2)}) collective-permute-start(f32[4,32,128]{2,1,0:T(8,128)S(1)} %get-tuple-element.51), channel_id=1, source_target_pairs={{0,8},{8,0},{1,9},{9,1},{2,10},{10,2},{3,11},{11,3},{4,12},{12,4},... | collective-permute-start | bytes 196616 | tf_op jit(solution)/shard_map/ppermute | solution.py:457
  173.7 7.1 %collective-permute-start.17 = (f32[4,32,128]{2,1,0:T(8,128)S(1)}, f32[4,32,128]{2,1,0:T(8,128)S(1)}, u32[]{:S(2)}, u32[]{:S(2)}) collective-permute-start(f32[4,32,128]{2,1,0:T(8,128)S(1)} %get-tuple-element.52), channel_id=1, source_target_pairs={{8,16},{24,32},{40,48},{56,64},{72,80},{88,96},{104,112},{120,128}... | collective-permute-start | bytes 196616 | tf_op jit(solution)/shard_map/ppermute | solution.py:462

commit v6 on v5

--- a/solution.py
+++ b/solution.py
@@ -214,7 +214,8 @@
     lane = lanes((WIN + 8, WIN))
     base = pl.multiple_of(oy // 8 * 8, 8)
     for a in range(4):
-        g_ref[a] = jnp.zeros((TALL, 2 * WIN), F32)
+        g_ref[a, :64] = jnp.zeros((64, 2 * WIN), F32)
+        g_ref[a, WIN + 8 :] = jnp.zeros((64, 2 * WIN), F32)
         turned = rows_down(pltpu.roll(grads[a], ox, 1), oy % 8)
         for t in range(2):
             part = jnp.where(lane >= ox if t == 0 else lane < ox, turned, 0.0)
@@ -259,7 +260,7 @@
             e_ref[a, :EXT, t * WIN : (t + 1) * WIN] = jnp.where(keep[t], value, 0.0)
 
 
-def step_core(info, b, e_ref, probe, loads, kernel, measured, tables, g_ref, w_ref, near, far):
+def step_core(info, b, e_ref, probe, loads, kernel, measured, tables, g_ref, w_ref, near, far, edge=None):
     oy, ox = info[2 * b], info[2 * b + 1]
     o1 = [place_window(e_ref, oy, ox, 0), place_window(e_ref, oy, ox, 1)]
     o2 = [place_window(e_ref, oy, ox, 2), place_window(e_ref, oy, ox, 3)]
@@ -291,6 +292,8 @@
     for a in range(4):
         first, second = g_ref[a, :EXT, :WIN], g_ref[a, :EXT, WIN:]
         if b < 2:
+            edge[a, : EXT // 2] = pack_rows(first[:64], second[:64])
+            edge[a, EXT // 2 :] = pack_rows(first[WIN:], second[WIN:])
             strips = (pack_cols(first), pack_cols(second))
         else:
             strips = (pack_strip(first, 0), pack_strip(second, OVL))
@@ -322,22 +325,22 @@
 
 
 def first_kernel(info, obj, row_near, row_far, col_near, col_far, probe, tables, kcos, ksin, measured,
-                 e_out, w_ref, near, far, keep, send, e_s, g_s, p_s, t_s, k_s, m_s, sem):
+                 e_out, w_ref, near, far, edge, keep, send, e_s, g_s, p_s, t_s, k_s, m_s, sem):
     loads = loads_of(0, probe, tables, kcos, ksin, measured, p_s, t_s, k_s, m_s, sem)
     build_extended(e_s, info, obj, row_near, row_far, col_near, col_far)
     pack_extended(e_s, e_out)
     loads[0].wait()
-    grads = step_core(info, 0, e_s, probe_blocks(p_s), loads, k_s, m_s, t_s, g_s, w_ref, near, far)
+    grads = step_core(info, 0, e_s, probe_blocks(p_s), loads, k_s, m_s, t_s, g_s, w_ref, near, far, edge)
     write_halves(info, grads, keep, send)
 
 
 def second_kernel(info, old, grad, cn, cf, rn, rf, probe, tables, kcos, ksin, measured,
-                  e_out, w_ref, near, far, held, e_s, g_s, p_s, t_s, k_s, m_s, h_s, sem):
+                  e_out, w_ref, near, far, edge, held, e_s, g_s, p_s, t_s, k_s, m_s, h_s, sem):
     loads = loads_of(1, probe, tables, kcos, ksin, measured, p_s, t_s, k_s, m_s, sem)
     update_extended(e_s, g_s, info, 1, old, grad, (cn, cf), (rn, rf))
     pack_extended(e_s, e_out)
     loads[0].wait()
-    grads = step_core(info, 1, e_s, probe_blocks(p_s), loads, k_s, m_s, t_s, g_s, w_ref, near, far)
+    grads = step_core(info, 1, e_s, probe_blocks(p_s), loads, k_s, m_s, t_s, g_s, w_ref, near, far, edge)
     for m in range(MODES):
         h_s[2 * m] = grads[m // 2][m % 2][0]
         h_s[2 * m + 1] = grads[m // 2][m % 2][1]
@@ -370,13 +373,11 @@
         out[4 + i] = probe[4 + i] - rate * jnp.where(first, other[i], mine[i])
 
 
-def middle_kernel(b, info, grad, cn, cf, near, far, g_s):
-    place_gradient(info, b, grad, g_s)
-    for a in range(4):
-        west_east = [unpack_cols(x) for x in sides(info[XLOW] == 1, cn, cf, a)]
-        full = [g_s[a, :EXT, t * WIN : (t + 1) * WIN] + west_east[t] for t in range(2)]
-        up = pack_rows(full[0][:64], full[1][:64])
-        down = pack_rows(full[0][128:], full[1][128:])
+def middle_kernel(info, edge, cn, cf, near, far):
+    for a in range(4):
+        tiles = [unpack_cols(x) for x in sides(info[XLOW] == 1, cn, cf, a)]
+        up = edge[a, : EXT // 2] + pack_rows(tiles[0][:64], tiles[1][:64])
+        down = edge[a, EXT // 2 :] + pack_rows(tiles[0][WIN:], tiles[1][WIN:])
         by_parity(info[CORE] == 1, (up, down), near, far, a)
 
 
@@ -495,12 +496,9 @@
     return chip_exchange(spread.reshape(N_CHIPS, -1, WIN)).reshape(HALF)
 
 
-def exchanged(info, grad, near, far, b):
+def exchanged(info, grad, near, far, edge):
     cols = cols_swapped(near, far)
-    near, far = call(
-        lambda *refs: middle_kernel(b, *refs), [BAND, BAND], info, grad, *cols,
-        scratch=(PLACE,),
-    )
+    near, far = call(middle_kernel, [BAND, BAND], info, edge, *cols)
     return grad, *cols, *rows_swapped(near, far)
 
 
@@ -531,20 +529,20 @@
     cols = call(halo_kernel, [(4, 48, WIN)] * 2, info, obj, *rows)
     cols = cols_swapped(*cols)
 
-    step_outs = [EXT_SHAPE, HALF, BAND, BAND]
+    step_outs = [EXT_SHAPE, HALF, BAND, BAND, (4, EXT, WIN)]
     whole = (2 * MODES, WIN, WIN)
-    extended, grad, near, far, keep0, send0 = call(
+    extended, grad, near, far, edge, keep0, send0 = call(
         first_kernel, step_outs + [HALF, HALF], info, obj, *rows, *cols,
         loads=loads, scratch=STEP_SCRATCH + SEMS,
     )
-    moves = exchanged(info, grad, near, far, 0)
+    moves = exchanged(info, grad, near, far, edge)
     mine0 = summed_half(keep0, send0)
     other0 = swap_cores(mine0)
-    extended, grad, near, far, held = call(
+    extended, grad, near, far, edge, held = call(
         second_kernel, step_outs, info, extended, *moves,
         loads=loads, stores=(whole,), scratch=STEP_SCRATCH + HELD + SEMS,
     )
-    moves = exchanged(info, grad, near, far, 1)
+    moves = exchanged(info, grad, near, far, edge)
     own, grad, near, far, keep2, send2, probe = call(
         lambda *refs: third_kernel(rate, *refs), [HALF, HALF, STRIP, STRIP, HALF, HALF, whole],
         info, extended, *moves, mine0, other0,

time: 184 us -> 184 us (level)
  no operation moved by 1% of the time
where the time goes in v6:
time: 184 us; the launch traced here: 183 us
  starting transfers between devices  67.2 us (37%)
  blocking collectives  45.9 us (25%)
  waiting for transfers between devices  37.7 us (20%)
  Pallas kernels  27.3 us (15%)
  local copies, waits for them, and re-layouts  2.06 us (1%)
  other arithmetic  1.87 us (1%)
    all_to_all x2, blocking collectives, chip_exchange(): return lax.all_to_all(x, CHIPS, 0, 0, tiled=True)  45.9 us
    ppermute x8, starting transfers between devices, swap_far(): return lax.ppermute(x, axes, pairs + [(j, i) for i, j in pairs])  31.8 us
    pallas_call x12, Pallas kernels, call(): pl.pallas_call(kernel, out_shape=[pltpu.VMEM(s, F32) if on_chip else jax....  27.3 us
    ppermute x8, waiting for transfers between devices, swap_far(): return lax.ppermute(x, axes, pairs + [(j, i) for i, j in pairs])  26 us
    all_to_all x2, starting transfers between devices, chip_exchange(): return lax.all_to_all(x, CHIPS, 0, 0, tiled=True)  23.8 us
    all_to_all x2, waiting for transfers between devices, chip_exchange(): return lax.all_to_all(x, CHIPS, 0, 0, tiled=True)  8.07 us
    ppermute x8, starting transfers between devices, swap_near(): return lax.ppermute(x, axis, [(0, 1), (1, 0)])  6.98 us
    ppermute x4, starting transfers between devices, swap_cores(): return lax.ppermute(x, 'core', [(0, 1), (1, 0)])  4.6 us
  transfers between devices with their start and end apart: 22, of which 12 were waited for; matrix products, arithmetic and copies ran while one was open for 1% of the time, Pallas kernels for 7%

profile of v6, /device:TPU:3, one launch (start us, length us, event | category | flops | bytes accessed | tf_op | source)
XLA Modules:
  0.0 183.0 jit_solution(16968125864442918236)
XLA Ops:
  0.6 0.9 slice_select_fusion
  1.6 4.3 %collective-permute-start.1 = (f32[4,32,128]{2,1,0:T(8,128)S(1)}, f32[4,32,128]{2,1,0:T(8,128)S(1)}, u32[]{:S(2)}, u32[]{:S(2)}) collective-permute-start(f32[4,32,128]{2,1,0:T(8,128)S(1)} %get-tuple-element.60), channel_id=1, source_target_pairs={{8,16},{24,32},{40,48},{56,64},{72,80},{88,96},{104,112},{120,128}... | collective-permute-start | bytes 196616 | tf_op jit(solution)/shard_map/ppermute | solution.py:463
  5.9 0.1 collective-permute-start
  6.0 0.0 copy-start.2
  6.0 0.7 copy-done.2
  6.7 0.1 copy.9
  6.8 0.1 reshape.54
  6.9 0.1 concatenate.3.info.refs_0_
  7.0 1.7 collective-permute-done.1.row_far
  8.7 0.0 collective-permute-done.row_near
  8.7 0.8 shard_map.77
  9.4 0.4 collective-permute-start.2
  9.8 4.1 %collective-permute-start.3 = (f32[4,48,128]{2,1,0:T(8,128)S(1)}, f32[4,48,128]{2,1,0:T(8,128)S(1)}, u32[]{:S(2)}, u32[]{:S(2)}) collective-permute-start(f32[4,48,128]{2,1,0:T(8,128)S(1)} %get-tuple-element.32), channel_id=1, source_target_pairs={{1,2},{3,4},{5,6},{2,1},{4,3},{6,5},{9,10},{11,12},{13,14},{10,9},... | collective-permute-start | bytes 294920 | tf_op jit(solution)/shard_map/ppermute | solution.py:463
  13.9 0.9 fusion
  14.8 0.0 collective-permute-done.2.col_near
  14.8 2.3 %collective-permute-done.3.col_far = f32[4,48,128]{2,1,0:T(8,128)S(1)} collective-permute-done((f32[4,48,128]{2,1,0:T(8,128)S(1)}, f32[4,48,128]{2,1,0:T(8,128)S(1)}, u32[]{:S(2)}, u32[]{:S(2)}) %collective-permute-start.3) | collective-permute-done | bytes 98336 | tf_op jit(solution)/shard_map/ppermute | solution.py:463
  17.1 6.7 %shard_map.78 = (f32[4,288,128]{2,1,0:T(8,128)S(1)}, f32[4,128,128]{2,1,0:T(8,128)S(1)}, f32[4,96,128]{2,1,0:T(8,128)S(1)}, f32[4,96,128]{2,1,0:T(8,128)S(1)}, f...) custom-call(s32[12]{0:T(128)S(1)} %concatenate.3.info.refs_0_, ...), custom_call_target="tpu_custom_call" | custom-call | tf_op jit(solution)/shard_map/pallas_call | solution.py:427
  23.7 0.9 collective-permute-start.12
  24.6 1.2 collective-permute-done.12.other
  25.8 0.7 shard_map.82
  26.5 16.4 %all-to-all-start = ((f32[128,4,128]{2,1,0:T(4,128)}), f32[128,4,128]{2,1,0:T(4,128)S(1)}, u32[]{:S(2)}, u32[]{:S(2)}) async-start(f32[128,4,128]{2,1,0:T(4,128)} %bitcast.9), calls=%async_computation | async-start | bytes 524288 | tf_op jit(solution)/shard_map/all_to_all | solution.py:479
  42.9 1.0 collective-permute-start.4
  43.9 3.4 %collective-permute-start.5 = (f32[4,96,128]{2,1,0:T(8,128)S(1)}, f32[4,96,128]{2,1,0:T(8,128)S(1)}, u32[]{:S(2)}, u32[]{:S(2)}) collective-permute-start(f32[4,96,128]{2,1,0:T(8,128)S(1)} %get-tuple-element.36), channel_id=1, source_target_pairs={{1,2},{3,4},{5,6},{2,1},{4,3},{6,5},{9,10},{11,12},{13,14},{10,9},... | collective-permute-start | bytes 589832 | tf_op jit(solution)/shard_map/ppermute | solution.py:463
  47.2 8.1 %all-to-all-done = f32[128,4,128]{2,1,0:T(4,128)S(1)} async-done(((f32[128,4,128]{2,1,0:T(4,128)}), f32[128,4,128]{2,1,0:T(4,128)S(1)}, u32[]{:S(2)}, u32[]{:S(2)}) %all-to-all-start) | async-done | bytes 262176 | tf_op jit(solution)/shard_map/all_to_all | solution.py:479
  55.3 0.8 shard_map.83
  56.1 7.4 %all-to-all-start.1 = ((f32[128,4,128]{2,1,0:T(4,128)}), f32[128,4,128]{2,1,0:T(4,128)S(1)}, u32[]{:S(2)}, u32[]{:S(2)}) async-start(f32[128,4,128]{2,1,0:T(4,128)} %bitcast.11), calls=%async_computation.1 | async-start | bytes 524288 | tf_op jit(solution)/shard_map/all_to_all | solution.py:479
  63.5 0.0 collective-permute-done.4.cn
  63.5 0.0 collective-permute-done.5.cf
  63.5 0.7 shard_map.79
  64.3 2.2 %collective-permute-start.6 = (f32[4,96,128]{2,1,0:T(8,128)S(1)}, f32[4,96,128]{2,1,0:T(8,128)S(1)}, u32[]{:S(2)}, u32[]{:S(2)}) collective-permute-start(f32[4,96,128]{2,1,0:T(8,128)S(1)} %get-tuple-element.38), channel_id=1, source_target_pairs={{0,8},{8,0},{1,9},{9,1},{2,10},{10,2},{3,11},{11,3},{4,12},{12,4},... | collective-permute-start | bytes 589832 | tf_op jit(solution)/shard_map/ppermute | solution.py:458
  66.4 3.8 %collective-permute-start.7 = (f32[4,96,128]{2,1,0:T(8,128)S(1)}, f32[4,96,128]{2,1,0:T(8,128)S(1)}, u32[]{:S(2)}, u32[]{:S(2)}) collective-permute-start(f32[4,96,128]{2,1,0:T(8,128)S(1)} %get-tuple-element.39), channel_id=1, source_target_pairs={{8,16},{24,32},{40,48},{56,64},{72,80},{88,96},{104,112},{120,128}... | collective-permute-start | bytes 589832 | tf_op jit(solution)/shard_map/ppermute | solution.py:463
  70.3 0.0 collective-permute-done.6.rn
  70.3 5.4 %collective-permute-done.7.rf = f32[4,96,128]{2,1,0:T(8,128)S(1)} collective-permute-done((f32[4,96,128]{2,1,0:T(8,128)S(1)}, f32[4,96,128]{2,1,0:T(8,128)S(1)}, u32[]{:S(2)}, u32[]{:S(2)}) %collective-permute-start.7) | collective-permute-done | bytes 196640 | tf_op jit(solution)/shard_map/ppermute | solution.py:463
  75.7 7.3 %shard_map.80 = (f32[4,288,128]{2,1,0:T(8,128)S(1)}, f32[4,128,128]{2,1,0:T(8,128)S(1)}, f32[4,96,128]{2,1,0:T(8,128)S(1)}, f32[4,96,128]{2,1,0:T(8,128)S(1)}, f...) custom-call(s32[12]{0:T(128)S(1)} %concatenate.3.info.refs_0_, f32[4,288,128]{2,1,0:T(8,128)S(1)} %get-tuple-element.33.old, ...), custom_call_target="tpu_custom_call" | custom-call | tf_op jit(solution)/shard_map/pallas_call | solution.py:427
  83.0 0.9 collective-permute-start.8
  83.9 3.5 %collective-permute-start.9 = (f32[4,96,128]{2,1,0:T(8,128)S(1)}, f32[4,96,128]{2,1,0:T(8,128)S(1)}, u32[]{:S(2)}, u32[]{:S(2)}) collective-permute-start(f32[4,96,128]{2,1,0:T(8,128)S(1)} %get-tuple-element.43), channel_id=1, source_target_pairs={{1,2},{3,4},{5,6},{2,1},{4,3},{6,5},{9,10},{11,12},{13,14},{10,9},... | collective-permute-start | bytes 589832 | tf_op jit(solution)/shard_map/ppermute | solution.py:463
  87.4 0.0 all-to-all-done.1
  87.4 0.1 collective-permute-start.13
  87.5 0.1 collective-permute-done.8.cn.refs_3_
  87.6 3.6 %collective-permute-done.9.cf.refs_4_ = f32[4,96,128]{2,1,0:T(8,128)S(1)} collective-permute-done((f32[4,96,128]{2,1,0:T(8,128)S(1)}, f32[4,96,128]{2,1,0:T(8,128)S(1)}, u32[]{:S(2)}, u32[]{:S(2)}) %collective-permute-start.9) | collective-permute-done | bytes 196640 | tf_op jit(solution)/shard_map/ppermute | solution.py:463
  91.2 0.7 shard_map.81
  92.0 0.1 collective-permute-start.10
  92.1 8.2 %collective-permute-start.11 = (f32[4,96,128]{2,1,0:T(8,128)S(1)}, f32[4,96,128]{2,1,0:T(8,128)S(1)}, u32[]{:S(2)}, u32[]{:S(2)}) collective-permute-start(f32[4,96,128]{2,1,0:T(8,128)S(1)} %get-tuple-element.46), channel_id=1, source_target_pairs={{8,16},{24,32},{40,48},{56,64},{72,80},{88,96},{104,112},{120,128}... | collective-permute-start | bytes 589832 | tf_op jit(solution)/shard_map/ppermute | solution.py:463
  100.3 4.7 %collective-permute-done.11.refs_6_ = f32[4,96,128]{2,1,0:T(8,128)S(1)} collective-permute-done((f32[4,96,128]{2,1,0:T(8,128)S(1)}, f32[4,96,128]{2,1,0:T(8,128)S(1)}, u32[]{:S(2)}, u32[]{:S(2)}) %collective-permute-start.11) | collective-permute-done | bytes 196640 | tf_op jit(solution)/shard_map/ppermute | solution.py:463
  105.0 7.1 %shard_map.84 = (f32[4,128,128]{2,1,0:T(8,128)S(1)}, f32[4,128,128]{2,1,0:T(8,128)S(1)}, f32[4,48,128]{2,1,0:T(8,128)S(1)}, f32[4,48,128]{2,1,0:T(8,128)S(1)}, f...) custom-call(s32[12]{0:T(128)S(1)} %concatenate.3.info.refs_0_, ...), custom_call_target="tpu_custom_call" | custom-call | tf_op jit(solution)/shard_map/pallas_call | solution.py:427
  112.1 0.1 collective-permute-start.18
  112.2 1.5 collective-permute-done.18.other
  113.8 27.2 %all_to_all.20 = f32[128,4,128]{2,1,0:T(4,128)S(1)} all-to-all(f32[128,4,128]{2,1,0:T(4,128)S(1)} %bitcast.26), channel_id=1, replica_groups=mesh['z'=8,'xh'=2,'core'=2,'y'=4,'xl'=2] {'z','xh','y','xl'}, dimensions={0} | all-to-all | bytes 524288 | tf_op jit(solution)/shard_map/all_to_all | solution.py:479
  141.0 0.1 shard_map.88
  141.1 18.7 %all_to_all.21 = f32[128,4,128]{2,1,0:T(4,128)S(1)} all-to-all(f32[128,4,128]{2,1,0:T(4,128)S(1)} %bitcast.29), channel_id=1, replica_groups=mesh['z'=8,'xh'=2,'core'=2,'y'=4,'xl'=2] {'z','xh','y','xl'}, dimensions={0} | all-to-all | bytes 524288 | tf_op jit(solution)/shard_map/all_to_all | solution.py:479
  159.8 3.6 %collective-permute-start.19 = (f32[4,128,128]{2,1,0:T(8,128)S(1)}, f32[4,128,128]{2,1,0:T(8,128)S(1)}, u32[]{:S(2)}, u32[]{:S(2)}) collective-permute-start(f32[4,128,128]{2,1,0:T(8,128)S(1)} %bitcast.41), channel_id=1, source_target_pairs={{0,8},{8,0},{1,9},{9,1},{2,10},{10,2},{3,11},{11,3},{4,12},{12,4},... | collective-permute-start | bytes 786440 | tf_op jit(solution)/shard_map/ppermute | solution.py:475
  163.3 1.1 collective-permute-start.14
  164.4 2.4 %collective-permute-start.15 = (f32[4,48,128]{2,1,0:T(8,128)S(1)}, f32[4,48,128]{2,1,0:T(8,128)S(1)}, u32[]{:S(2)}, u32[]{:S(2)}) collective-permute-start(f32[4,48,128]{2,1,0:T(8,128)S(1)} %get-tuple-element.53), channel_id=1, source_target_pairs={{1,2},{3,4},{5,6},{2,1},{4,3},{6,5},{9,10},{11,12},{13,14},{10,9},... | collective-permute-start | bytes 294920 | tf_op jit(solution)/shard_map/ppermute | solution.py:463
  166.9 0.8 collective-permute-done.14.cn
  167.7 3.6 %collective-permute-done.15.cf = f32[4,48,128]{2,1,0:T(8,128)S(1)} collective-permute-done((f32[4,48,128]{2,1,0:T(8,128)S(1)}, f32[4,48,128]{2,1,0:T(8,128)S(1)}, u32[]{:S(2)}, u32[]{:S(2)}) %collective-permute-start.15) | collective-permute-done | bytes 98336 | tf_op jit(solution)/shard_map/ppermute | solution.py:463
  171.3 1.1 shard_map.85
  172.4 1.2 collective-permute-start.16
  173.6 2.1 %collective-permute-start.17 = (f32[4,32,128]{2,1,0:T(8,128)S(1)}, f32[4,32,128]{2,1,0:T(8,128)S(1)}, u32[]{:S(2)}, u32[]{:S(2)}) collective-permute-start(f32[4,32,128]{2,1,0:T(8,128)S(1)} %get-tuple-element.56), channel_id=1, source_target_pairs={{8,16},{24,32},{40,48},{56,64},{72,80},{88,96},{104,112},{120,128}... | collective-permute-start | bytes 196616 | tf_op jit(solution)/shard_map/ppermute | solution.py:463
  175.8 0.1 broadcast_in_dim.24
  175.8 0.1 broadcast_in_dim.25
  175.9 4.8 %collective-permute-done.17.rf = f32[4,32,128]{2,1,0:T(8,128)S(1)} collective-permute-done((f32[4,32,128]{2,1,0:T(8,128)S(1)}, f32[4,32,128]{2,1,0:T(8,128)S(1)}, u32[]{:S(2)}, u32[]{:S(2)}) %collective-permute-start.17) | collective-permute-done | bytes 65568 | tf_op jit(solution)/shard_map/ppermute | solution.py:463
  180.7 1.3 shard_map.86
  182.0 0.0 collective-permute-done.19
  182.1 0.9 multiply_subtract_fusion
  (11 shorter events, 0.1 us)
Async XLA Ops:
  0.6 8.0 %copy-start = (f32[2,2,128,128]{3,2,1,0:T(8,128)S(1)}, f32[2,2,128,128]{3,2,1,0:T(8,128)}, u32[]{:S(2)}) copy-start(f32[2,2,128,128]{3,2,1,0:T(8,128)} %param.6) | copy-start | bytes 786436
  1.6 7.1 %collective-permute-start.1 = (f32[4,32,128]{2,1,0:T(8,128)S(1)}, f32[4,32,128]{2,1,0:T(8,128)S(1)}, u32[]{:S(2)}, u32[]{:S(2)}) collective-permute-start(f32[4,32,128]{2,1,0:T(8,128)S(1)} %get-tuple-element.60), channel_id=1, source_target_pairs={{8,16},{24,32},{40,48},{56,64},{72,80},{88,96},{104,112},{120,128}... | collective-permute-start | bytes 196616 | tf_op jit(solution)/shard_map/ppermute | solution.py:463
  5.9 2.8 %collective-permute-start = (f32[4,32,128]{2,1,0:T(8,128)S(1)}, f32[4,32,128]{2,1,0:T(8,128)S(1)}, u32[]{:S(2)}, u32[]{:S(2)}) collective-permute-start(f32[4,32,128]{2,1,0:T(8,128)S(1)} %get-tuple-element.61), channel_id=1, source_target_pairs={{0,8},{8,0},{1,9},{9,1},{2,10},{10,2},{3,11},{11,3},{4,12},{12,4},... | collective-permute-start | bytes 196616 | tf_op jit(solution)/shard_map/ppermute | solution.py:458
  6.0 0.7 copy-start.2
  7.0 6.9 %copy-start.1 = (f32[128,128]{1,0:T(8,128)S(1)}, f32[128,128]{1,0:T(8,128)}, u32[]{:S(2)}) copy-start(f32[128,128]{1,0:T(8,128)} %param.8) | copy-start | bytes 196612
  9.4 5.4 %collective-permute-start.2 = (f32[4,48,128]{2,1,0:T(8,128)S(1)}, f32[4,48,128]{2,1,0:T(8,128)S(1)}, u32[]{:S(2)}, u32[]{:S(2)}) collective-permute-start(f32[4,48,128]{2,1,0:T(8,128)S(1)} %get-tuple-element.31), channel_id=1, source_target_pairs={{0,1},{1,0},{2,3},{3,2},{4,5},{5,4},{6,7},{7,6},{8,9},{9,8},{10,11... | collective-permute-start | bytes 294920 | tf_op jit(solution)/shard_map/ppermute | solution.py:458
  9.8 7.2 %collective-permute-start.3 = (f32[4,48,128]{2,1,0:T(8,128)S(1)}, f32[4,48,128]{2,1,0:T(8,128)S(1)}, u32[]{:S(2)}, u32[]{:S(2)}) collective-permute-start(f32[4,48,128]{2,1,0:T(8,128)S(1)} %get-tuple-element.32), channel_id=1, source_target_pairs={{1,2},{3,4},{5,6},{2,1},{4,3},{6,5},{9,10},{11,12},{13,14},{10,9},... | collective-permute-start | bytes 294920 | tf_op jit(solution)/shard_map/ppermute | solution.py:463
  23.7 2.0 %collective-permute-start.12 = (f32[4,128,128]{2,1,0:T(8,128)S(1)}, f32[4,128,128]{2,1,0:T(8,128)S(1)}, u32[]{:S(2)}, u32[]{:S(2)}) collective-permute-start(f32[4,128,128]{2,1,0:T(8,128)S(1)} %get-tuple-element.48), channel_id=1, source_target_pairs={{0,8},{8,0},{1,9},{9,1},{2,10},{10,2},{3,11},{11,3},{4,12},{12,4},... | collective-permute-start | bytes 786440 | tf_op jit(solution)/shard_map/ppermute | solution.py:475
  26.5 28.8 %all-to-all-start = ((f32[128,4,128]{2,1,0:T(4,128)}), f32[128,4,128]{2,1,0:T(4,128)S(1)}, u32[]{:S(2)}, u32[]{:S(2)}) async-start(f32[128,4,128]{2,1,0:T(4,128)} %bitcast.9), calls=%async_computation | async-start | bytes 524288 | tf_op jit(solution)/shard_map/all_to_all | solution.py:479
  42.9 20.6 %collective-permute-start.4 = (f32[4,96,128]{2,1,0:T(8,128)S(1)}, f32[4,96,128]{2,1,0:T(8,128)S(1)}, u32[]{:S(2)}, u32[]{:S(2)}) collective-permute-start(f32[4,96,128]{2,1,0:T(8,128)S(1)} %get-tuple-element.35), channel_id=1, source_target_pairs={{0,1},{1,0},{2,3},{3,2},{4,5},{5,4},{6,7},{7,6},{8,9},{9,8},{10,11... | collective-permute-start | bytes 589832 | tf_op jit(solution)/shard_map/ppermute | solution.py:458
  43.9 19.7 %collective-permute-start.5 = (f32[4,96,128]{2,1,0:T(8,128)S(1)}, f32[4,96,128]{2,1,0:T(8,128)S(1)}, u32[]{:S(2)}, u32[]{:S(2)}) collective-permute-start(f32[4,96,128]{2,1,0:T(8,128)S(1)} %get-tuple-element.36), channel_id=1, source_target_pairs={{1,2},{3,4},{5,6},{2,1},{4,3},{6,5},{9,10},{11,12},{13,14},{10,9},... | collective-permute-start | bytes 589832 | tf_op jit(solution)/shard_map/ppermute | solution.py:463
  56.1 31.3 %all-to-all-start.1 = ((f32[128,4,128]{2,1,0:T(4,128)}), f32[128,4,128]{2,1,0:T(4,128)S(1)}, u32[]{:S(2)}, u32[]{:S(2)}) async-start(f32[128,4,128]{2,1,0:T(4,128)} %bitcast.11), calls=%async_computation.1 | async-start | bytes 524288 | tf_op jit(solution)/shard_map/all_to_all | solution.py:479
  64.3 6.0 %collective-permute-start.6 = (f32[4,96,128]{2,1,0:T(8,128)S(1)}, f32[4,96,128]{2,1,0:T(8,128)S(1)}, u32[]{:S(2)}, u32[]{:S(2)}) collective-permute-start(f32[4,96,128]{2,1,0:T(8,128)S(1)} %get-tuple-element.38), channel_id=1, source_target_pairs={{0,8},{8,0},{1,9},{9,1},{2,10},{10,2},{3,11},{11,3},{4,12},{12,4},... | collective-permute-start | bytes 589832 | tf_op jit(solution)/shard_map/ppermute | solution.py:458
  66.4 9.3 %collective-permute-start.7 = (f32[4,96,128]{2,1,0:T(8,128)S(1)}, f32[4,96,128]{2,1,0:T(8,128)S(1)}, u32[]{:S(2)}, u32[]{:S(2)}) collective-permute-start(f32[4,96,128]{2,1,0:T(8,128)S(1)} %get-tuple-element.39), channel_id=1, source_target_pairs={{8,16},{24,32},{40,48},{56,64},{72,80},{88,96},{104,112},{120,128}... | collective-permute-start | bytes 589832 | tf_op jit(solution)/shard_map/ppermute | solution.py:463
  83.0 4.6 %collective-permute-start.8 = (f32[4,96,128]{2,1,0:T(8,128)S(1)}, f32[4,96,128]{2,1,0:T(8,128)S(1)}, u32[]{:S(2)}, u32[]{:S(2)}) collective-permute-start(f32[4,96,128]{2,1,0:T(8,128)S(1)} %get-tuple-element.42), channel_id=1, source_target_pairs={{0,1},{1,0},{2,3},{3,2},{4,5},{5,4},{6,7},{7,6},{8,9},{9,8},{10,11... | collective-permute-start | bytes 589832 | tf_op jit(solution)/shard_map/ppermute | solution.py:458
  83.9 7.3 %collective-permute-start.9 = (f32[4,96,128]{2,1,0:T(8,128)S(1)}, f32[4,96,128]{2,1,0:T(8,128)S(1)}, u32[]{:S(2)}, u32[]{:S(2)}) collective-permute-start(f32[4,96,128]{2,1,0:T(8,128)S(1)} %get-tuple-element.43), channel_id=1, source_target_pairs={{1,2},{3,4},{5,6},{2,1},{4,3},{6,5},{9,10},{11,12},{13,14},{10,9},... | collective-permute-start | bytes 589832 | tf_op jit(solution)/shard_map/ppermute | solution.py:463
  87.4 17.6 %collective-permute-start.13 = (f32[4,128,128]{2,1,0:T(8,128)S(1)}, f32[4,128,128]{2,1,0:T(8,128)S(1)}, u32[]{:S(2)}, u32[]{:S(2)}) collective-permute-start(f32[4,128,128]{2,1,0:T(8,128)S(1)} %bitcast.30), channel_id=1, source_target_pairs={{0,8},{8,0},{1,9},{9,1},{2,10},{10,2},{3,11},{11,3},{4,12},{12,4},... | collective-permute-start | bytes 786440 | tf_op jit(solution)/shard_map/ppermute | solution.py:475
  92.0 8.4 %collective-permute-start.10 = (f32[4,96,128]{2,1,0:T(8,128)S(1)}, f32[4,96,128]{2,1,0:T(8,128)S(1)}, u32[]{:S(2)}, u32[]{:S(2)}) collective-permute-start(f32[4,96,128]{2,1,0:T(8,128)S(1)} %get-tuple-element.45), channel_id=1, source_target_pairs={{0,8},{8,0},{1,9},{9,1},{2,10},{10,2},{3,11},{11,3},{4,12},{12,4},... | collective-permute-start | bytes 589832 | tf_op jit(solution)/shard_map/ppermute | solution.py:458
  92.1 13.0 %collective-permute-start.11 = (f32[4,96,128]{2,1,0:T(8,128)S(1)}, f32[4,96,128]{2,1,0:T(8,128)S(1)}, u32[]{:S(2)}, u32[]{:S(2)}) collective-permute-start(f32[4,96,128]{2,1,0:T(8,128)S(1)} %get-tuple-element.46), channel_id=1, source_target_pairs={{8,16},{24,32},{40,48},{56,64},{72,80},{88,96},{104,112},{120,128}... | collective-permute-start | bytes 589832 | tf_op jit(solution)/shard_map/ppermute | solution.py:463
  112.1 1.6 collective-permute-start.18
  159.8 22.2 %collective-permute-start.19 = (f32[4,128,128]{2,1,0:T(8,128)S(1)}, f32[4,128,128]{2,1,0:T(8,128)S(1)}, u32[]{:S(2)}, u32[]{:S(2)}) collective-permute-start(f32[4,128,128]{2,1,0:T(8,128)S(1)} %bitcast.41), channel_id=1, source_target_pairs={{0,8},{8,0},{1,9},{9,1},{2,10},{10,2},{3,11},{11,3},{4,12},{12,4},... | collective-permute-start | bytes 786440 | tf_op jit(solution)/shard_map/ppermute | solution.py:475
  163.3 4.3 %collective-permute-start.14 = (f32[4,48,128]{2,1,0:T(8,128)S(1)}, f32[4,48,128]{2,1,0:T(8,128)S(1)}, u32[]{:S(2)}, u32[]{:S(2)}) collective-permute-start(f32[4,48,128]{2,1,0:T(8,128)S(1)} %get-tuple-element.52), channel_id=1, source_target_pairs={{0,1},{1,0},{2,3},{3,2},{4,5},{5,4},{6,7},{7,6},{8,9},{9,8},{10,11... | collective-permute-start | bytes 294920 | tf_op jit(solution)/shard_map/ppermute | solution.py:458
  164.4 6.8 %collective-permute-start.15 = (f32[4,48,128]{2,1,0:T(8,128)S(1)}, f32[4,48,128]{2,1,0:T(8,128)S(1)}, u32[]{:S(2)}, u32[]{:S(2)}) collective-permute-start(f32[4,48,128]{2,1,0:T(8,128)S(1)} %get-tuple-element.53), channel_id=1, source_target_pairs={{1,2},{3,4},{5,6},{2,1},{4,3},{6,5},{9,10},{11,12},{13,14},{10,9},... | collective-permute-start | bytes 294920 | tf_op jit(solution)/shard_map/ppermute | solution.py:463
  172.4 3.5 %collective-permute-start.16 = (f32[4,32,128]{2,1,0:T(8,128)S(1)}, f32[4,32,128]{2,1,0:T(8,128)S(1)}, u32[]{:S(2)}, u32[]{:S(2)}) collective-permute-start(f32[4,32,128]{2,1,0:T(8,128)S(1)} %get-tuple-element.55), channel_id=1, source_target_pairs={{0,8},{8,0},{1,9},{9,1},{2,10},{10,2},{3,11},{11,3},{4,12},{12,4},... | collective-permute-start | bytes 196616 | tf_op jit(solution)/shard_map/ppermute | solution.py:458
  173.6 7.1 %collective-permute-start.17 = (f32[4,32,128]{2,1,0:T(8,128)S(1)}, f32[4,32,128]{2,1,0:T(8,128)S(1)}, u32[]{:S(2)}, u32[]{:S(2)}) collective-permute-start(f32[4,32,128]{2,1,0:T(8,128)S(1)} %get-tuple-element.56), channel_id=1, source_target_pairs={{8,16},{24,32},{40,48},{56,64},{72,80},{88,96},{104,112},{120,128}... | collective-permute-start | bytes 196616 | tf_op jit(solution)/shard_map/ppermute | solution.py:463
